TPU v7x, 32 devices: a whole 2x2x4 slice. The times are simulated.
32 devices in a mesh: gx: 8 (over y, x, core), gy: 4 (over z).
Axes of the slice: x: 2, y: 2, z: 4, core: 2. Of those that a mesh axis runs over, the one named last changes fastest.
Arguments:
- tracer: float32 [2, 16, 1792, 1024], P(None, None, 'gx', 'gy'), may hold values from -6 to 6
- zonal_flow: bfloat16 [16, 1792, 1024], P(None, 'gx', 'gy'), may hold values from -3 to 3
- meridional_flow: bfloat16 [16, 1792, 1024], P(None, 'gx', 'gy'), may hold values from -3 to 3
- surface_prev: float32 [1792, 1024], P('gx', 'gy'), may hold values from -6 to 6
- transport_x: float32 [1792, 1024], P('gx', 'gy'), may hold values from -6 to 6
- transport_y: float32 [1792, 1024], P('gx', 'gy'), may hold values from -6 to 6
- land_mask: int32 [1792, 1024], P('gx', 'gy'), may hold values 0 or 1
- levels: int32 [1792, 1024], P('gx', 'gy'), may hold values from 1 to 16
Outputs:
- tracer_next: float32 [2, 16, 1792, 1024], P(None, None, 'gx', 'gy')
- surface: float32 [1792, 1024], P('gx', 'gy')
- transport_x_next: float32 [1792, 1024], P('gx', 'gy')
- transport_y_next: float32 [1792, 1024], P('gx', 'gy')
All inputs are finite; a program needn't handle non-finite values. No bound on the sum of `land_mask` on one device may be relied on, other than what follows from the above.
Results may differ from a plain program's by a relative error of at most 0.0003.
Values sent between devices are 32-bit elements; how exact they have to be, the bound alone decides.
No kernel may reach another device: no remote copies, remote signals or barrier semaphores. Data moves between devices by JAX's collectives and lax.ppermute only.
A program may use at most 192 MiB of HBM per device.

v0:
```python
import functools

import jax
import jax.numpy as jnp
from jax import lax
from jax.experimental import pallas as pl
from jax.experimental.pallas import tpu as pltpu
from jax.sharding import PartitionSpec as P

ITERS = 4
WIDTH = ITERS + 1
LANES = 128
SUB = 8
HALF = LANES // 2
FIELDS = 5
F32 = jnp.float32


def lane_ids(rows):
    return lax.broadcasted_iota(jnp.int32, (rows, LANES), 1)


def put_lane(value, source, target):
    shift = (target - source) % LANES
    return pltpu.roll(value, shift, 1) if shift else value


def column_kernel(tracer, land, levels, force, depth, edge, first, last):
    step = pl.program_id(0)
    count = tracer.shape[1]
    rows, cols = land.shape
    sides = cols // LANES
    lanes = lane_ids(SUB)
    for r in range(0, rows, SUB):
        at = pl.ds(r, SUB)
        packed = jnp.zeros((SUB, LANES), F32)
        for h in range(sides):
            span = pl.ds(h * LANES, LANES)
            deep = (land[at, span] * levels[at, span]).astype(F32)
            total = jnp.zeros((SUB, LANES), F32)
            for k in range(count):
                warm = tracer[0, k, at, span]
                salt = tracer[1, k, at, span]
                total = total + jnp.maximum(deep - k, 0.0) * (0.8 * warm - 0.6 * salt)
                for c, value in ((0, warm), (1, salt)):
                    lane = c * count + k
                    if h == 0:
                        packed = jnp.where(lanes == lane, put_lane(value, 0, lane), packed)
                    if h == sides - 1:
                        there = 2 * count + lane
                        packed = jnp.where(
                            lanes == there, put_lane(value, LANES - 1, there), packed
                        )
            force[at, span] = total * (1.0 / count)
            depth[at, span] = deep
        edge[at, :] = packed

    @pl.when(step == 0)
    def _():
        for c in range(2):
            for k in range(count):
                first[pl.ds(c * count + k, 1), :] = tracer[c, k, pl.ds(0, 1), :]

    @pl.when(step == pl.num_programs(0) - 1)
    def _():
        for c in range(2):
            for k in range(count):
                last[pl.ds(c * count + k, 1), :] = tracer[c, k, pl.ds(rows - 1, 1), :]


def column_pass(tracer, land, levels, chunk):
    two, count, rows, cols = tracer.shape
    flat = pl.BlockSpec((chunk, cols), lambda i: (i, 0))
    whole = pl.BlockSpec((two * count, cols), lambda i: (0, 0))
    return pl.pallas_call(
        column_kernel,
        grid=(rows // chunk,),
        in_specs=[
            pl.BlockSpec((two, count, chunk, cols), lambda i: (0, 0, i, 0)),
            flat,
            flat,
        ],
        out_specs=[flat, flat, pl.BlockSpec((chunk, LANES), lambda i: (i, 0)), whole, whole],
        out_shape=[
            jax.ShapeDtypeStruct((rows, cols), F32),
            jax.ShapeDtypeStruct((rows, cols), F32),
            jax.ShapeDtypeStruct((rows, LANES), F32),
            jax.ShapeDtypeStruct((two * count, cols), F32),
            jax.ShapeDtypeStruct((two * count, cols), F32),
        ],
        cost_estimate=pl.CostEstimate(
            flops=6 * tracer.size, bytes_accessed=4 * tracer.size, transcendentals=0
        ),
        name="columns",
    )(tracer, land, levels)


def pack_kernel(count, edge, depth, surf, flow_x, flow_y, force, west, east, south_out, north_out):
    rows, cols = depth.shape
    sides = cols // LANES
    half = rows // 2
    lanes = lane_ids(SUB)
    fields = (depth, surf, flow_x, flow_y, force)
    base = 2 * count

    def strips(load):
        low = jnp.zeros((SUB, LANES), F32)
        high = jnp.zeros((SUB, LANES), F32)
        for f in range(FIELDS):
            at = base + f * WIDTH
            inside = (lanes >= at) & (lanes < at + WIDTH)
            low = jnp.where(inside, put_lane(load(f, 0), 0, at), low)
            high = jnp.where(inside, put_lane(load(f, sides - 1), LANES - WIDTH, at), high)
        return low, high

    def centre(r):
        def load(f, h):
            return fields[f][pl.ds(r, SUB), pl.ds(h * LANES, LANES)]

        low, high = strips(load)
        both = edge[pl.ds(r, SUB), :]
        low = jnp.where(lanes < base, both, low)
        high = jnp.where(lanes < base, put_lane(both, base, 0), high)
        return low, high

    def beyond(ref):
        def load(f, h):
            return ref[pl.ds(base + f * SUB, SUB), pl.ds(h * LANES, LANES)]

        return strips(load)

    def emit(row, lower, upper):
        for out, index in ((south_out, 0), (north_out, 1)):
            out[pl.ds(row, SUB), :] = jnp.where(
                lanes < HALF, lower[index], pltpu.roll(upper[index], HALF, 1)
            )

    for r in range(0, half, SUB):
        emit(r, centre(r), centre(half + r))
    emit(half, beyond(west), beyond(east))


def pack_pass(count, edge, depth, surf, flow_x, flow_y, force, west, east):
    rows, _ = depth.shape
    shape = jax.ShapeDtypeStruct((rows // 2 + SUB, LANES), F32)
    return pl.pallas_call(
        functools.partial(pack_kernel, count),
        out_shape=[shape, shape],
        cost_estimate=pl.CostEstimate(
            flops=depth.size, bytes_accessed=24 * depth.size, transcendentals=0
        ),
        name="pack",
    )(edge, depth, surf, flow_x, flow_y, force, west, east)


def message_rows(ref, rows, r):
    half = rows // 2
    if r < 0:
        return ref[pl.ds(half, SUB), :]
    if r >= rows:
        return pltpu.roll(ref[pl.ds(half, SUB), :], HALF, 1)
    if r < half:
        return ref[pl.ds(r, SUB), :]
    return pltpu.roll(ref[pl.ds(r - half, SUB), :], HALF, 1)


def outer_tile(south, north, rows, r, at, open_south, open_north, lanes):
    up = put_lane(message_rows(north, rows, r), at, 0)
    down = put_lane(message_rows(south, rows, r), at, LANES - WIDTH)
    up = jnp.where((lanes < WIDTH) & open_north, up, 0.0)
    return jnp.where((lanes >= LANES - WIDTH) & open_south, down, up)


def extend(target, base, f, field, west, east, south, north, open_south, open_north):
    rows, cols = field.shape
    sides = cols // LANES
    lanes = lane_ids(SUB)
    at = base + f * WIDTH
    for r in range(-SUB, rows + 1, SUB):
        to = pl.ds(SUB + r, SUB)
        for h in range(sides):
            span = pl.ds(h * LANES, LANES)
            if r < 0:
                target[h, to, :] = west[pl.ds(base + f * SUB, SUB), span]
            elif r >= rows:
                target[h, to, :] = east[pl.ds(base + f * SUB, SUB), span]
            else:
                target[h, to, :] = field[pl.ds(r, SUB), span]
        target[sides, to, :] = outer_tile(
            south, north, rows, r, at, open_south, open_north, lanes
        )


def latitude_ends():
    place, size = lax.axis_index("gy"), lax.axis_size("gy")
    return place > 0, place < size - 1


def ring_shift(tiles, lanes):
    size = len(tiles)
    after = [pltpu.roll(t, LANES - 1, 1) for t in tiles]
    before = [pltpu.roll(t, 1, 1) for t in tiles]
    nxt = [jnp.where(lanes == LANES - 1, after[(h + 1) % size], after[h]) for h in range(size)]
    prv = [jnp.where(lanes == 0, before[(h - 1) % size], before[h]) for h in range(size)]
    return nxt, prv


def nine_sum(ref, r, lanes):
    sides = [ref[h, pl.ds(r + 1, SUB), :] + ref[h, pl.ds(r - 1, SUB), :] for h in range(ref.shape[0])]
    mixed = [ref[h, pl.ds(r, SUB), :] + 0.5 * sides[h] for h in range(ref.shape[0])]
    nxt, prv = ring_shift(mixed, lanes)
    return [sides[h] + (nxt[h] + prv[h]) for h in range(ref.shape[0])]


def peak_kernel(base, depth, west, east, south, north, peak, deep, wet):
    rows, cols = depth.shape
    sides = cols // LANES
    lanes = lane_ids(SUB)
    open_south, open_north = latitude_ends()
    scale = 1.0 / (base // 2)
    extend(deep, base, 0, depth, west, east, south, north, open_south, open_north)
    for r in range(0, rows + 2 * SUB, SUB):
        for h in range(sides + 1):
            d = deep[h, pl.ds(r, SUB), :] * scale
            deep[h, pl.ds(r, SUB), :] = d
            wet[h, pl.ds(r, SUB), :] = jnp.where(d > 0, 1.0, 0.0)
    best = jnp.full((SUB, LANES), 0.0, F32)
    for r in range(SUB, rows + SUB, SUB):
        sum_wet = nine_sum(wet, r, lanes)
        sum_deep = nine_sum(deep, r, lanes)
        for h in range(sides):
            d = deep[h, pl.ds(r, SUB), :]
            m = wet[h, pl.ds(r, SUB), :]
            best = jnp.maximum(best, 0.5 + 2.0 * (d * sum_wet[h] + m * sum_deep[h]))
    best = jnp.max(jnp.max(best, axis=1, keepdims=True), axis=0, keepdims=True)
    peak[...] = jnp.broadcast_to(best, (SUB, LANES))


def peak_pass(base, depth, west, east, south, north):
    rows, cols = depth.shape
    ext = pltpu.VMEM((cols // LANES + 1, rows + 2 * SUB, LANES), F32)
    return pl.pallas_call(
        functools.partial(peak_kernel, base),
        out_shape=jax.ShapeDtypeStruct((SUB, LANES), F32),
        scratch_shapes=[ext, ext],
        cost_estimate=pl.CostEstimate(
            flops=30 * depth.size, bytes_accessed=4 * depth.size, transcendentals=0
        ),
        name="peak",
    )(depth, west, east, south, north)


def tracer_kernel(
    start, tracer, zonal, merid, depth, west, east, south, north, *rest
):
    out, edge_x, edge_y, around, masked = rest[-5:]
    step = pl.program_id(0)
    count = edge_x.shape[0] // 4
    rows, cols = depth.shape
    sides = cols // LANES
    base = 2 * count
    level = step + start
    lanes = lane_ids(SUB)

    @pl.when(step == 0)
    def _():
        open_south, open_north = latitude_ends()
        kinds = lax.broadcasted_iota(jnp.int32, (base, LANES), 0)
        kinds = jnp.where(kinds < count, kinds, kinds - count).astype(F32)
        for side, (ref, line) in enumerate(((west, SUB - 1), (east, 0))):
            for h in range(sides):
                span = pl.ds(h * LANES, LANES)
                deep = ref[pl.ds(base + line, 1), span]
                value = jnp.where(deep > kinds, ref[pl.ds(0, base), span], 0.0)
                for i in range(base):
                    edge_x[side * base + i, h : h + 1, :] = value[i : i + 1]
        kinds = jnp.where(lanes < count, lanes, lanes - count).astype(F32)
        for side, (ref, column, is_open) in enumerate(
            ((south, base + WIDTH - 1, open_south), (north, base, open_north))
        ):
            for r in range(0, rows, SUB):
                value = message_rows(ref, rows, r)
                deep = jnp.where(is_open, value[:, column : column + 1], 0.0)
                edge_y[side, pl.ds(r, SUB), :] = jnp.where(deep > kinds, value, 0.0)
                deep_lane = put_lane(value, column, LANES - 1 if side else 0)
                deep_lane = jnp.where(is_open, deep_lane, 0.0)
                if side == 0:
                    tile = depth[pl.ds(r, SUB), pl.ds(0, LANES)]
                    prev = jnp.where(lanes == 0, deep_lane, pltpu.roll(tile, 1, 1))
                    around[3, 0, pl.ds(r, SUB), :] = prev
                    for h in range(1, sides):
                        back = pltpu.roll(depth[pl.ds(r, SUB), pl.ds((h - 1) * LANES, LANES)], 1, 1)
                        here = pltpu.roll(depth[pl.ds(r, SUB), pl.ds(h * LANES, LANES)], 1, 1)
                        around[3, h, pl.ds(r, SUB), :] = jnp.where(lanes == 0, back, here)
                else:
                    for h in range(sides):
                        here = pltpu.roll(
                            depth[pl.ds(r, SUB), pl.ds(h * LANES, LANES)], LANES - 1, 1
                        )
                        ahead = deep_lane
                        if h + 1 < sides:
                            ahead = pltpu.roll(
                                depth[pl.ds(r, SUB), pl.ds((h + 1) * LANES, LANES)], LANES - 1, 1
                            )
                        around[2, h, pl.ds(r, SUB), :] = jnp.where(
                            lanes == LANES - 1, ahead, here
                        )
        for h in range(sides):
            span = pl.ds(h * LANES, LANES)
            masked[0, h, pl.ds(0, SUB), :] = west[pl.ds(base, SUB), span]
            masked[0, h, pl.ds(SUB, rows), :] = depth[:, span]
            masked[0, h, pl.ds(SUB + rows, SUB), :] = east[pl.ds(base, SUB), span]
            for r in range(0, rows, SUB):
                around[0, h, pl.ds(r, SUB), :] = masked[0, h, pl.ds(SUB + r + 1, SUB), :]
                around[1, h, pl.ds(r, SUB), :] = masked[0, h, pl.ds(SUB + r - 1, SUB), :]

    mark = level.astype(F32)
    for h in range(sides):
        span = pl.ds(h * LANES, LANES)
        for c in range(2):
            masked[c, h, pl.ds(SUB - 1, 1), :] = edge_x[c * count + level, h : h + 1, :]
            masked[c, h, pl.ds(SUB + rows, 1), :] = edge_x[base + c * count + level, h : h + 1, :]
            for r in range(0, rows, SUB):
                here = depth[pl.ds(r, SUB), span] > mark
                masked[c, h, pl.ds(SUB + r, SUB), :] = jnp.where(
                    here, tracer[c, 0, pl.ds(r, SUB), span], 0.0
                )
    for big in range(0, rows, 2 * SUB):
        speeds = []
        for h in range(sides):
            span = pl.ds(h * LANES, LANES)
            speeds.append(
                (
                    zonal[0, pl.ds(big, 2 * SUB), span].astype(F32),
                    merid[0, pl.ds(big, 2 * SUB), span].astype(F32),
                )
            )
        for sub in range(2):
            r = big + sub * SUB
            at = pl.ds(r, SUB)
            factors = []
            for h in range(sides):
                span = pl.ds(h * LANES, LANES)
                here = depth[at, span] > mark
                near = jnp.zeros((SUB, LANES), F32)
                for n in range(4):
                    near = near + jnp.where(around[n, h, at, :] > mark, 1.0, 0.0)
                mix = jnp.where(here, 0.2, 0.0)
                u = jnp.where(here, 0.25 * speeds[h][0][sub * SUB : (sub + 1) * SUB], 0.0)
                v = jnp.where(here, 0.25 * speeds[h][1][sub * SUB : (sub + 1) * SUB], 0.0)
                factors.append((1.0 - mix * near, mix - u, mix + u, mix - v, mix + v))
            for c in range(2):
                tiles = [masked[c, h, pl.ds(SUB + r, SUB), :] for h in range(sides)]
                lane = c * count + level
                from_south = pltpu.roll(edge_y[0, at, :], LANES - lane, 1)
                from_north = pltpu.roll(edge_y[1, at, :], LANES - 1 - lane, 1)
                after = [pltpu.roll(t, LANES - 1, 1) for t in tiles] + [from_north]
                before = [from_south] + [pltpu.roll(t, 1, 1) for t in tiles]
                for h in range(sides):
                    span = pl.ds(h * LANES, LANES)
                    own, to_e, to_w, to_n, to_s = factors[h]
                    nxt = jnp.where(lanes == LANES - 1, after[h + 1], after[h])
                    prv = jnp.where(lanes == 0, before[h], before[h + 1])
                    value = own * tracer[c, 0, at, span] + to_n * nxt + to_s * prv
                    value = value + to_e * masked[c, h, pl.ds(SUB + r + 1, SUB), :]
                    value = value + to_w * masked[c, h, pl.ds(SUB + r - 1, SUB), :]
                    out[c, 0, at, span] = value


def tracer_pass(start, stop, tracer, zonal, merid, depth, west, east, south, north, into=None):
    two, count, rows, cols = tracer.shape
    sides = cols // LANES
    block = pl.BlockSpec((two, 1, rows, cols), lambda k: (0, k + start, 0, 0))
    speed = pl.BlockSpec((1, rows, cols), lambda k: (k + start, 0, 0))

    def fixed(value):
        return pl.BlockSpec(value.shape, lambda k: (0, 0))

    small = [depth, west, east, south, north]
    operands = [tracer, zonal, merid, *small]
    specs = [block, speed, speed] + [fixed(v) for v in small]
    aliases = {}
    if into is not None:
        aliases = {len(operands): 0}
        operands.append(into)
        specs.append(pl.BlockSpec(memory_space=pl.ANY))
    part = stop - start
    return pl.pallas_call(
        functools.partial(tracer_kernel, start),
        grid=(part,),
        in_specs=specs,
        out_specs=block,
        out_shape=jax.ShapeDtypeStruct(tracer.shape, F32),
        scratch_shapes=[
            pltpu.VMEM((4 * count, sides, LANES), F32),
            pltpu.VMEM((2, rows, LANES), F32),
            pltpu.VMEM((4, sides, rows, LANES), F32),
            pltpu.VMEM((2, sides, rows + 2 * SUB, LANES), F32),
        ],
        input_output_aliases=aliases,
        cost_estimate=pl.CostEstimate(
            flops=40 * tracer.size * part // count,
            bytes_accessed=10 * tracer.size * part // count,
            transcendentals=0,
        ),
        name="tracers",
    )(*operands)


def solve_kernel(
    base, peak, depth, surf, flow_x, flow_y, force, west, east, south, north,
    surf_out, x_out, y_out, deep, wet, surf0, flux_x, flux_y, forced, left, right, start, step_by, total,
):
    rows, cols = depth.shape
    sides = cols // LANES
    tiles = sides + 1
    lanes = lane_ids(SUB)
    open_south, open_north = latitude_ends()
    halo = (west, east, south, north, open_south, open_north)
    scale = 1.0 / (base // 2)
    extend(deep, base, 0, depth, *halo)
    extend(surf0, base, 1, surf, *halo)
    extend(flux_x, base, 2, flow_x, *halo)
    extend(flux_y, base, 3, flow_y, *halo)
    extend(forced, base, 4, force, *halo)
    every = range(0, rows + 2 * SUB, SUB)
    inner = range(SUB, rows + SUB, SUB)

    for r in every:
        at = pl.ds(r, SUB)
        for h in range(tiles):
            d = deep[h, at, :] * scale
            m = jnp.where(d > 0, 1.0, 0.0)
            deep[h, at, :] = d
            wet[h, at, :] = m
            flux_x[h, at, :] = m * flux_x[h, at, :]
            flux_y[h, at, :] = m * flux_y[h, at, :]
            total[h, at, :] = m * surf0[h, at, :]
            step_by[h, at, :] = d * surf0[h, at, :]

    def clamp_rows(r):
        return min(max(r, 1), rows + 2 * SUB - SUB - 1)

    spans = [clamp_rows(r) for r in every]
    for r in spans:
        at = pl.ds(r, SUB)
        sum_wet = nine_sum(wet, r, lanes)
        sum_deep = nine_sum(deep, r, lanes)
        sum_f = nine_sum(total, r, lanes)
        sum_g = nine_sum(step_by, r, lanes)
        nxt, prv = ring_shift([flux_y[h, at, :] for h in range(tiles)], lanes)
        for h in range(tiles):
            d = deep[h, at, :]
            m = wet[h, at, :]
            inverse = 1.0 / (0.5 + 2.0 * (d * sum_wet[h] + m * sum_deep[h]))
            a = 2.0 * d * inverse
            b = 2.0 * m * inverse
            left[h, at, :] = a
            right[h, at, :] = b
            e = surf0[h, at, :]
            div = 0.5 * (
                flux_x[h, pl.ds(r + 1, SUB), :] - flux_x[h, pl.ds(r - 1, SUB), :]
            ) + 0.5 * (nxt[h] - prv[h])
            rhs = 0.5 * e + forced[h, at, :] - 0.5 * div
            start[h, at, :] = rhs * inverse - e + a * sum_f[h] + b * sum_g[h]

    top = peak[...]
    lowest = 0.5 / top
    shrink = (1.0 - lowest) * (1.0 - lowest)
    omega = jnp.full((SUB, LANES), 2.0, F32)
    for r in every:
        at = pl.ds(r, SUB)
        for h in range(tiles):
            z = start[h, at, :]
            total[h, at, :] = z
            step_by[h, at, :] = z
            flux_x[h, at, :] = wet[h, at, :] * z
            flux_y[h, at, :] = deep[h, at, :] * z
    for turn in range(1, ITERS):
        omega = 1.0 / (1.0 - omega * shrink * 0.25)
        for r in spans:
            at = pl.ds(r, SUB)
            sum_f = nine_sum(flux_x, r, lanes)
            sum_g = nine_sum(flux_y, r, lanes)
            for h in range(tiles):
                s = total[h, at, :]
                y = start[h, at, :] - s + left[h, at, :] * sum_f[h] + right[h, at, :] * sum_g[h]
                delta = omega * y + (omega - 1.0) * step_by[h, at, :]
                forced[h, at, :] = delta
        for r in every:
            at = pl.ds(r, SUB)
            for h in range(tiles):
                delta = forced[h, at, :]
                s = total[h, at, :] + delta
                total[h, at, :] = s
                step_by[h, at, :] = delta
                flux_x[h, at, :] = wet[h, at, :] * s
                flux_y[h, at, :] = deep[h, at, :] * s

    for r in every:
        at = pl.ds(r, SUB)
        for h in range(tiles):
            value = surf0[h, at, :] + total[h, at, :]
            if h == sides:
                value = jnp.where((lanes < WIDTH) & open_north, value, jnp.where(
                    (lanes >= LANES - WIDTH) & open_south, value, 0.0))
            total[h, at, :] = value
    for r in inner:
        at = pl.ds(r, SUB)
        back = pl.ds(r - SUB, SUB)
        nxt, prv = ring_shift([total[h, at, :] for h in range(tiles)], lanes)
        for h in range(sides):
            span = pl.ds(h * LANES, LANES)
            m = wet[h, at, :]
            surf_out[back, span] = total[h, at, :]
            slope = total[h, pl.ds(r + 1, SUB), :] - total[h, pl.ds(r - 1, SUB), :]
            x_out[back, span] = m * (flow_x[back, span] - 0.25 * slope)
            y_out[back, span] = m * (flow_y[back, span] - 0.25 * (nxt[h] - prv[h]))


def solve_pass(base, peak, depth, surf, flow_x, flow_y, force, west, east, south, north):
    rows, cols = depth.shape
    ext = pltpu.VMEM((cols // LANES + 1, rows + 2 * SUB, LANES), F32)
    shape = jax.ShapeDtypeStruct((rows, cols), F32)
    return pl.pallas_call(
        functools.partial(solve_kernel, base),
        out_shape=[shape] * 3,
        scratch_shapes=[ext] * 11,
        cost_estimate=pl.CostEstimate(
            flops=200 * depth.size, bytes_accessed=32 * depth.size, transcendentals=0
        ),
        name="solve",
    )(peak, depth, surf, flow_x, flow_y, force, west, east, south, north)


def both_ways(axis, to_next, to_previous):
    size = lax.axis_size(axis)
    up = [(i, (i + 1) % size) for i in range(size)]
    down = [(j, i) for i, j in up]
    return lax.ppermute(to_next, axis, up), lax.ppermute(to_previous, axis, down)


def spread_max(value, axis):
    size = lax.axis_size(axis)
    reach = 1
    while reach < size:
        if size & (size - 1) == 0:
            pairs = [(i, i ^ reach) for i in range(size)]
        else:
            pairs = [(i, (i + reach) % size) for i in range(size)]
        value = jnp.maximum(value, lax.ppermute(value, axis, pairs))
        reach *= 2
    return value


def local(
    tracer, zonal_flow, meridional_flow, surface_prev, transport_x, transport_y, land_mask, levels
):
    _, count, rows, cols = tracer.shape
    base = 2 * count
    force, depth, edge, first, last = column_pass(tracer, land_mask, levels, rows // 4)
    fields = (depth, surface_prev, transport_x, transport_y, force)
    to_next = jnp.concatenate([last] + [f[rows - SUB :] for f in fields], 0)
    to_previous = jnp.concatenate([first] + [f[:SUB] for f in fields], 0)
    west, east = both_ways("gx", to_next, to_previous)
    to_south, to_north = pack_pass(count, edge, *fields, west, east)
    south, north = both_ways("gy", to_north, to_south)
    peak = peak_pass(base, depth, west, east, south, north)
    peak = spread_max(spread_max(peak, "gx"), "gy")
    tracer_next = tracer_pass(
        0, count, tracer, zonal_flow, meridional_flow, depth, west, east, south, north
    )
    surf, next_x, next_y = solve_pass(base, peak, *fields, west, east, south, north)
    return (tracer_next, surf, next_x, next_y)


def solution(mesh):
    cell = P("gx", "gy")
    level = P(None, "gx", "gy")
    stack = P(None, None, "gx", "gy")
    return jax.shard_map(
        local,
        mesh=mesh,
        in_specs=(stack, level, level, cell, cell, cell, cell, cell),
        out_specs=(stack, cell, cell, cell),
        check_vma=False,
    )
```

profile of v0, /device:TPU:0, one launch (start us, length us, event | category | flops | bytes accessed | tf_op | source)
XLA Modules:
  0.0 69.6 jit_solution(14054107108639518222)
XLA Ops:
  0.6 5.7 %columns.1 = (f32[224,256]{1,0:T(8,128)}, f32[224,256]{1,0:T(8,128)}, f32[224,128]{1,0:T(8,128)}, f32[32,256]{1,0:T(8,128)}, f32[32,256]{1,0:T(8,128)}) custom-call(f32[2,16,224,256]{3,2,1,0:T(8,128)} %tracer.3, s32[224,256]{1,0:T(8,128)} %land.1, s32[224,256]{1,0:T(8,128)} %levels.1), custom_call_target="tpu_custom_call" | custom-call | flops 11010048 | bytes 7340032 | tf_op jit(solution)/shard_map/columns/pallas_call | solution.py:75
  6.3 0.8 %constant_dynamic-update-slice_fusion.5 = (f32[72,256]{1,0:T(8,128)S(1)}, f32[72,256]{1,0:T(8,128)S(1)}) fusion(f32[32,256]{1,0:T(8,128)} %get-tuple-element.15, f32[32,256]{1,0:T(8,128)} %get-tuple-element.17), kind=kLoop, calls=%fused_computation.5 | loop fusion | bytes 131072
  7.1 0.7 %constant_dynamic-update-slice_fusion.10 = (f32[72,256]{1,0:T(8,128)S(1)}, f32[72,256]{1,0:T(8,128)S(1)}) fusion(f32[72,256]{1,0:T(8,128)S(1)} %get-tuple-element.35, f32[224,256]{1,0:T(8,128)} %get-tuple-element.14.depth, f32[72,256]{1,0:T(8,128)S(1)} %get-tuple-element.34), kind=kLoop, calls=%fused_computation.10 | loop fusion | bytes 32768
  7.8 0.7 %constant_dynamic-update-slice_fusion.9 = (f32[72,256]{1,0:T(8,128)S(1)}, f32[72,256]{1,0:T(8,128)S(1)}) fusion(f32[72,256]{1,0:T(8,128)S(1)} %get-tuple-element.32, f32[224,256]{1,0:T(8,128)} %surf.3, f32[72,256]{1,0:T(8,128)S(1)} %get-tuple-element.33), kind=kLoop, calls=%fused_computation.9 | loop fusion | bytes 32768
  8.5 0.7 %constant_dynamic-update-slice_fusion.8 = (f32[72,256]{1,0:T(8,128)S(1)}, f32[72,256]{1,0:T(8,128)S(1)}) fusion(f32[72,256]{1,0:T(8,128)S(1)} %get-tuple-element.30, f32[224,256]{1,0:T(8,128)} %flow_x.3, f32[72,256]{1,0:T(8,128)S(1)} %get-tuple-element.31), kind=kLoop, calls=%fused_computation.8 | loop fusion | bytes 32768
  9.2 0.7 %constant_dynamic-update-slice_fusion.7 = (f32[72,256]{1,0:T(8,128)S(1)}, f32[72,256]{1,0:T(8,128)S(1)}) fusion(f32[72,256]{1,0:T(8,128)S(1)} %get-tuple-element.28, f32[224,256]{1,0:T(8,128)} %flow_y.3, f32[72,256]{1,0:T(8,128)S(1)} %get-tuple-element.29), kind=kLoop, calls=%fused_computation.7 | loop fusion | bytes 32768
  9.9 0.7 %constant_dynamic-update-slice_fusion.6 = (f32[72,256]{1,0:T(8,128)S(1)}, f32[72,256]{1,0:T(8,128)S(1)}) fusion(f32[72,256]{1,0:T(8,128)S(1)} %get-tuple-element.26, f32[224,256]{1,0:T(8,128)} %get-tuple-element.16.force, f32[72,256]{1,0:T(8,128)S(1)} %get-tuple-element.27), kind=kLoop, calls=%fused_computation.6 | loop fusion | bytes 32768 | tf_op jit(solution)/shard_map/concatenate | solution.py:564
  10.7 3.4 %collective-permute-start.1 = (f32[72,256]{1,0:T(8,128)S(1)}, f32[72,256]{1,0:T(8,128)S(1)}, u32[]{:S(2)}, u32[]{:S(2)}) collective-permute-start(f32[72,256]{1,0:T(8,128)S(1)} %get-tuple-element.24), channel_id=1, source_target_pairs={{4,0},{8,4},{12,8},{16,12},{20,16},{24,20},{28,24},{0,28},{5,1},{9... | collective-permute-start | bytes 221192 | tf_op jit(solution)/shard_map/ppermute | solution.py:540
  14.0 0.0 collective-permute-start
  14.0 2.0 %collective-permute-done.1.east = f32[72,256]{1,0:T(8,128)S(1)} collective-permute-done((f32[72,256]{1,0:T(8,128)S(1)}, f32[72,256]{1,0:T(8,128)S(1)}, u32[]{:S(2)}, u32[]{:S(2)}) %collective-permute-start.1) | collective-permute-done | bytes 73760 | tf_op jit(solution)/shard_map/ppermute | solution.py:540
  16.0 0.0 copy-start
  16.0 2.7 %collective-permute-done.west = f32[72,256]{1,0:T(8,128)S(1)} collective-permute-done((f32[72,256]{1,0:T(8,128)S(1)}, f32[72,256]{1,0:T(8,128)S(1)}, u32[]{:S(2)}, u32[]{:S(2)}) %collective-permute-start) | collective-permute-done | bytes 73760 | tf_op jit(solution)/shard_map/ppermute | solution.py:540
  18.7 0.0 copy-start.1
  18.7 0.0 copy-done
  18.7 0.6 copy-done.1
  19.3 3.2 %pack.1 = (f32[120,128]{1,0:T(8,128)}, f32[120,128]{1,0:T(8,128)}) custom-call(f32[224,128]{1,0:T(8,128)} %get-tuple-element.18.edge, f32[224,256]{1,0:T(8,128)} %get-tuple-element.14.depth, f32[224,256]{1,0:T(8,128)} %surf.3, f32[224,256]{1,0:T(8,128)} %flow_x.3, f32[224,256]{1,0:T(8,128)} %flow_y.3, f32[224,256]{1,0:T(8,128)} %get-tuple-element.16.force, ...), custom_call_target="tpu_custom_call" | custom-call | flops 57344 | bytes 1376256 | tf_op jit(solution)/shard_map/pack/pallas_call | solution.py:146
  22.5 1.6 %collective-permute-start.2 = (f32[120,128]{1,0:T(8,128)}, f32[120,128]{1,0:T(8,128)S(1)}, u32[]{:S(2)}, u32[]{:S(2)}) collective-permute-start(f32[120,128]{1,0:T(8,128)} %get-tuple-element.19), channel_id=1, source_target_pairs={{0,1},{1,2},{2,3},{3,0},{4,5},{5,6},{6,7},{7,4},{8,9},{9,10},{10,1... | collective-permute-start | bytes 184328 | tf_op jit(solution)/shard_map/ppermute | solution.py:540
  24.1 2.2 %collective-permute-start.3 = (f32[120,128]{1,0:T(8,128)}, f32[120,128]{1,0:T(8,128)S(1)}, u32[]{:S(2)}, u32[]{:S(2)}) collective-permute-start(f32[120,128]{1,0:T(8,128)} %get-tuple-element.20), channel_id=1, source_target_pairs={{1,0},{2,1},{3,2},{0,3},{5,4},{6,5},{7,6},{4,7},{9,8},{10,9},{11,1... | collective-permute-start | bytes 184328 | tf_op jit(solution)/shard_map/ppermute | solution.py:540
  26.4 2.5 %collective-permute-done.2.south = f32[120,128]{1,0:T(8,128)S(1)} collective-permute-done((f32[120,128]{1,0:T(8,128)}, f32[120,128]{1,0:T(8,128)S(1)}, u32[]{:S(2)}, u32[]{:S(2)}) %collective-permute-start.2) | collective-permute-done | bytes 61472 | tf_op jit(solution)/shard_map/ppermute | solution.py:540
  28.9 0.0 copy-start.2
  28.9 0.3 collective-permute-done.3.north
  29.2 0.3 copy-done.2
  29.5 0.0 copy-start.3
  29.5 0.6 copy-done.3
  30.1 2.3 %peak.1 = f32[8,128]{1,0:T(8,128)} custom-call(f32[224,256]{1,0:T(8,128)} %get-tuple-element.14.depth, f32[72,256]{1,0:T(8,128)} %copy-done.1, f32[72,256]{1,0:T(8,128)} %copy-done, f32[120,128]{1,0:T(8,128)} %copy-done.2, f32[120,128]{1,0:T(8,128)} %copy-done.3), custom_call_target="tpu_custom_call" | custom-call | flops 1720320 | bytes 229376 | tf_op jit(solution)/shard_map/peak/pallas_call | solution.py:242
  32.4 0.0 collective-permute-start.4
  32.4 1.4 %collective-permute-done.4 = f32[8,128]{1,0:T(8,128)S(1)} collective-permute-done((f32[8,128]{1,0:T(8,128)}, f32[8,128]{1,0:T(8,128)S(1)}, u32[]{:S(2)}, u32[]{:S(2)}) %collective-permute-start.4) | collective-permute-done | bytes 4128 | tf_op jit(solution)/shard_map/ppermute | solution.py:551
  33.8 0.7 max.15
  34.5 0.0 collective-permute-start.5
  34.5 3.6 %collective-permute-done.5 = f32[8,128]{1,0:T(8,128)S(1)} collective-permute-done((f32[8,128]{1,0:T(8,128)S(1)}, f32[8,128]{1,0:T(8,128)S(1)}, u32[]{:S(2)}, u32[]{:S(2)}) %collective-permute-start.5) | collective-permute-done | bytes 4128 | tf_op jit(solution)/shard_map/ppermute | solution.py:551
  38.1 0.5 collective-permute-start.6
  38.6 3.1 %collective-permute-done.6 = f32[8,128]{1,0:T(8,128)S(1)} collective-permute-done((f32[8,128]{1,0:T(8,128)S(1)}, f32[8,128]{1,0:T(8,128)S(1)}, u32[]{:S(2)}, u32[]{:S(2)}) %collective-permute-start.6) | collective-permute-done | bytes 4128 | tf_op jit(solution)/shard_map/ppermute | solution.py:551
  41.7 0.6 collective-permute-start.7
  42.4 3.0 %collective-permute-done.7 = f32[8,128]{1,0:T(8,128)S(1)} collective-permute-done((f32[8,128]{1,0:T(8,128)S(1)}, f32[8,128]{1,0:T(8,128)S(1)}, u32[]{:S(2)}, u32[]{:S(2)}) %collective-permute-start.7) | collective-permute-done | bytes 4128 | tf_op jit(solution)/shard_map/ppermute | solution.py:551
  45.3 1.6 %collective-permute-start.8 = (f32[8,128]{1,0:T(8,128)S(1)}, f32[8,128]{1,0:T(8,128)S(1)}, u32[]{:S(2)}, u32[]{:S(2)}) collective-permute-start(f32[8,128]{1,0:T(8,128)S(1)} %max.18), channel_id=1, source_target_pairs={{0,2},{1,3},{2,0},{3,1},{4,6},{5,7},{6,4},{7,5},{8,10},{9,11},{10,... | collective-permute-start | bytes 12296 | tf_op jit(solution)/shard_map/ppermute | solution.py:551
  47.0 16.8 %tracers.1 = f32[2,16,224,256]{3,2,1,0:T(8,128)} custom-call(f32[2,16,224,256]{3,2,1,0:T(8,128)} %tracer.3, bf16[16,224,256]{2,1,0:T(8,128)(2,1)} %zonal.1, bf16[16,224,256]{2,1,0:T(8,128)(2,1)} %merid.1, f32[224,256]{1,0:T(8,128)} %get-tuple-element.14.depth, f32[72,256]{1,0:T(8,128)} %copy-done.1, f32[72,256]{1,0:T(8,128)} %copy-done, ...), custom_call_target="tpu_custom_call" | custom-call | flops 73400320 | bytes 18350080 | tf_op jit(solution)/shard_map/tracers/pallas_call | solution.py:388
  63.8 0.0 collective-permute-done.8
  63.8 0.6 max.19.peak
  64.4 5.2 %solve.1 = (f32[224,256]{1,0:T(8,128)}, f32[224,256]{1,0:T(8,128)}, f32[224,256]{1,0:T(8,128)}) custom-call(f32[8,128]{1,0:T(8,128)} %max.19.peak, f32[224,256]{1,0:T(8,128)} %get-tuple-element.14.depth, f32[224,256]{1,0:T(8,128)} %surf.3, f32[224,256]{1,0:T(8,128)} %flow_x.3, f32[224,256]{1,0:T(8,128)} %flow_y.3, f32[224,256]{1,0:T(8,128)} %get-tuple-element.16.force, ...), custom_call_target="tpu_custom_call" | custom-call | flops 11468800 | bytes 1835008 | tf_op jit(solution)/shard_map/solve/pallas_call | solution.py:525
  (3 shorter events, 0.0 us)
Async XLA Ops:
  10.7 5.3 %collective-permute-start.1 = (f32[72,256]{1,0:T(8,128)S(1)}, f32[72,256]{1,0:T(8,128)S(1)}, u32[]{:S(2)}, u32[]{:S(2)}) collective-permute-start(f32[72,256]{1,0:T(8,128)S(1)} %get-tuple-element.24), channel_id=1, source_target_pairs={{4,0},{8,4},{12,8},{16,12},{20,16},{24,20},{28,24},{0,28},{5,1},{9... | collective-permute-start | bytes 221192 | tf_op jit(solution)/shard_map/ppermute | solution.py:540
  14.0 4.7 %collective-permute-start = (f32[72,256]{1,0:T(8,128)S(1)}, f32[72,256]{1,0:T(8,128)S(1)}, u32[]{:S(2)}, u32[]{:S(2)}) collective-permute-start(f32[72,256]{1,0:T(8,128)S(1)} %get-tuple-element.25), channel_id=1, source_target_pairs={{0,4},{4,8},{8,12},{12,16},{16,20},{20,24},{24,28},{28,0},{1,5},{5... | collective-permute-start | bytes 221192 | tf_op jit(solution)/shard_map/ppermute | solution.py:540
  16.0 2.7 %copy-start = (f32[72,256]{1,0:T(8,128)}, f32[72,256]{1,0:T(8,128)S(1)}, u32[]{:S(2)}) copy-start(f32[72,256]{1,0:T(8,128)S(1)} %collective-permute-done.1.east) | copy-start | bytes 221188
  18.7 0.6 copy-start.1
  22.5 6.3 %collective-permute-start.2 = (f32[120,128]{1,0:T(8,128)}, f32[120,128]{1,0:T(8,128)S(1)}, u32[]{:S(2)}, u32[]{:S(2)}) collective-permute-start(f32[120,128]{1,0:T(8,128)} %get-tuple-element.19), channel_id=1, source_target_pairs={{0,1},{1,2},{2,3},{3,0},{4,5},{5,6},{6,7},{7,4},{8,9},{9,10},{10,1... | collective-permute-start | bytes 184328 | tf_op jit(solution)/shard_map/ppermute | solution.py:540
  24.1 5.1 %collective-permute-start.3 = (f32[120,128]{1,0:T(8,128)}, f32[120,128]{1,0:T(8,128)S(1)}, u32[]{:S(2)}, u32[]{:S(2)}) collective-permute-start(f32[120,128]{1,0:T(8,128)} %get-tuple-element.20), channel_id=1, source_target_pairs={{1,0},{2,1},{3,2},{0,3},{5,4},{6,5},{7,6},{4,7},{9,8},{10,9},{11,1... | collective-permute-start | bytes 184328 | tf_op jit(solution)/shard_map/ppermute | solution.py:540
  28.9 0.6 copy-start.2
  29.5 0.6 copy-start.3
  32.4 1.4 %collective-permute-start.4 = (f32[8,128]{1,0:T(8,128)}, f32[8,128]{1,0:T(8,128)S(1)}, u32[]{:S(2)}, u32[]{:S(2)}) collective-permute-start(f32[8,128]{1,0:T(8,128)} %peak.1), channel_id=1, source_target_pairs={{0,4},{4,0},{8,12},{12,8},{16,20},{20,16},{24,28},{28,24},{1,5},{5... | collective-permute-start | bytes 12296 | tf_op jit(solution)/shard_map/ppermute | solution.py:551
  34.5 3.6 %collective-permute-start.5 = (f32[8,128]{1,0:T(8,128)S(1)}, f32[8,128]{1,0:T(8,128)S(1)}, u32[]{:S(2)}, u32[]{:S(2)}) collective-permute-start(f32[8,128]{1,0:T(8,128)S(1)} %max.15), channel_id=1, source_target_pairs={{0,8},{4,12},{8,0},{12,4},{16,24},{20,28},{24,16},{28,20},{1,9},{5... | collective-permute-start | bytes 12296 | tf_op jit(solution)/shard_map/ppermute | solution.py:551
  38.1 3.6 %collective-permute-start.6 = (f32[8,128]{1,0:T(8,128)S(1)}, f32[8,128]{1,0:T(8,128)S(1)}, u32[]{:S(2)}, u32[]{:S(2)}) collective-permute-start(f32[8,128]{1,0:T(8,128)S(1)} %max.16), channel_id=1, source_target_pairs={{0,16},{4,20},{8,24},{12,28},{16,0},{20,4},{24,8},{28,12},{1,17},{... | collective-permute-start | bytes 12296 | tf_op jit(solution)/shard_map/ppermute | solution.py:551
  41.7 3.6 %collective-permute-start.7 = (f32[8,128]{1,0:T(8,128)S(1)}, f32[8,128]{1,0:T(8,128)S(1)}, u32[]{:S(2)}, u32[]{:S(2)}) collective-permute-start(f32[8,128]{1,0:T(8,128)S(1)} %max.17), channel_id=1, source_target_pairs={{0,1},{1,0},{2,3},{3,2},{4,5},{5,4},{6,7},{7,6},{8,9},{9,8},{10,11... | collective-permute-start | bytes 12296 | tf_op jit(solution)/shard_map/ppermute | solution.py:551
  45.3 18.5 %collective-permute-start.8 = (f32[8,128]{1,0:T(8,128)S(1)}, f32[8,128]{1,0:T(8,128)S(1)}, u32[]{:S(2)}, u32[]{:S(2)}) collective-permute-start(f32[8,128]{1,0:T(8,128)S(1)} %max.18), channel_id=1, source_target_pairs={{0,2},{1,3},{2,0},{3,1},{4,6},{5,7},{6,4},{7,5},{8,10},{9,11},{10,... | collective-permute-start | bytes 12296 | tf_op jit(solution)/shard_map/ppermute | solution.py:551
where the time goes:
time: 70.5 us; the launch traced here: 69.6 us
  Pallas kernels  33.2 us (47%)
  waiting for transfers between devices  18.6 us (26%)
  starting transfers between devices  9.96 us (14%)
  local copies, waits for them, and re-layouts  5.91 us (8%)
  other arithmetic  1.29 us (2%)
    pallas_call x1, Pallas kernels, tracer_pass(): pl.pallas_call(functools.partial(tracer_kernel, start), grid=(part,), in_...  16.8 us
    ppermute x5, waiting for transfers between devices, spread_max(): value = jnp.maximum(value, lax.ppermute(value, axis, pairs))  11.1 us
    pallas_call x1, Pallas kernels, column_pass(): pl.pallas_call(column_kernel, grid=(rows // chunk,), in_specs=[pl.BlockSp...  5.66 us
    ppermute x2, starting transfers between devices, both_ways(): lax.ppermute(to_previous, axis, down)  5.61 us
    ppermute x2, waiting for transfers between devices, both_ways(): lax.ppermute(to_next, axis, up)  5.2 us
    unnamed x13, local copies, waits for them, and re-layouts  5.2 us
    pallas_call x1, Pallas kernels, solve_pass(): pl.pallas_call(functools.partial(solve_kernel, base), out_shape=[shape] *...  5.18 us
    pallas_call x1, Pallas kernels, pack_pass(): pl.pallas_call(functools.partial(pack_kernel, count), out_shape=[shape, s...  3.19 us
  transfers between devices with their start and end apart: 9, of which 8 were waited for; matrix products, arithmetic and copies ran while one was open for 0% of the time, Pallas kernels for 24%

commit v1 on v0

v1 whole, which is shorter than its diff:
```python
import functools

import jax
import jax.numpy as jnp
from jax import lax
from jax.experimental import pallas as pl
from jax.experimental.pallas import tpu as pltpu
from jax.sharding import PartitionSpec as P

ITERS = 4
WIDTH = ITERS + 1
LANES = 128
SUB = 8
HALF = LANES // 2
FIELDS = 5
F32 = jnp.float32
BF16 = jnp.bfloat16
VMEM_LIMIT = 12 * 1024 * 1024
LEVELS = 16
BASE = 2 * LEVELS
CODE = 1024.0
PARTS = 4


def lane_ids(rows):
    return lax.broadcasted_iota(jnp.int32, (rows, LANES), 1)


def put_lane(value, source, target):
    shift = (target - source) % LANES
    return pltpu.roll(value, shift, 1) if shift else value


def strip_pair(low, high, lanes, values):
    for f, (begin, end) in enumerate(values):
        at = BASE + (f + 1) * WIDTH
        turned = put_lane(jnp.where(lanes < HALF, begin, end), 0, at)
        low = jnp.where((lanes >= at) & (lanes < at + WIDTH), turned, low)
        high = jnp.where((lanes >= at - WIDTH) & (lanes < at), turned, high)
    return low, high


def column_kernel(
    tracer, land, levels, surf, flow_x, flow_y,
    force, depth, to_south, to_north, to_previous, to_next,
):
    step, steps = pl.program_id(0), pl.num_programs(0)
    count = tracer.shape[1]
    rows, cols = land.shape
    sides = cols // LANES
    base = 2 * count
    lanes = lane_ids(SUB)
    upper = step >= steps // 2
    turn = jnp.where(upper, HALF, 0)
    keep = (lanes < HALF) & upper
    first_row = jnp.where(upper, step - steps // 2, step) * rows
    low_kind = jnp.where((lanes >= 1) & (lanes <= base), lax.rem(lanes - 1 + count, count), -1)
    low_kind = low_kind.astype(F32)
    high_kind = jnp.where(lanes < base, lax.rem(lanes, count), -1).astype(F32)
    for r in range(0, rows, SUB):
        at = pl.ds(r, SUB)
        packed = [jnp.zeros((SUB, LANES), F32)] * 2
        totals = [jnp.zeros((SUB, LANES), F32)] * sides
        deeps = []
        for h in range(sides):
            span = pl.ds(h * LANES, LANES)
            deeps.append((land[at, span] * levels[at, span]).astype(F32))
        for k in range(count):
            values = [
                [tracer[c, k, at, pl.ds(h * LANES, LANES)] for h in range(sides)] for c in range(2)
            ]
            for h in range(sides):
                gain = jnp.maximum(deeps[h] - k, 0.0)
                totals[h] = totals[h] + gain * (values[0][h] - 0.75 * values[1][h])
            for c in range(2):
                i = c * count + k
                both = jnp.where(lanes < HALF, values[c][0], values[c][-1])
                both = put_lane(both, 0, i + 1)
                packed[i % 2] = jnp.where((lanes == i) | (lanes == i + 1), both, packed[i % 2])
        totals = [t * (0.8 / count) for t in totals]
        for h in range(sides):
            span = pl.ds(h * LANES, LANES)
            force[at, span] = totals[h]
            depth[at, span] = deeps[h]
        odd = (lanes & 1) == 1
        low = jnp.where(odd, packed[0], packed[1])
        high = jnp.where(odd, packed[1], packed[0])
        low = jnp.where(deeps[0][:, 0:1] > low_kind, low, 0.0)
        high = jnp.where(deeps[-1][:, LANES - 1 : LANES] > high_kind, high, 0.0)
        ends = [pl.ds(0, LANES), pl.ds((sides - 1) * LANES, LANES)]
        low, high = strip_pair(
            low,
            high,
            lanes,
            [(deeps[0], deeps[-1])]
            + [tuple(ref[at, span] for span in ends) for ref in (surf, flow_x, flow_y)]
            + [(totals[0], totals[-1])],
        )
        to = pl.ds(pl.multiple_of(first_row + r, SUB), SUB)
        for out, value in ((to_south, low), (to_north, high)):
            out[to, :] = jnp.where(keep, out[to, :], pltpu.roll(value, turn, 1))

    def edge_rows(out, line, tile):
        for h in range(sides):
            span = pl.ds(h * LANES, LANES)
            deep = depth[pl.ds(line, 1), span]
            for c in range(2):
                for k in range(count):
                    out[pl.ds(c * count + k, 1), span] = jnp.where(
                        deep > k, tracer[c, k, pl.ds(line, 1), span], 0.0
                    )
            for f, ref in enumerate((depth, surf, flow_x, flow_y, force)):
                out[pl.ds(base + f * SUB, SUB), span] = ref[pl.ds(tile, SUB), span]

    pl.when(step == 0)(lambda: edge_rows(to_previous, 0, 0))
    pl.when(step == steps - 1)(lambda: edge_rows(to_next, rows - 1, rows - SUB))


def column_pass(tracer, land, levels, surf, flow_x, flow_y):
    two, count, rows, cols = tracer.shape
    chunk = rows // 4
    flat = pl.BlockSpec((chunk, cols), lambda i: (i, 0))
    lines = (two * count + FIELDS * SUB, cols)
    strip = (rows // 2 + SUB, LANES)
    plain = jax.ShapeDtypeStruct((rows, cols), F32)
    shapes = [plain, plain] + [jax.ShapeDtypeStruct(s, F32) for s in (strip, strip, lines, lines)]
    return pl.pallas_call(
        column_kernel,
        grid=(rows // chunk,),
        in_specs=[pl.BlockSpec((two, count, chunk, cols), lambda i: (0, 0, i, 0))] + [flat] * 5,
        out_specs=[flat, flat] + [pl.BlockSpec(s.shape, lambda i: (0, 0)) for s in shapes[2:]],
        out_shape=shapes,
        compiler_params=pltpu.CompilerParams(vmem_limit_bytes=VMEM_LIMIT),
        cost_estimate=pl.CostEstimate(
            flops=6 * tracer.size, bytes_accessed=4 * tracer.size, transcendentals=0
        ),
        name="columns",
    )(tracer, land, levels, surf, flow_x, flow_y)


def pack_kernel(south_in, north_in, west, east, south_out, north_out):
    half = south_in.shape[0] - SUB
    sides = west.shape[1] // LANES
    lanes = lane_ids(SUB)
    strips = []
    for ref in (west, east):
        zero = jnp.zeros((SUB, LANES), F32)
        ends = [pl.ds(0, LANES), pl.ds((sides - 1) * LANES, LANES)]
        values = [
            tuple(ref[pl.ds(BASE + f * SUB, SUB), span] for span in ends) for f in range(FIELDS)
        ]
        strips.append(strip_pair(zero, zero, lanes, values))
    for index, (source, out) in enumerate(((south_in, south_out), (north_in, north_out))):
        out[pl.ds(0, half), :] = source[pl.ds(0, half), :]
        out[pl.ds(half, SUB), :] = jnp.where(
            lanes < HALF, strips[0][index], pltpu.roll(strips[1][index], HALF, 1)
        )


def pack_pass(to_south, to_north, west, east):
    shape = jax.ShapeDtypeStruct(to_south.shape, F32)
    return pl.pallas_call(
        pack_kernel,
        out_shape=[shape, shape],
        compiler_params=pltpu.CompilerParams(vmem_limit_bytes=VMEM_LIMIT),
        cost_estimate=pl.CostEstimate(
            flops=to_south.size, bytes_accessed=16 * to_south.size, transcendentals=0
        ),
        name="corners",
    )(to_south, to_north, west, east)


def message_rows(ref, rows, r):
    half = rows // 2
    if r < 0:
        return ref[pl.ds(half, SUB), :]
    if r >= rows:
        return pltpu.roll(ref[pl.ds(half, SUB), :], HALF, 1)
    if r < half:
        return ref[pl.ds(r, SUB), :]
    return pltpu.roll(ref[pl.ds(r - half, SUB), :], HALF, 1)


def outer_tile(south, north, rows, r, f, open_south, open_north, lanes):
    at = BASE + (f + 1) * WIDTH
    mixed = jnp.where(lanes < at, message_rows(south, rows, r), message_rows(north, rows, r))
    mixed = put_lane(mixed, at, 0)
    valid = ((lanes < WIDTH) & open_north) | ((lanes >= LANES - WIDTH) & open_south)
    return jnp.where(valid, mixed, 0.0)


def extend(target, base, f, field, west, east, south, north, open_south, open_north):
    rows, cols = field.shape
    sides = cols // LANES
    lanes = lane_ids(SUB)
    for r in range(-SUB, rows + 1, SUB):
        to = pl.ds(SUB + r, SUB)
        for h in range(sides):
            span = pl.ds(h * LANES, LANES)
            if r < 0:
                target[h, to, :] = west[pl.ds(base + f * SUB, SUB), span]
            elif r >= rows:
                target[h, to, :] = east[pl.ds(base + f * SUB, SUB), span]
            else:
                target[h, to, :] = field[pl.ds(r, SUB), span]
        target[sides, to, :] = outer_tile(
            south, north, rows, r, f, open_south, open_north, lanes
        )


def latitude_ends():
    place, size = lax.axis_index("gy"), lax.axis_size("gy")
    return place > 0, place < size - 1


def ring_shift(tiles, lanes):
    size = len(tiles)
    after = [pltpu.roll(t, LANES - 1, 1) for t in tiles]
    before = [pltpu.roll(t, 1, 1) for t in tiles]
    nxt = [jnp.where(lanes == LANES - 1, after[(h + 1) % size], after[h]) for h in range(size)]
    prv = [jnp.where(lanes == 0, before[(h - 1) % size], before[h]) for h in range(size)]
    return nxt, prv


def nine_sum(ref, r, lanes):
    sides = [ref[h, pl.ds(r + 1, SUB), :] + ref[h, pl.ds(r - 1, SUB), :] for h in range(ref.shape[0])]
    mixed = [ref[h, pl.ds(r, SUB), :] + 0.5 * sides[h] for h in range(ref.shape[0])]
    nxt, prv = ring_shift(mixed, lanes)
    return [sides[h] + (nxt[h] + prv[h]) for h in range(ref.shape[0])]


def peak_kernel(depth, west, east, south, north, peak, coded):
    rows, cols = depth.shape
    sides = cols // LANES
    lanes = lane_ids(SUB)
    open_south, open_north = latitude_ends()
    scale = 2.0 / (BASE // 2)
    extend(coded, BASE, 0, depth, west, east, south, north, open_south, open_north)
    for r in range(0, rows + 2 * SUB, SUB):
        for h in range(sides + 1):
            d = coded[h, pl.ds(r, SUB), :]
            coded[h, pl.ds(r, SUB), :] = d + jnp.where(d > 0, CODE, 0.0)
    best = jnp.full((SUB, LANES), 0.0, F32)
    for r in range(SUB, rows + SUB, SUB):
        sums = nine_sum(coded, r, lanes)
        for h in range(sides):
            wet, deep = decode(sums[h])
            d = depth[pl.ds(r - SUB, SUB), pl.ds(h * LANES, LANES)]
            best = jnp.maximum(best, d * wet + jnp.where(d > 0, deep, 0.0))
    best = jnp.max(jnp.max(best, axis=1, keepdims=True), axis=0, keepdims=True)
    peak[...] = jnp.broadcast_to(0.5 + scale * best, (SUB, LANES))


def decode(sums):
    wet = jnp.floor(sums * (2.0 / CODE)) * 0.5
    return wet, sums - CODE * wet


def peak_pass(depth, west, east, south, north):
    rows, cols = depth.shape
    ext = pltpu.VMEM((cols // LANES + 1, rows + 2 * SUB, LANES), F32)
    return pl.pallas_call(
        peak_kernel,
        out_shape=jax.ShapeDtypeStruct((SUB, LANES), F32),
        scratch_shapes=[ext],
        compiler_params=pltpu.CompilerParams(vmem_limit_bytes=VMEM_LIMIT),
        cost_estimate=pl.CostEstimate(
            flops=30 * depth.size, bytes_accessed=4 * depth.size, transcendentals=0
        ),
        name="peak",
    )(depth, west, east, south, north)


def tracer_kernel(start, tracer, zonal, merid, depth, west, east, south, north, *rest):
    out, edge_y, around, masked = rest[-4:]
    step = pl.program_id(0)
    rows, cols = depth.shape
    sides = cols // LANES
    count = BASE // 2
    level = step + start
    lanes = lane_ids(SUB)
    spans = [pl.ds(h * LANES, LANES) for h in range(sides)]

    @pl.when(step == 0)
    def _():
        open_south, open_north = latitude_ends()
        for h in range(sides):
            masked[0, h, pl.ds(0, SUB), :] = west[pl.ds(BASE, SUB), spans[h]]
            masked[0, h, pl.ds(SUB, rows), :] = depth[:, spans[h]]
            masked[0, h, pl.ds(SUB + rows, SUB), :] = east[pl.ds(BASE, SUB), spans[h]]
        for big in range(0, rows, 2 * SUB):
            shifted = []
            for r in (big, big + SUB):
                low, high = message_rows(south, rows, r), message_rows(north, rows, r)
                edge_y[0, pl.ds(r, SUB), :] = jnp.where(open_south, low, 0.0)
                edge_y[1, pl.ds(r, SUB), :] = jnp.where(
                    open_north, pltpu.roll(high, LANES - 2, 1), 0.0
                )
                tiles = [depth[pl.ds(r, SUB), span] for span in spans]
                tiles.append(
                    outer_tile(south, north, rows, r, 0, open_south, open_north, lanes)
                )
                shifted.append(ring_shift(tiles, lanes))
            at = pl.ds(big, 2 * SUB)
            for h in range(sides):
                around[0, h, at, :] = masked[0, h, pl.ds(SUB + big + 1, 2 * SUB), :].astype(BF16)
                around[1, h, at, :] = masked[0, h, pl.ds(SUB + big - 1, 2 * SUB), :].astype(BF16)
                for n in range(2):
                    pair = jnp.concatenate([shifted[0][n][h], shifted[1][n][h]], 0)
                    around[2 + n, h, at, :] = pair.astype(BF16)

    mark = level.astype(F32)
    for c in range(2):
        line = c * count + level
        group = pl.multiple_of(lax.div(line, SUB) * SUB, SUB)
        place = lax.rem(line, SUB)
        for h in range(sides):
            before = west[pl.ds(group, SUB), spans[h]]
            masked[c, h, pl.ds(0, SUB), :] = pltpu.roll(before, SUB - 1 - place, 0)
            after = east[pl.ds(group, SUB), spans[h]]
            masked[c, h, pl.ds(SUB + rows, SUB), :] = pltpu.roll(after, lax.rem(SUB - place, SUB), 0)
    for r in range(0, rows, SUB):
        for h in range(sides):
            here = depth[pl.ds(r, SUB), spans[h]] > mark
            for c in range(2):
                masked[c, h, pl.ds(SUB + r, SUB), :] = jnp.where(
                    here, tracer[c, 0, pl.ds(r, SUB), spans[h]], 0.0
                )
    mark_pair = jnp.full((2 * SUB, LANES), mark, F32).astype(BF16)
    one, none = jnp.ones((2 * SUB, LANES), BF16), jnp.zeros((2 * SUB, LANES), BF16)
    quarter = jnp.full((2 * SUB, LANES), 0.25, BF16)
    picks = []
    for c in range(2):
        line = c * count + level
        picks.append(((lanes >= line) & (lanes < line + HALF), lax.rem(LANES - line, LANES)))
    for big in range(0, rows, 2 * SUB):
        wide = pl.ds(big, 2 * SUB)
        pairs = []
        for h in range(sides):
            near = none
            for n in range(4):
                near = near + jnp.where(around[n, h, wide, :] > mark_pair, one, none)
            pairs.append(
                (
                    1.0 - 0.2 * near.astype(F32),
                    (zonal[0, wide, spans[h]] * quarter).astype(F32),
                    (merid[0, wide, spans[h]] * quarter).astype(F32),
                )
            )
        for sub in range(2):
            r = big + sub * SUB
            at = pl.ds(r, SUB)
            part = slice(sub * SUB, (sub + 1) * SUB)
            factors = []
            for h in range(sides):
                own, u, v = (value[part] for value in pairs[h])
                here = depth[at, spans[h]] > mark
                factors.append((here, own, 0.2 - u, 0.2 + u, 0.2 - v, 0.2 + v))
            for c in range(2):
                tiles = [masked[c, h, pl.ds(SUB + r, SUB), :] for h in range(sides)]
                pick, turn = picks[c]
                outer = pltpu.roll(jnp.where(pick, edge_y[0, at, :], edge_y[1, at, :]), turn, 1)
                after = [pltpu.roll(t, LANES - 1, 1) for t in tiles] + [outer]
                before = [outer] + [pltpu.roll(t, 1, 1) for t in tiles]
                for h in range(sides):
                    here, own, to_e, to_w, to_n, to_s = factors[h]
                    nxt = jnp.where(lanes == LANES - 1, after[h + 1], after[h])
                    prv = jnp.where(lanes == 0, before[h], before[h + 1])
                    value = own * tiles[h] + to_n * nxt + to_s * prv
                    value = value + to_e * masked[c, h, pl.ds(SUB + r + 1, SUB), :]
                    value = value + to_w * masked[c, h, pl.ds(SUB + r - 1, SUB), :]
                    out[c, 0, at, spans[h]] = jnp.where(
                        here, value, tracer[c, 0, at, spans[h]]
                    )


def tracer_pass(start, stop, tracer, zonal, merid, depth, west, east, south, north, into=None):
    two, count, rows, cols = tracer.shape
    sides = cols // LANES
    block = pl.BlockSpec((two, 1, rows, cols), lambda k: (0, k + start, 0, 0))
    speed = pl.BlockSpec((1, rows, cols), lambda k: (k + start, 0, 0))

    def fixed(value):
        return pl.BlockSpec(value.shape, lambda k: (0, 0))

    small = [depth, west, east, south, north]
    operands = [tracer, zonal, merid, *small]
    specs = [block, speed, speed] + [fixed(v) for v in small]
    aliases = {}
    if into is not None:
        aliases = {len(operands): 0}
        operands.append(into)
        specs.append(pl.BlockSpec(memory_space=pl.ANY))
    part = stop - start
    return pl.pallas_call(
        functools.partial(tracer_kernel, start),
        grid=(part,),
        in_specs=specs,
        out_specs=block,
        out_shape=jax.ShapeDtypeStruct(tracer.shape, F32),
        scratch_shapes=[
            pltpu.VMEM((2, rows, LANES), F32),
            pltpu.VMEM((4, sides, rows, LANES), BF16),
            pltpu.VMEM((2, sides, rows + 2 * SUB, LANES), F32),
        ],
        input_output_aliases=aliases,
        compiler_params=pltpu.CompilerParams(vmem_limit_bytes=VMEM_LIMIT),
        cost_estimate=pl.CostEstimate(
            flops=40 * tracer.size * part // count,
            bytes_accessed=10 * tracer.size * part // count,
            transcendentals=0,
        ),
        name="tracers",
    )(*operands)


def solve_kernel(
    peak, depth, surf, flow_x, flow_y, force, west, east, south, north,
    surf_out, x_out, y_out, deep, wet, surf0, flux_x, flux_y, forced, left, right, start, step_by, total,
):
    rows, cols = depth.shape
    sides = cols // LANES
    tiles = sides + 1
    lanes = lane_ids(SUB)
    open_south, open_north = latitude_ends()
    halo = (west, east, south, north, open_south, open_north)
    base = BASE
    scale = 1.0 / (base // 2)
    extend(deep, base, 0, depth, *halo)
    extend(surf0, base, 1, surf, *halo)
    extend(flux_x, base, 2, flow_x, *halo)
    extend(flux_y, base, 3, flow_y, *halo)
    extend(forced, base, 4, force, *halo)
    every = range(0, rows + 2 * SUB, SUB)
    inner = range(SUB, rows + SUB, SUB)

    for r in every:
        at = pl.ds(r, SUB)
        for h in range(tiles):
            d = deep[h, at, :] * scale
            m = jnp.where(d > 0, 1.0, 0.0)
            deep[h, at, :] = d
            wet[h, at, :] = m
            flux_x[h, at, :] = m * flux_x[h, at, :]
            flux_y[h, at, :] = m * flux_y[h, at, :]
            total[h, at, :] = m * surf0[h, at, :]
            step_by[h, at, :] = d * surf0[h, at, :]

    def clamp_rows(r):
        return min(max(r, 1), rows + 2 * SUB - SUB - 1)

    spans = [clamp_rows(r) for r in every]
    for r in spans:
        at = pl.ds(r, SUB)
        sum_wet = nine_sum(wet, r, lanes)
        sum_deep = nine_sum(deep, r, lanes)
        sum_f = nine_sum(total, r, lanes)
        sum_g = nine_sum(step_by, r, lanes)
        nxt, prv = ring_shift([flux_y[h, at, :] for h in range(tiles)], lanes)
        for h in range(tiles):
            d = deep[h, at, :]
            m = wet[h, at, :]
            inverse = 1.0 / (0.5 + 2.0 * (d * sum_wet[h] + m * sum_deep[h]))
            a = 2.0 * d * inverse
            b = 2.0 * m * inverse
            left[h, at, :] = a
            right[h, at, :] = b
            e = surf0[h, at, :]
            div = 0.5 * (
                flux_x[h, pl.ds(r + 1, SUB), :] - flux_x[h, pl.ds(r - 1, SUB), :]
            ) + 0.5 * (nxt[h] - prv[h])
            rhs = 0.5 * e + forced[h, at, :] - 0.5 * div
            start[h, at, :] = rhs * inverse - e + a * sum_f[h] + b * sum_g[h]

    top = peak[...]
    lowest = 0.5 / top
    shrink = (1.0 - lowest) * (1.0 - lowest)
    omega = jnp.full((SUB, LANES), 2.0, F32)
    for r in every:
        at = pl.ds(r, SUB)
        for h in range(tiles):
            z = start[h, at, :]
            total[h, at, :] = z
            step_by[h, at, :] = z
            flux_x[h, at, :] = wet[h, at, :] * z
            flux_y[h, at, :] = deep[h, at, :] * z
    for turn in range(1, ITERS):
        omega = 1.0 / (1.0 - omega * shrink * 0.25)
        for r in spans:
            at = pl.ds(r, SUB)
            sum_f = nine_sum(flux_x, r, lanes)
            sum_g = nine_sum(flux_y, r, lanes)
            for h in range(tiles):
                s = total[h, at, :]
                y = start[h, at, :] - s + left[h, at, :] * sum_f[h] + right[h, at, :] * sum_g[h]
                delta = omega * y + (omega - 1.0) * step_by[h, at, :]
                forced[h, at, :] = delta
        for r in every:
            at = pl.ds(r, SUB)
            for h in range(tiles):
                delta = forced[h, at, :]
                s = total[h, at, :] + delta
                total[h, at, :] = s
                step_by[h, at, :] = delta
                flux_x[h, at, :] = wet[h, at, :] * s
                flux_y[h, at, :] = deep[h, at, :] * s

    for r in every:
        at = pl.ds(r, SUB)
        for h in range(tiles):
            value = surf0[h, at, :] + total[h, at, :]
            if h == sides:
                value = jnp.where((lanes < WIDTH) & open_north, value, jnp.where(
                    (lanes >= LANES - WIDTH) & open_south, value, 0.0))
            total[h, at, :] = value
    for r in inner:
        at = pl.ds(r, SUB)
        back = pl.ds(r - SUB, SUB)
        nxt, prv = ring_shift([total[h, at, :] for h in range(tiles)], lanes)
        for h in range(sides):
            span = pl.ds(h * LANES, LANES)
            m = wet[h, at, :]
            surf_out[back, span] = total[h, at, :]
            slope = total[h, pl.ds(r + 1, SUB), :] - total[h, pl.ds(r - 1, SUB), :]
            x_out[back, span] = m * (flow_x[back, span] - 0.25 * slope)
            y_out[back, span] = m * (flow_y[back, span] - 0.25 * (nxt[h] - prv[h]))


def solve_pass(peak, depth, surf, flow_x, flow_y, force, west, east, south, north):
    rows, cols = depth.shape
    ext = pltpu.VMEM((cols // LANES + 1, rows + 2 * SUB, LANES), F32)
    shape = jax.ShapeDtypeStruct((rows, cols), F32)
    return pl.pallas_call(
        solve_kernel,
        out_shape=[shape] * 3,
        scratch_shapes=[ext] * 11,
        compiler_params=pltpu.CompilerParams(vmem_limit_bytes=VMEM_LIMIT),
        cost_estimate=pl.CostEstimate(
            flops=200 * depth.size, bytes_accessed=32 * depth.size, transcendentals=0
        ),
        name="solve",
    )(peak, depth, surf, flow_x, flow_y, force, west, east, south, north)


def both_ways(axis, to_next, to_previous):
    size = lax.axis_size(axis)
    up = [(i, (i + 1) % size) for i in range(size)]
    down = [(j, i) for i, j in up]
    return lax.ppermute(to_next, axis, up), lax.ppermute(to_previous, axis, down)


def spread_rounds(axis):
    size = lax.axis_size(axis)
    reach = 1
    while reach < size:
        if size & (size - 1) == 0:
            yield axis, [(i, i ^ reach) for i in range(size)]
        else:
            yield axis, [(i, (i + reach) % size) for i in range(size)]
        reach *= 2


def local(
    tracer, zonal_flow, meridional_flow, surface_prev, transport_x, transport_y, land_mask, levels
):
    count = tracer.shape[1]
    force, depth, to_south, to_north, to_previous, to_next = column_pass(
        tracer, land_mask, levels, surface_prev, transport_x, transport_y
    )
    fields = (depth, surface_prev, transport_x, transport_y, force)
    west, east = both_ways("gx", to_next, to_previous)
    to_south, to_north = pack_pass(to_south, to_north, west, east)
    south, north = both_ways("gy", to_north, to_south)
    halo = (west, east, south, north)
    peak = peak_pass(depth, *halo)
    tracer_next = None
    rounds = [r for axis in ("gx", "gy") for r in spread_rounds(axis)]
    cuts = [count * i // PARTS for i in range(PARTS + 1)]
    first = len(rounds) - PARTS
    for turn, (axis, pairs) in enumerate(rounds):
        moved = lax.ppermute(peak, axis, pairs)
        if turn >= first:
            part = turn - first
            tracer_next = tracer_pass(
                cuts[part], cuts[part + 1], tracer, zonal_flow, meridional_flow, depth, *halo,
                into=tracer_next,
            )
        peak = jnp.maximum(peak, moved)
        if first <= turn < len(rounds) - 1:
            peak, tracer_next = lax.optimization_barrier((peak, tracer_next))
    surf, next_x, next_y = solve_pass(peak, *fields, *halo)
    return (tracer_next, surf, next_x, next_y)


def solution(mesh):
    cell = P("gx", "gy")
    level = P(None, "gx", "gy")
    stack = P(None, None, "gx", "gy")
    return jax.shard_map(
        local,
        mesh=mesh,
        in_specs=(stack, level, level, cell, cell, cell, cell, cell),
        out_specs=(stack, cell, cell, cell),
        check_vma=False,
    )
```

time: 70.5 us -> 57.9 us (0.82)
  waiting for transfers between devices: 18.6 us -> 6.73 us
  Pallas kernels: 33.2 us -> 27.3 us
  starting transfers between devices: 9.96 us -> 13.5 us
  local copies, waits for them, and re-layouts: 5.91 us -> 9.29 us
  other arithmetic: 1.29 us -> 0.02 us
    ppermute x5, waiting for transfers between devices: 11.1 us -> 1.17 us  [local(): moved = lax.ppermute(peak, axis, pairs)]
    unnamed x13 -> x24, local copies, waits for them, and re-layouts: 5.2 us -> 9.29 us
    ppermute x5, starting transfers between devices: 2.77 us -> 5.67 us  [local(): moved = lax.ppermute(peak, axis, pairs)]
    pallas_call x3, Pallas kernels: 10.7 us -> 8.24 us  [the longest x1 7.65 us: solve_pass(): pl.pallas_call(solve_kernel, out_shape=[shape] * 3, scratch_shapes=[ext]...]
    pallas_call x1, Pallas kernels: 5.66 us -> 3.46 us  [column_pass(): pl.pallas_call(column_kernel, grid=(rows // chunk,), in_specs=[pl.BlockSp...]
    ppermute x2, waiting for transfers between devices: 2.31 us -> 0.69 us  [both_ways(): lax.ppermute(to_previous, axis, down)]
    ppermute x2, starting transfers between devices: 1.58 us -> 2.87 us  [both_ways(): lax.ppermute(to_next, axis, up)]
    max x5, other arithmetic: 1.29 us -> 0.02 us  [local(): peak = jnp.maximum(peak, moved)]
  transfers between devices with their start and end apart: 9 -> 9, of which waited for: 8 -> 4; matrix products, arithmetic and copies ran while one was open for 0% -> 0% of each run, Pallas kernels for 24% -> 27%
where the time goes in v1:
time: 57.9 us; the launch traced here: 57.6 us
  Pallas kernels  27.3 us (47%)
  starting transfers between devices  13.5 us (23%)
  local copies, waits for them, and re-layouts  9.29 us (16%)
  waiting for transfers between devices  6.73 us (12%)
  between operations  0.71 us (1%)
    pallas_call x4, Pallas kernels, tracer_pass(): pl.pallas_call(functools.partial(tracer_kernel, start), grid=(part,), in_...  15.6 us
    unnamed x24, local copies, waits for them, and re-layouts  9.29 us
    pallas_call x1, Pallas kernels, solve_pass(): pl.pallas_call(solve_kernel, out_shape=[shape] * 3, scratch_shapes=[ext]...  7.65 us
    ppermute x5, starting transfers between devices, local(): moved = lax.ppermute(peak, axis, pairs)  5.67 us
    ppermute x2, starting transfers between devices, both_ways(): lax.ppermute(to_previous, axis, down)  5.01 us
    ppermute x2, waiting for transfers between devices, both_ways(): lax.ppermute(to_next, axis, up)  4.87 us
    pallas_call x1, Pallas kernels, column_pass(): pl.pallas_call(column_kernel, grid=(rows // chunk,), in_specs=[pl.BlockSp...  3.46 us
    ppermute x2, starting transfers between devices, both_ways(): lax.ppermute(to_next, axis, up)  2.87 us
  transfers between devices with their start and end apart: 9, of which 4 were waited for; matrix products, arithmetic and copies ran while one was open for 0% of the time, Pallas kernels for 27%

profile of v1, /device:TPU:0, one launch (start us, length us, event | category | flops | bytes accessed | tf_op | source)
XLA Modules:
  0.0 57.6 jit_solution(3613594327956955273)
XLA Ops:
  0.6 0.0 copy-start
  0.6 3.1 %copy-done = f32[2,16,224,256]{3,2,1,0:T(8,128)S(1)} copy-done((f32[2,16,224,256]{3,2,1,0:T(8,128)S(1)}, f32[2,16,224,256]{3,2,1,0:T(8,128)}, u32[]{:S(2)}) %copy-start) | copy-done | bytes 7340056
  3.7 0.0 copy-start.4
  3.7 0.9 %copy-done.4 = f32[224,256]{1,0:T(8,128)S(1)} copy-done((f32[224,256]{1,0:T(8,128)S(1)}, f32[224,256]{1,0:T(8,128)}, u32[]{:S(2)}) %copy-start.4) | copy-done | bytes 229400
  4.7 0.0 copy-start.6
  4.7 0.9 %copy-done.6 = f32[224,256]{1,0:T(8,128)S(1)} copy-done((f32[224,256]{1,0:T(8,128)S(1)}, f32[224,256]{1,0:T(8,128)}, u32[]{:S(2)}) %copy-start.6) | copy-done | bytes 229400
  5.6 0.0 copy-start.8
  5.6 0.9 %copy-done.8 = f32[224,256]{1,0:T(8,128)S(1)} copy-done((f32[224,256]{1,0:T(8,128)S(1)}, f32[224,256]{1,0:T(8,128)}, u32[]{:S(2)}) %copy-start.8) | copy-done | bytes 229400
  6.5 0.0 copy-start.10
  6.5 0.9 %copy-done.10 = s32[224,256]{1,0:T(8,128)S(1)} copy-done((s32[224,256]{1,0:T(8,128)S(1)}, s32[224,256]{1,0:T(8,128)}, u32[]{:S(2)}) %copy-start.10) | copy-done | bytes 229400
  7.5 0.0 copy-start.11
  7.5 0.9 %copy-done.11 = s32[224,256]{1,0:T(8,128)S(1)} copy-done((s32[224,256]{1,0:T(8,128)S(1)}, s32[224,256]{1,0:T(8,128)}, u32[]{:S(2)}) %copy-start.11) | copy-done | bytes 229400
  8.4 0.0 copy-start.1
  8.4 0.0 copy-start.2
  8.4 3.5 %columns.1 = (f32[224,256]{1,0:T(8,128)S(1)}, f32[224,256]{1,0:T(8,128)S(1)}, f32[120,128]{1,0:T(8,128)S(1)}, f32[120,128]{1,0:T(8,128)S(1)}, f32[72,256]{1,0:T(8,128)S(1)}, /*index=5*/f32[72,256]{1,0:T(8,128)S(1)}) custom-call(f32[2,16,224,256]{3,2,1,0:T(8,128)S(1)} %copy-done, s32[224,256]{1,0:T(8,128)S(1)} %copy-done.10, s32[224,256]{1,0:T(8,128)S(1)} %copy-done.11, ...), custom_call_target="tpu_custom_call" | custom-call | flops 11010048 | bytes 7340032 | tf_op jit(solution)/shard_map/columns/pallas_call | solution.py:127
  11.9 0.5 collective-permute-start
  12.4 2.9 %collective-permute-start.1 = (f32[72,256]{1,0:T(8,128)S(1)}, f32[72,256]{1,0:T(8,128)S(1)}, u32[]{:S(2)}, u32[]{:S(2)}) collective-permute-start(f32[72,256]{1,0:T(8,128)S(1)} %get-tuple-element.23), channel_id=1, source_target_pairs={{4,0},{8,4},{12,8},{16,12},{20,16},{24,20},{28,24},{0,28},{5,1},{9... | collective-permute-start | bytes 221192 | tf_op jit(solution)/shard_map/ppermute | solution.py:549
  15.4 2.0 %collective-permute-done.west = f32[72,256]{1,0:T(8,128)S(1)} collective-permute-done((f32[72,256]{1,0:T(8,128)S(1)}, f32[72,256]{1,0:T(8,128)S(1)}, u32[]{:S(2)}, u32[]{:S(2)}) %collective-permute-start) | collective-permute-done | bytes 73760 | tf_op jit(solution)/shard_map/ppermute | solution.py:549
  17.3 0.0 collective-permute-done.1.east
  17.3 0.1 corners.1
  17.5 2.3 %collective-permute-start.2 = (f32[120,128]{1,0:T(8,128)S(1)}, f32[120,128]{1,0:T(8,128)S(1)}, u32[]{:S(2)}, u32[]{:S(2)}) collective-permute-start(f32[120,128]{1,0:T(8,128)S(1)} %get-tuple-element.26), channel_id=1, source_target_pairs={{0,1},{1,2},{2,3},{3,0},{4,5},{5,6},{6,7},{7,4},{8,9},{9,10},{10,1... | collective-permute-start | bytes 184328 | tf_op jit(solution)/shard_map/ppermute | solution.py:549
  19.8 2.1 %collective-permute-start.3 = (f32[120,128]{1,0:T(8,128)S(1)}, f32[120,128]{1,0:T(8,128)S(1)}, u32[]{:S(2)}, u32[]{:S(2)}) collective-permute-start(f32[120,128]{1,0:T(8,128)S(1)} %get-tuple-element.27), channel_id=1, source_target_pairs={{1,0},{2,1},{3,2},{0,3},{5,4},{6,5},{7,6},{4,7},{9,8},{10,9},{11,1... | collective-permute-start | bytes 184328 | tf_op jit(solution)/shard_map/ppermute | solution.py:549
  21.9 2.9 %collective-permute-done.2.south = f32[120,128]{1,0:T(8,128)S(1)} collective-permute-done((f32[120,128]{1,0:T(8,128)S(1)}, f32[120,128]{1,0:T(8,128)S(1)}, u32[]{:S(2)}, u32[]{:S(2)}) %collective-permute-start.2) | collective-permute-done | bytes 61472 | tf_op jit(solution)/shard_map/ppermute | solution.py:549
  24.8 0.7 %collective-permute-done.3.north = f32[120,128]{1,0:T(8,128)S(1)} collective-permute-done((f32[120,128]{1,0:T(8,128)S(1)}, f32[120,128]{1,0:T(8,128)S(1)}, u32[]{:S(2)}, u32[]{:S(2)}) %collective-permute-start.3) | collective-permute-done | bytes 61472 | tf_op jit(solution)/shard_map/ppermute | solution.py:549
  25.5 0.4 peak.1
  25.9 0.0 collective-permute-start.4
  25.9 1.2 %collective-permute-done.4 = f32[8,128]{1,0:T(8,128)S(1)} collective-permute-done((f32[8,128]{1,0:T(8,128)S(1)}, f32[8,128]{1,0:T(8,128)S(1)}, u32[]{:S(2)}, u32[]{:S(2)}) %collective-permute-start.4) | collective-permute-done | bytes 4128 | tf_op jit(solution)/shard_map/ppermute | solution.py:581
  27.1 0.9 %collective-permute-start.5 = (f32[8,128]{1,0:T(8,128)S(1)}, f32[8,128]{1,0:T(8,128)S(1)}, u32[]{:S(2)}, u32[]{:S(2)}) collective-permute-start(f32[8,128]{1,0:T(8,128)S(1)} %max.15), channel_id=1, source_target_pairs={{0,8},{4,12},{8,0},{12,4},{16,24},{20,28},{24,16},{28,20},{1,9},{5... | collective-permute-start | bytes 12296 | tf_op jit(solution)/shard_map/ppermute | solution.py:581
  28.0 0.0 copy-done.1
  28.0 0.0 copy-done.2
  28.0 0.0 copy-start.3
  28.0 1.5 %copy-done.3 = bf16[16,224,256]{2,1,0:T(8,128)(2,1)S(1)} copy-done((bf16[16,224,256]{2,1,0:T(8,128)(2,1)S(1)}, bf16[16,224,256]{2,1,0:T(8,128)(2,1)}, u32[]{:S(2)}) %copy-start.3) | copy-done | bytes 1835032
  29.5 3.9 %tracers.4.rest_0_ = f32[2,16,224,256]{3,2,1,0:T(8,128)} custom-call(f32[2,16,224,256]{3,2,1,0:T(8,128)S(1)} %copy-done.1, bf16[16,224,256]{2,1,0:T(8,128)(2,1)S(1)} %copy-done.2, bf16[16,224,256]{2,1,0:T(8,128)(2,1)S(1)} %copy-done.3, f32[224,256]{1,0:T(8,128)S(1)} %get-tuple-element.21.depth, f32[72,256]{1,0:T(8,128)S(1)} %collective-permute-done.west, ...), custom_call_target="tpu_custom_call" | custom-call | flops 18350080 | bytes 4587520 | tf_op jit(solution)/shard_map/tracers/pallas_call | solution.py:395
  33.4 0.0 collective-permute-done.5
  33.4 1.5 %collective-permute-start.6 = (f32[8,128]{1,0:T(8,128)S(1)}, f32[8,128]{1,0:T(8,128)S(1)}, u32[]{:S(2)}, u32[]{:S(2)}) collective-permute-start(f32[8,128]{1,0:T(8,128)S(1)} %max.16), channel_id=1, source_target_pairs={{0,16},{4,20},{8,24},{12,28},{16,0},{20,4},{24,8},{28,12},{1,17},{... | collective-permute-start | bytes 12296 | tf_op jit(solution)/shard_map/ppermute | solution.py:581
  34.9 3.9 %tracers.5.rest_0_ = f32[2,16,224,256]{3,2,1,0:T(8,128)} custom-call(f32[2,16,224,256]{3,2,1,0:T(8,128)S(1)} %copy-done.1, bf16[16,224,256]{2,1,0:T(8,128)(2,1)S(1)} %copy-done.2, bf16[16,224,256]{2,1,0:T(8,128)(2,1)S(1)} %copy-done.3, f32[224,256]{1,0:T(8,128)S(1)} %get-tuple-element.21.depth, ...), custom_call_target="tpu_custom_call", output_to_operand_aliasing={{}: (8, {})} | custom-call | flops 18350080 | bytes 4587520 | tf_op jit(solution)/shard_map/tracers/pallas_call | solution.py:395
  38.8 0.0 collective-permute-done.6
  38.8 1.0 %collective-permute-start.7 = (f32[8,128]{1,0:T(8,128)S(1)}, f32[8,128]{1,0:T(8,128)S(1)}, u32[]{:S(2)}, u32[]{:S(2)}) collective-permute-start(f32[8,128]{1,0:T(8,128)S(1)} %max.17), channel_id=1, source_target_pairs={{0,1},{1,0},{2,3},{3,2},{4,5},{5,4},{6,7},{7,6},{8,9},{9,8},{10,11... | collective-permute-start | bytes 12296 | tf_op jit(solution)/shard_map/ppermute | solution.py:581
  39.8 3.9 %tracers.6.rest_0_ = f32[2,16,224,256]{3,2,1,0:T(8,128)} custom-call(f32[2,16,224,256]{3,2,1,0:T(8,128)S(1)} %copy-done.1, bf16[16,224,256]{2,1,0:T(8,128)(2,1)S(1)} %copy-done.2, bf16[16,224,256]{2,1,0:T(8,128)(2,1)S(1)} %copy-done.3, f32[224,256]{1,0:T(8,128)S(1)} %get-tuple-element.21.depth, ...), custom_call_target="tpu_custom_call", output_to_operand_aliasing={{}: (8, {})} | custom-call | flops 18350080 | bytes 4587520 | tf_op jit(solution)/shard_map/tracers/pallas_call | solution.py:395
  43.7 0.0 collective-permute-done.7
  43.7 0.0 copy-start.5
  43.7 0.0 copy-start.7
  43.7 0.0 copy-start.9
  43.7 2.3 %collective-permute-start.8 = (f32[8,128]{1,0:T(8,128)S(1)}, f32[8,128]{1,0:T(8,128)S(1)}, u32[]{:S(2)}, u32[]{:S(2)}) collective-permute-start(f32[8,128]{1,0:T(8,128)S(1)} %max.18), channel_id=1, source_target_pairs={{0,2},{1,3},{2,0},{3,1},{4,6},{5,7},{6,4},{7,5},{8,10},{9,11},{10,... | collective-permute-start | bytes 12296 | tf_op jit(solution)/shard_map/ppermute | solution.py:581
  46.0 3.9 %tracers.7 = f32[2,16,224,256]{3,2,1,0:T(8,128)} custom-call(f32[2,16,224,256]{3,2,1,0:T(8,128)S(1)} %copy-done.1, bf16[16,224,256]{2,1,0:T(8,128)(2,1)S(1)} %copy-done.2, bf16[16,224,256]{2,1,0:T(8,128)(2,1)S(1)} %copy-done.3, f32[224,256]{1,0:T(8,128)S(1)} %get-tuple-element.21.depth, ...), custom_call_target="tpu_custom_call", output_to_operand_aliasing={{}: (8, {})} | custom-call | flops 18350080 | bytes 4587520 | tf_op jit(solution)/shard_map/tracers/pallas_call | solution.py:395
  49.9 0.0 collective-permute-done.8
  49.9 0.0 copy-done.5
  49.9 0.0 copy-done.7
  49.9 0.0 copy-done.9
  49.9 7.6 %solve.1 = (f32[224,256]{1,0:T(8,128)}, f32[224,256]{1,0:T(8,128)}, f32[224,256]{1,0:T(8,128)}) custom-call(f32[8,128]{1,0:T(8,128)S(1)} %max.19.peak, f32[224,256]{1,0:T(8,128)S(1)} %get-tuple-element.21.depth, f32[224,256]{1,0:T(8,128)S(1)} %copy-done.5, f32[224,256]{1,0:T(8,128)S(1)} %copy-done.7, f32[224,256]{1,0:T(8,128)S(1)} %copy-done.9, ...), custom_call_target="tpu_custom_call" | custom-call | flops 11468800 | bytes 1835008 | tf_op jit(solution)/shard_map/solve/pallas_call | solution.py:533
  (5 shorter events, 0.0 us)
Async XLA Ops:
  0.6 3.1 %copy-start = (f32[2,16,224,256]{3,2,1,0:T(8,128)S(1)}, f32[2,16,224,256]{3,2,1,0:T(8,128)}, u32[]{:S(2)}) copy-start(f32[2,16,224,256]{3,2,1,0:T(8,128)} %tracer.9) | copy-start | bytes 22020100
  3.7 0.9 %copy-start.4 = (f32[224,256]{1,0:T(8,128)S(1)}, f32[224,256]{1,0:T(8,128)}, u32[]{:S(2)}) copy-start(f32[224,256]{1,0:T(8,128)} %surf.3) | copy-start | bytes 688132
  4.7 0.9 %copy-start.6 = (f32[224,256]{1,0:T(8,128)S(1)}, f32[224,256]{1,0:T(8,128)}, u32[]{:S(2)}) copy-start(f32[224,256]{1,0:T(8,128)} %flow_x.3) | copy-start | bytes 688132
  5.6 0.9 %copy-start.8 = (f32[224,256]{1,0:T(8,128)S(1)}, f32[224,256]{1,0:T(8,128)}, u32[]{:S(2)}) copy-start(f32[224,256]{1,0:T(8,128)} %flow_y.3) | copy-start | bytes 688132
  6.5 0.9 %copy-start.10 = (s32[224,256]{1,0:T(8,128)S(1)}, s32[224,256]{1,0:T(8,128)}, u32[]{:S(2)}) copy-start(s32[224,256]{1,0:T(8,128)} %land.1) | copy-start | bytes 688132
  7.5 0.9 %copy-start.11 = (s32[224,256]{1,0:T(8,128)S(1)}, s32[224,256]{1,0:T(8,128)}, u32[]{:S(2)}) copy-start(s32[224,256]{1,0:T(8,128)} %levels.1) | copy-start | bytes 688132
  8.4 19.6 %copy-start.1 = (f32[2,16,224,256]{3,2,1,0:T(8,128)S(1)}, f32[2,16,224,256]{3,2,1,0:T(8,128)}, u32[]{:S(2)}) copy-start(f32[2,16,224,256]{3,2,1,0:T(8,128)} %tracer.9) | copy-start | bytes 22020100
  8.4 19.6 %copy-start.2 = (bf16[16,224,256]{2,1,0:T(8,128)(2,1)S(1)}, bf16[16,224,256]{2,1,0:T(8,128)(2,1)}, u32[]{:S(2)}) copy-start(bf16[16,224,256]{2,1,0:T(8,128)(2,1)} %zonal.7) | copy-start | bytes 5505028
  11.9 5.5 %collective-permute-start = (f32[72,256]{1,0:T(8,128)S(1)}, f32[72,256]{1,0:T(8,128)S(1)}, u32[]{:S(2)}, u32[]{:S(2)}) collective-permute-start(f32[72,256]{1,0:T(8,128)S(1)} %get-tuple-element.22), channel_id=1, source_target_pairs={{0,4},{4,8},{8,12},{12,16},{16,20},{20,24},{24,28},{28,0},{1,5},{5... | collective-permute-start | bytes 221192 | tf_op jit(solution)/shard_map/ppermute | solution.py:549
  12.4 4.9 %collective-permute-start.1 = (f32[72,256]{1,0:T(8,128)S(1)}, f32[72,256]{1,0:T(8,128)S(1)}, u32[]{:S(2)}, u32[]{:S(2)}) collective-permute-start(f32[72,256]{1,0:T(8,128)S(1)} %get-tuple-element.23), channel_id=1, source_target_pairs={{4,0},{8,4},{12,8},{16,12},{20,16},{24,20},{28,24},{0,28},{5,1},{9... | collective-permute-start | bytes 221192 | tf_op jit(solution)/shard_map/ppermute | solution.py:549
  17.5 7.3 %collective-permute-start.2 = (f32[120,128]{1,0:T(8,128)S(1)}, f32[120,128]{1,0:T(8,128)S(1)}, u32[]{:S(2)}, u32[]{:S(2)}) collective-permute-start(f32[120,128]{1,0:T(8,128)S(1)} %get-tuple-element.26), channel_id=1, source_target_pairs={{0,1},{1,2},{2,3},{3,0},{4,5},{5,6},{6,7},{7,4},{8,9},{9,10},{10,1... | collective-permute-start | bytes 184328 | tf_op jit(solution)/shard_map/ppermute | solution.py:549
  19.8 5.7 %collective-permute-start.3 = (f32[120,128]{1,0:T(8,128)S(1)}, f32[120,128]{1,0:T(8,128)S(1)}, u32[]{:S(2)}, u32[]{:S(2)}) collective-permute-start(f32[120,128]{1,0:T(8,128)S(1)} %get-tuple-element.27), channel_id=1, source_target_pairs={{1,0},{2,1},{3,2},{0,3},{5,4},{6,5},{7,6},{4,7},{9,8},{10,9},{11,1... | collective-permute-start | bytes 184328 | tf_op jit(solution)/shard_map/ppermute | solution.py:549
  25.9 1.2 %collective-permute-start.4 = (f32[8,128]{1,0:T(8,128)S(1)}, f32[8,128]{1,0:T(8,128)S(1)}, u32[]{:S(2)}, u32[]{:S(2)}) collective-permute-start(f32[8,128]{1,0:T(8,128)S(1)} %peak.1), channel_id=1, source_target_pairs={{0,4},{4,0},{8,12},{12,8},{16,20},{20,16},{24,28},{28,24},{1,5},{5... | collective-permute-start | bytes 12296 | tf_op jit(solution)/shard_map/ppermute | solution.py:581
  27.1 6.3 %collective-permute-start.5 = (f32[8,128]{1,0:T(8,128)S(1)}, f32[8,128]{1,0:T(8,128)S(1)}, u32[]{:S(2)}, u32[]{:S(2)}) collective-permute-start(f32[8,128]{1,0:T(8,128)S(1)} %max.15), channel_id=1, source_target_pairs={{0,8},{4,12},{8,0},{12,4},{16,24},{20,28},{24,16},{28,20},{1,9},{5... | collective-permute-start | bytes 12296 | tf_op jit(solution)/shard_map/ppermute | solution.py:581
  28.0 1.5 %copy-start.3 = (bf16[16,224,256]{2,1,0:T(8,128)(2,1)S(1)}, bf16[16,224,256]{2,1,0:T(8,128)(2,1)}, u32[]{:S(2)}) copy-start(bf16[16,224,256]{2,1,0:T(8,128)(2,1)} %merid.7) | copy-start | bytes 5505028
  33.4 5.4 %collective-permute-start.6 = (f32[8,128]{1,0:T(8,128)S(1)}, f32[8,128]{1,0:T(8,128)S(1)}, u32[]{:S(2)}, u32[]{:S(2)}) collective-permute-start(f32[8,128]{1,0:T(8,128)S(1)} %max.16), channel_id=1, source_target_pairs={{0,16},{4,20},{8,24},{12,28},{16,0},{20,4},{24,8},{28,12},{1,17},{... | collective-permute-start | bytes 12296 | tf_op jit(solution)/shard_map/ppermute | solution.py:581
  38.8 4.9 %collective-permute-start.7 = (f32[8,128]{1,0:T(8,128)S(1)}, f32[8,128]{1,0:T(8,128)S(1)}, u32[]{:S(2)}, u32[]{:S(2)}) collective-permute-start(f32[8,128]{1,0:T(8,128)S(1)} %max.17), channel_id=1, source_target_pairs={{0,1},{1,0},{2,3},{3,2},{4,5},{5,4},{6,7},{7,6},{8,9},{9,8},{10,11... | collective-permute-start | bytes 12296 | tf_op jit(solution)/shard_map/ppermute | solution.py:581
  43.7 6.2 %copy-start.5 = (f32[224,256]{1,0:T(8,128)S(1)}, f32[224,256]{1,0:T(8,128)}, u32[]{:S(2)}) copy-start(f32[224,256]{1,0:T(8,128)} %surf.3) | copy-start | bytes 688132
  43.7 6.2 %copy-start.7 = (f32[224,256]{1,0:T(8,128)S(1)}, f32[224,256]{1,0:T(8,128)}, u32[]{:S(2)}) copy-start(f32[224,256]{1,0:T(8,128)} %flow_x.3) | copy-start | bytes 688132
  43.7 6.2 %copy-start.9 = (f32[224,256]{1,0:T(8,128)S(1)}, f32[224,256]{1,0:T(8,128)}, u32[]{:S(2)}) copy-start(f32[224,256]{1,0:T(8,128)} %flow_y.3) | copy-start | bytes 688132
  43.7 6.2 %collective-permute-start.8 = (f32[8,128]{1,0:T(8,128)S(1)}, f32[8,128]{1,0:T(8,128)S(1)}, u32[]{:S(2)}, u32[]{:S(2)}) collective-permute-start(f32[8,128]{1,0:T(8,128)S(1)} %max.18), channel_id=1, source_target_pairs={{0,2},{1,3},{2,0},{3,1},{4,6},{5,7},{6,4},{7,5},{8,10},{9,11},{10,... | collective-permute-start | bytes 12296 | tf_op jit(solution)/shard_map/ppermute | solution.py:581

commit v2 on v1

v2 whole, which is shorter than its diff:
```python
import functools

import jax
import jax.numpy as jnp
from jax import lax
from jax.experimental import pallas as pl
from jax.experimental.pallas import tpu as pltpu
from jax.sharding import PartitionSpec as P

ITERS = 4
WIDTH = ITERS + 1
LANES = 128
SUB = 8
HALF = LANES // 2
FIELDS = 5
F32 = jnp.float32
BF16 = jnp.bfloat16
VMEM_LIMIT = 12 * 1024 * 1024
LEVELS = 16
BASE = 2 * LEVELS
CODE = 1024.0
PARTS = 4
CHUNKS = 4


def lane_ids(rows):
    return lax.broadcasted_iota(jnp.int32, (rows, LANES), 1)


def put_lane(value, source, target):
    shift = (target - source) % LANES
    return pltpu.roll(value, shift, 1) if shift else value


def strip_pair(low, high, lanes, values):
    for f, (begin, end) in enumerate(values):
        at = BASE + (f + 1) * WIDTH
        turned = put_lane(jnp.where(lanes < HALF, begin, end), 0, at)
        low = jnp.where((lanes >= at) & (lanes < at + WIDTH), turned, low)
        high = jnp.where((lanes >= at - WIDTH) & (lanes < at), turned, high)
    return low, high


def column_kernel(
    tracer_hbm, land_hbm, levels_hbm, surf_hbm, flow_x_hbm, flow_y_hbm,
    force, depth, to_south, to_north, to_previous, to_next, tracer, surf, flow_x, flow_y,
    land, levels, flat_sem, chunk_sem,
):
    count = tracer.shape[1]
    rows, cols = land.shape
    sides = cols // LANES
    base = 2 * count
    lanes = lane_ids(SUB)
    size = rows // CHUNKS

    def copy_in(i):
        part = pl.ds(pl.multiple_of(i * size, SUB), size)
        return pltpu.make_async_copy(
            tracer_hbm.at[:, :, part, :], tracer.at[:, :, part, :], chunk_sem.at[i]
        )

    flats = [
        pltpu.make_async_copy(source, target, flat_sem.at[i])
        for i, (source, target) in enumerate(
            (
                (land_hbm, land),
                (levels_hbm, levels),
                (surf_hbm, surf),
                (flow_x_hbm, flow_x),
                (flow_y_hbm, flow_y),
            )
        )
    ]
    for copy in flats:
        copy.start()
    for i in range(CHUNKS):
        copy_in(i).start()
    low_kind = jnp.where((lanes >= 1) & (lanes <= base), lax.rem(lanes - 1 + count, count), -1)
    low_kind = low_kind.astype(F32)
    high_kind = jnp.where(lanes < base, lax.rem(lanes, count), -1).astype(F32)
    odd = (lanes & 1) == 1
    ends = [pl.ds(0, LANES), pl.ds((sides - 1) * LANES, LANES)]
    for copy in flats:
        copy.wait()

    def chunk(i, carry):
        copy_in(i).wait()
        upper = i >= CHUNKS // 2
        turn = jnp.where(upper, HALF, 0)
        keep = (lanes < HALF) & upper
        first_row = jnp.where(upper, i - CHUNKS // 2, i) * size
        for r in range(0, size, SUB):
            at = pl.ds(pl.multiple_of(i * size + r, SUB), SUB)
            packed = [jnp.zeros((SUB, LANES), F32)] * 2
            totals = [jnp.zeros((SUB, LANES), F32)] * sides
            deeps = []
            for h in range(sides):
                span = pl.ds(h * LANES, LANES)
                deeps.append((land[at, span] * levels[at, span]).astype(F32))
            for k in range(count):
                values = [
                    [tracer[c, k, at, pl.ds(h * LANES, LANES)] for h in range(sides)]
                    for c in range(2)
                ]
                for h in range(sides):
                    gain = jnp.maximum(deeps[h] - k, 0.0)
                    totals[h] = totals[h] + gain * (values[0][h] - 0.75 * values[1][h])
                for c in range(2):
                    line = c * count + k
                    both = jnp.where(lanes < HALF, values[c][0], values[c][-1])
                    both = put_lane(both, 0, line + 1)
                    packed[line % 2] = jnp.where(
                        (lanes == line) | (lanes == line + 1), both, packed[line % 2]
                    )
            totals = [t * (0.8 / count) for t in totals]
            for h in range(sides):
                span = pl.ds(h * LANES, LANES)
                force[at, span] = totals[h]
                depth[at, span] = deeps[h]
            low = jnp.where(odd, packed[0], packed[1])
            high = jnp.where(odd, packed[1], packed[0])
            low = jnp.where(deeps[0][:, 0:1] > low_kind, low, 0.0)
            high = jnp.where(deeps[-1][:, LANES - 1 : LANES] > high_kind, high, 0.0)
            low, high = strip_pair(
                low,
                high,
                lanes,
                [(deeps[0], deeps[-1])]
                + [tuple(ref[at, span] for span in ends) for ref in (surf, flow_x, flow_y)]
                + [(totals[0], totals[-1])],
            )
            to = pl.ds(pl.multiple_of(first_row + r, SUB), SUB)
            for out, value in ((to_south, low), (to_north, high)):
                out[to, :] = jnp.where(keep, out[to, :], pltpu.roll(value, turn, 1))
        return carry

    lax.fori_loop(0, CHUNKS, chunk, 0)
    for out, line, tile in ((to_previous, 0, 0), (to_next, rows - 1, rows - SUB)):
        for h in range(sides):
            span = pl.ds(h * LANES, LANES)
            deep = depth[pl.ds(line, 1), span]
            for c in range(2):
                for k in range(count):
                    out[pl.ds(c * count + k, 1), span] = jnp.where(
                        deep > k, tracer[c, k, pl.ds(line, 1), span], 0.0
                    )
            for f, ref in enumerate((depth, surf, flow_x, flow_y, force)):
                out[pl.ds(base + f * SUB, SUB), span] = ref[pl.ds(tile, SUB), span]


IN_HBM = pl.BlockSpec(memory_space=pltpu.HBM)
IN_VMEM = pl.BlockSpec(memory_space=pltpu.VMEM)


def column_pass(tracer, land, levels, surf, flow_x, flow_y):
    two, count, rows, cols = tracer.shape
    lines = (two * count + FIELDS * SUB, cols)
    strip = (rows // 2 + SUB, LANES)
    plain = (rows, cols)
    shapes = [plain, plain, strip, strip, lines, lines, tracer.shape, plain, plain, plain]
    return pl.pallas_call(
        column_kernel,
        in_specs=[IN_HBM] * 6,
        out_specs=[IN_VMEM] * len(shapes),
        out_shape=[jax.ShapeDtypeStruct(shape, F32) for shape in shapes],
        scratch_shapes=[
            pltpu.VMEM(plain, jnp.int32),
            pltpu.VMEM(plain, jnp.int32),
            pltpu.SemaphoreType.DMA((5,)),
            pltpu.SemaphoreType.DMA((CHUNKS,)),
        ],
        compiler_params=pltpu.CompilerParams(vmem_limit_bytes=VMEM_LIMIT),
        cost_estimate=pl.CostEstimate(
            flops=6 * tracer.size, bytes_accessed=4 * tracer.size, transcendentals=0
        ),
        name="columns",
    )(
        *(
            pltpu.with_memory_space_constraint(value, pltpu.HBM)
            for value in (tracer, land, levels, surf, flow_x, flow_y)
        )
    )


def pack_kernel(south_in, north_in, west, east, south_out, north_out):
    half = south_in.shape[0] - SUB
    sides = west.shape[1] // LANES
    lanes = lane_ids(SUB)
    strips = []
    for ref in (west, east):
        zero = jnp.zeros((SUB, LANES), F32)
        ends = [pl.ds(0, LANES), pl.ds((sides - 1) * LANES, LANES)]
        values = [
            tuple(ref[pl.ds(BASE + f * SUB, SUB), span] for span in ends) for f in range(FIELDS)
        ]
        strips.append(strip_pair(zero, zero, lanes, values))
    for index, (source, out) in enumerate(((south_in, south_out), (north_in, north_out))):
        out[pl.ds(0, half), :] = source[pl.ds(0, half), :]
        out[pl.ds(half, SUB), :] = jnp.where(
            lanes < HALF, strips[0][index], pltpu.roll(strips[1][index], HALF, 1)
        )


def pack_pass(to_south, to_north, west, east):
    shape = jax.ShapeDtypeStruct(to_south.shape, F32)
    return pl.pallas_call(
        pack_kernel,
        out_shape=[shape, shape],
        compiler_params=pltpu.CompilerParams(vmem_limit_bytes=VMEM_LIMIT),
        cost_estimate=pl.CostEstimate(
            flops=to_south.size, bytes_accessed=16 * to_south.size, transcendentals=0
        ),
        name="corners",
    )(to_south, to_north, west, east)


def message_rows(ref, rows, r):
    half = rows // 2
    if r < 0:
        return ref[pl.ds(half, SUB), :]
    if r >= rows:
        return pltpu.roll(ref[pl.ds(half, SUB), :], HALF, 1)
    if r < half:
        return ref[pl.ds(r, SUB), :]
    return pltpu.roll(ref[pl.ds(r - half, SUB), :], HALF, 1)


def outer_tile(south, north, rows, r, f, open_south, open_north, lanes):
    at = BASE + (f + 1) * WIDTH
    mixed = jnp.where(lanes < at, message_rows(south, rows, r), message_rows(north, rows, r))
    mixed = put_lane(mixed, at, 0)
    valid = ((lanes < WIDTH) & open_north) | ((lanes >= LANES - WIDTH) & open_south)
    return jnp.where(valid, mixed, 0.0)


def extend(target, base, f, field, west, east, south, north, open_south, open_north):
    rows, cols = field.shape
    sides = cols // LANES
    lanes = lane_ids(SUB)
    for r in range(-SUB, rows + 1, SUB):
        to = pl.ds(SUB + r, SUB)
        for h in range(sides):
            span = pl.ds(h * LANES, LANES)
            if r < 0:
                target[h, to, :] = west[pl.ds(base + f * SUB, SUB), span]
            elif r >= rows:
                target[h, to, :] = east[pl.ds(base + f * SUB, SUB), span]
            else:
                target[h, to, :] = field[pl.ds(r, SUB), span]
        target[sides, to, :] = outer_tile(
            south, north, rows, r, f, open_south, open_north, lanes
        )


def latitude_ends():
    place, size = lax.axis_index("gy"), lax.axis_size("gy")
    return place > 0, place < size - 1


def ring_shift(tiles, lanes):
    size = len(tiles)
    after = [pltpu.roll(t, LANES - 1, 1) for t in tiles]
    before = [pltpu.roll(t, 1, 1) for t in tiles]
    nxt = [jnp.where(lanes == LANES - 1, after[(h + 1) % size], after[h]) for h in range(size)]
    prv = [jnp.where(lanes == 0, before[(h - 1) % size], before[h]) for h in range(size)]
    return nxt, prv


def nine_sum(ref, r, lanes):
    sides = [ref[h, pl.ds(r + 1, SUB), :] + ref[h, pl.ds(r - 1, SUB), :] for h in range(ref.shape[0])]
    mixed = [ref[h, pl.ds(r, SUB), :] + 0.5 * sides[h] for h in range(ref.shape[0])]
    nxt, prv = ring_shift(mixed, lanes)
    return [sides[h] + (nxt[h] + prv[h]) for h in range(ref.shape[0])]


def peak_kernel(depth, west, east, south, north, peak, coded):
    rows, cols = depth.shape
    sides = cols // LANES
    lanes = lane_ids(SUB)
    open_south, open_north = latitude_ends()
    scale = 2.0 / (BASE // 2)
    extend(coded, BASE, 0, depth, west, east, south, north, open_south, open_north)
    for r in range(0, rows + 2 * SUB, SUB):
        for h in range(sides + 1):
            d = coded[h, pl.ds(r, SUB), :]
            coded[h, pl.ds(r, SUB), :] = d + jnp.where(d > 0, CODE, 0.0)
    best = jnp.full((SUB, LANES), 0.0, F32)
    for r in range(SUB, rows + SUB, SUB):
        sums = nine_sum(coded, r, lanes)
        for h in range(sides):
            wet, deep = decode(sums[h])
            d = depth[pl.ds(r - SUB, SUB), pl.ds(h * LANES, LANES)]
            best = jnp.maximum(best, d * wet + jnp.where(d > 0, deep, 0.0))
    best = jnp.max(jnp.max(best, axis=1, keepdims=True), axis=0, keepdims=True)
    peak[...] = jnp.broadcast_to(0.5 + scale * best, (SUB, LANES))


def decode(sums):
    wet = jnp.floor(sums * (2.0 / CODE)) * 0.5
    return wet, sums - CODE * wet


def peak_pass(depth, west, east, south, north):
    rows, cols = depth.shape
    ext = pltpu.VMEM((cols // LANES + 1, rows + 2 * SUB, LANES), F32)
    return pl.pallas_call(
        peak_kernel,
        out_shape=jax.ShapeDtypeStruct((SUB, LANES), F32),
        scratch_shapes=[ext],
        compiler_params=pltpu.CompilerParams(vmem_limit_bytes=VMEM_LIMIT),
        cost_estimate=pl.CostEstimate(
            flops=30 * depth.size, bytes_accessed=4 * depth.size, transcendentals=0
        ),
        name="peak",
    )(depth, west, east, south, north)


def tracer_kernel(start, stop, tracer, zonal, merid, depth, west, east, south, north, *rest):
    out, edge_y, around, masked = rest[-4:]
    rows, cols = depth.shape
    sides = cols // LANES
    count = BASE // 2
    lanes = lane_ids(SUB)
    spans = [pl.ds(h * LANES, LANES) for h in range(sides)]

    if start == 0:
        open_south, open_north = latitude_ends()
        for h in range(sides):
            masked[0, h, pl.ds(0, SUB), :] = west[pl.ds(BASE, SUB), spans[h]]
            masked[0, h, pl.ds(SUB, rows), :] = depth[:, spans[h]]
            masked[0, h, pl.ds(SUB + rows, SUB), :] = east[pl.ds(BASE, SUB), spans[h]]
        for big in range(0, rows, 2 * SUB):
            shifted = []
            for r in (big, big + SUB):
                low, high = message_rows(south, rows, r), message_rows(north, rows, r)
                edge_y[0, pl.ds(r, SUB), :] = jnp.where(open_south, low, 0.0)
                edge_y[1, pl.ds(r, SUB), :] = jnp.where(
                    open_north, pltpu.roll(high, LANES - 2, 1), 0.0
                )
                tiles = [depth[pl.ds(r, SUB), span] for span in spans]
                tiles.append(
                    outer_tile(south, north, rows, r, 0, open_south, open_north, lanes)
                )
                shifted.append(ring_shift(tiles, lanes))
            at = pl.ds(big, 2 * SUB)
            for h in range(sides):
                around[0, h, at, :] = masked[0, h, pl.ds(SUB + big + 1, 2 * SUB), :].astype(BF16)
                around[1, h, at, :] = masked[0, h, pl.ds(SUB + big - 1, 2 * SUB), :].astype(BF16)
                for n in range(2):
                    pair = jnp.concatenate([shifted[0][n][h], shifted[1][n][h]], 0)
                    around[2 + n, h, at, :] = pair.astype(BF16)

    def one_level(level, carry):
        mark = lax.convert_element_type(level, F32)
        for c in range(2):
            line = c * count + level
            group = pl.multiple_of(lax.div(line, SUB) * SUB, SUB)
            place = lax.rem(line, SUB)
            for h in range(sides):
                before = west[pl.ds(group, SUB), spans[h]]
                masked[c, h, pl.ds(0, SUB), :] = pltpu.roll(before, SUB - 1 - place, 0)
                after = east[pl.ds(group, SUB), spans[h]]
                masked[c, h, pl.ds(SUB + rows, SUB), :] = pltpu.roll(after, lax.rem(SUB - place, SUB), 0)
        for r in range(0, rows, SUB):
            for h in range(sides):
                here = depth[pl.ds(r, SUB), spans[h]] > mark
                for c in range(2):
                    masked[c, h, pl.ds(SUB + r, SUB), :] = jnp.where(
                        here, tracer[c, level, pl.ds(r, SUB), spans[h]], 0.0
                    )
        mark_pair = jnp.full((2 * SUB, LANES), mark, F32).astype(BF16)
        one, none = jnp.ones((2 * SUB, LANES), BF16), jnp.zeros((2 * SUB, LANES), BF16)
        quarter = jnp.full((2 * SUB, LANES), 0.25, BF16)
        picks = []
        for c in range(2):
            line = c * count + level
            picks.append(((lanes >= line) & (lanes < line + HALF), lax.rem(LANES - line, LANES)))
        for big in range(0, rows, 2 * SUB):
            wide = pl.ds(big, 2 * SUB)
            pairs = []
            for h in range(sides):
                near = none
                for n in range(4):
                    near = near + jnp.where(around[n, h, wide, :] > mark_pair, one, none)
                pairs.append(
                    (
                        1.0 - 0.2 * near.astype(F32),
                        (zonal[level, wide, spans[h]] * quarter).astype(F32),
                        (merid[level, wide, spans[h]] * quarter).astype(F32),
                    )
                )
            for sub in range(2):
                r = big + sub * SUB
                at = pl.ds(r, SUB)
                part = slice(sub * SUB, (sub + 1) * SUB)
                factors = []
                for h in range(sides):
                    own, u, v = (value[part] for value in pairs[h])
                    here = depth[at, spans[h]] > mark
                    factors.append((here, own, 0.2 - u, 0.2 + u, 0.2 - v, 0.2 + v))
                for c in range(2):
                    tiles = [masked[c, h, pl.ds(SUB + r, SUB), :] for h in range(sides)]
                    pick, turn = picks[c]
                    outer = pltpu.roll(jnp.where(pick, edge_y[0, at, :], edge_y[1, at, :]), turn, 1)
                    after = [pltpu.roll(t, LANES - 1, 1) for t in tiles] + [outer]
                    before = [outer] + [pltpu.roll(t, 1, 1) for t in tiles]
                    for h in range(sides):
                        here, own, to_e, to_w, to_n, to_s = factors[h]
                        nxt = jnp.where(lanes == LANES - 1, after[h + 1], after[h])
                        prv = jnp.where(lanes == 0, before[h], before[h + 1])
                        value = own * tiles[h] + to_n * nxt + to_s * prv
                        value = value + to_e * masked[c, h, pl.ds(SUB + r + 1, SUB), :]
                        value = value + to_w * masked[c, h, pl.ds(SUB + r - 1, SUB), :]
                        out[c, level, at, spans[h]] = jnp.where(
                            here, value, tracer[c, level, at, spans[h]]
                        )
        return carry

    lax.fori_loop(start, stop, one_level, 0)


def tracer_pass(start, stop, tracer, zonal, merid, depth, west, east, south, north, before=()):
    two, count, rows, cols = tracer.shape
    sides = cols // LANES
    operands = [tracer, zonal, merid, depth, west, east, south, north, *before]
    first = len(operands) - len(before)
    shapes = [
        jax.ShapeDtypeStruct(tracer.shape, F32),
        jax.ShapeDtypeStruct((2, rows, LANES), F32),
        jax.ShapeDtypeStruct((4, sides, rows, LANES), BF16),
    ]
    part = stop - start
    return pl.pallas_call(
        functools.partial(tracer_kernel, start, stop),
        in_specs=[IN_VMEM] * len(operands),
        out_specs=[IN_VMEM] * 3,
        out_shape=shapes,
        scratch_shapes=[pltpu.VMEM((2, sides, rows + 2 * SUB, LANES), F32)],
        input_output_aliases={first + i: i for i in range(len(before))},
        compiler_params=pltpu.CompilerParams(vmem_limit_bytes=VMEM_LIMIT),
        cost_estimate=pl.CostEstimate(
            flops=40 * tracer.size * part // count,
            bytes_accessed=10 * tracer.size * part // count,
            transcendentals=0,
        ),
        name="tracers",
    )(*operands)


def group_of(tiles):
    return max(n for n in range(1, 8) if tiles % n == 0)


def solve_kernel(
    tracer_in, peak, depth, surf, flow_x, flow_y, force, west, east, south, north,
    tracer_hbm, surf_out, x_out, y_out,
    old, deep, deep_n, deep_s, coded, flux, part, ease, pairs, now, then, total, sem,
):
    rows, cols = depth.shape
    sides = cols // LANES
    tiles = sides + 1
    lanes = lane_ids(SUB)
    scale = 2.0 / BASE
    open_south, open_north = latitude_ends()
    beyond = ((lanes < WIDTH) & open_north) | ((lanes >= LANES - WIDTH) & open_south)
    outward = pltpu.make_async_copy(tracer_in, tracer_hbm, sem)
    outward.start()

    lowest = 0.5 / peak[...]
    shrink = (1.0 - lowest) * (1.0 - lowest)
    omega = jnp.full((SUB, LANES), 2.0, F32)
    weights, change = [jnp.ones((SUB, LANES), F32)], [jnp.ones((SUB, LANES), F32)]
    for _ in range(1, ITERS):
        omega = 1.0 / (1.0 - omega * shrink * 0.25)
        resid = [1.0 - weights[0]] + [p - w for p, w in zip(weights, weights[1:])] + [weights[-1]]
        held = change + [jnp.zeros((SUB, LANES), F32)]
        change = [omega * y + (omega - 1.0) * d for y, d in zip(resid, held)]
        weights = [w + d for w, d in zip(weights + [jnp.zeros((SUB, LANES), F32)], change)]

    edge = (pl.ds(0, SUB), pl.ds(rows + 3 * SUB, SUB))
    for ref in (deep, deep_n, deep_s, coded, flux):
        for at in edge:
            for h in range(tiles):
                ref[h, at, :] = jnp.zeros((SUB, LANES), F32)
    for ref in (pairs, now, then):
        for i in range(ref.shape[0]):
            for at in edge:
                for h in range(tiles):
                    ref[i, h, at, :] = jnp.zeros((SUB, LANES), F32)

    def spread(ref, at, values):
        nxt, prv = ring_shift(values, lanes)
        for h in range(tiles):
            ref[0, h, at, :] = values[h]
            ref[1, h, at, :] = nxt[h]
            ref[2, h, at, :] = prv[h]

    def load_tile(to, field, low, high):
        def ring(f):
            at = BASE + (f + 1) * WIDTH
            outer = put_lane(jnp.where(lanes < at, low, high), at, 0)
            return [field(f, h) for h in range(sides)] + [jnp.where(beyond, outer, 0.0)]

        levels = ring(0)
        deeps = [v * scale for v in levels]
        wets = [jnp.where(v > 0, 1.0, 0.0) for v in levels]
        nxt, prv = ring_shift(deeps, lanes)
        surfs, drives = ring(1), ring(4)
        cross, crosses = ring_shift([m * v for m, v in zip(wets, ring(3))], lanes)
        along = ring(2)
        for h in range(tiles):
            deep[h, to, :] = deeps[h]
            deep_n[h, to, :] = nxt[h]
            deep_s[h, to, :] = prv[h]
            coded[h, to, :] = levels[h] + CODE * wets[h]
            old[h, to, :] = surfs[h]
            flux[h, to, :] = wets[h] * along[h]
            part[h, to, :] = 0.5 * surfs[h] + drives[h] - 0.25 * (cross[h] - crosses[h])
        spread(now, to, [m * v for m, v in zip(wets, surfs)])

    fields = (depth, surf, flow_x, flow_y, force)
    half = rows // 2
    for ref, to, turn in ((west, SUB, 0), (east, rows + 2 * SUB, HALF)):
        tail = [message[pl.ds(half, SUB), :] for message in (south, north)]
        if turn:
            tail = [pltpu.roll(v, turn, 1) for v in tail]
        load_tile(
            pl.ds(to, SUB),
            lambda f, h, ref=ref: ref[pl.ds(BASE + f * SUB, SUB), pl.ds(h * LANES, LANES)],
            *tail,
        )
    size = rows // CHUNKS

    def load_chunk(i, carry):
        upper = i >= CHUNKS // 2
        turn = jnp.where(upper, HALF, 0)
        first_row = jnp.where(upper, i - CHUNKS // 2, i) * size
        for r in range(0, size, SUB):
            at = pl.ds(pl.multiple_of(i * size + r, SUB), SUB)
            line = pl.ds(pl.multiple_of(first_row + r, SUB), SUB)
            load_tile(
                pl.ds(pl.multiple_of(i * size + r + 2 * SUB, SUB), SUB),
                lambda f, h, at=at: fields[f][at, pl.ds(h * LANES, LANES)],
                *(pltpu.roll(message[line, :], turn, 1) for message in (south, north)),
            )
        return carry

    lax.fori_loop(0, CHUNKS, load_chunk, 0)

    count = rows // SUB + 2
    group = group_of(count)

    def over_tiles(body):
        def step(i, carry):
            window = pl.ds(pl.multiple_of(i * (group * SUB), SUB), (group + 2) * SUB)

            def view(ref, *index):
                return ref.at[(*index, window, slice(None))]

            for j in range(SUB, (group + 1) * SUB, SUB):
                body(view, j)
            return carry

        lax.fori_loop(0, count // group, step, 0)

    def nine(view, source, j, near, far):
        result = []
        for h in range(tiles):
            def value(i, shift):
                return view(source, i, h)[pl.ds(j + shift, SUB), :]

            side = near[h][0] * value(0, 1) + near[h][1] * value(0, -1)
            side = side + near[h][2] * value(1, 0) + near[h][3] * value(2, 0)
            corner = far[h][0] * value(1, 1) + far[h][1] * value(1, -1)
            corner = corner + far[h][2] * value(2, 1) + far[h][3] * value(2, -1)
            result.append(side + corner)
        return result

    def prepare(view, j):
        mixed, sides_of = [], []
        for h in range(tiles):
            code = view(coded, h)
            sides_of.append(code[pl.ds(j + 1, SUB), :] + code[pl.ds(j - 1, SUB), :])
            mixed.append(code[pl.ds(j, SUB), :] + 0.5 * sides_of[h])
        nxt, prv = ring_shift(mixed, lanes)
        near, far, inverses, masks = [], [], [], []
        for h in range(tiles):
            own = view(deep, h)[pl.ds(j, SUB), :]
            wet_sum, deep_sum = decode(sides_of[h] + (nxt[h] + prv[h]))
            wet = jnp.where(own > 0, 1.0, 0.0)
            diag = 0.5 + 2.0 * (own * wet_sum + wet * (deep_sum * scale))
            inverse = 1.0 / diag
            inverses.append(inverse)
            masks.append(wet)
            ease_h = wet * inverse
            view(ease, h)[pl.ds(j, SUB), :] = ease_h
            twice = own + own
            e = twice + 2.0 * view(deep, h)[pl.ds(j + 1, SUB), :]
            w = twice + 2.0 * view(deep, h)[pl.ds(j - 1, SUB), :]
            n = twice + 2.0 * view(deep_n, h)[pl.ds(j, SUB), :]
            s = twice + 2.0 * view(deep_s, h)[pl.ds(j, SUB), :]
            ne = own + view(deep_n, h)[pl.ds(j + 1, SUB), :]
            nw = own + view(deep_n, h)[pl.ds(j - 1, SUB), :]
            se = own + view(deep_s, h)[pl.ds(j + 1, SUB), :]
            sw = own + view(deep_s, h)[pl.ds(j - 1, SUB), :]
            for i, value in enumerate((e, n, s, ne, nw, se, sw)):
                view(pairs, i, h)[pl.ds(j, SUB), :] = value
            near.append((e, w, n, s))
            far.append((ne, nw, se, sw))
        sums = nine(view, now, j, near, far)
        firsts = []
        for h in range(tiles):
            e = view(old, h)[pl.ds(j, SUB), :]
            across = view(flux, h)[pl.ds(j + 1, SUB), :] - view(flux, h)[pl.ds(j - 1, SUB), :]
            drive = view(part, h)[pl.ds(j, SUB), :] - 0.25 * across
            z = drive * inverses[h] - e + masks[h] * inverses[h] * sums[h]
            view(total, h)[pl.ds(j, SUB), :] = e + weights[0] * z
            firsts.append(masks[h] * z)
        nxt, prv = ring_shift(firsts, lanes)
        for h in range(tiles):
            for i, value in enumerate((firsts[h], nxt[h], prv[h])):
                view(then, i, h)[pl.ds(j, SUB), :] = value

    over_tiles(prepare)

    source, target = then, now
    for k in range(1, ITERS):
        def apply(view, j, k=k, source=source, target=target):
            near, far = [], []
            for h in range(tiles):
                def pair(i, shift=0):
                    return view(pairs, i, h)[pl.ds(j + shift, SUB), :]

                near.append((pair(0), pair(0, -1), pair(1), pair(2)))
                far.append((pair(3), pair(4), pair(5), pair(6)))
            sums = nine(view, source, j, near, far)
            values = [view(ease, h)[pl.ds(j, SUB), :] * sums[h] for h in range(tiles)]
            for h in range(tiles):
                here = view(total, h)
                here[pl.ds(j, SUB), :] = here[pl.ds(j, SUB), :] + weights[k] * values[h]
            if k < ITERS - 1:
                nxt, prv = ring_shift(values, lanes)
                for h in range(tiles):
                    for i, value in enumerate((values[h], nxt[h], prv[h])):
                        view(target, i, h)[pl.ds(j, SUB), :] = value

        over_tiles(apply)
        source, target = target, source

    def finish(i, carry):
        window = pl.ds(pl.multiple_of(i * size + SUB, SUB), size + 2 * SUB)
        for r in range(0, size, SUB):
            j = r + SUB
            at = pl.ds(pl.multiple_of(i * size + r, SUB), SUB)
            views = [total.at[h, window, :] for h in range(tiles)]
            here = [v[pl.ds(j, SUB), :] for v in views]
            here[sides] = jnp.where(beyond, here[sides], 0.0)
            nxt, prv = ring_shift(here, lanes)
            for h in range(sides):
                span = pl.ds(h * LANES, LANES)
                wet = depth[at, span] > 0
                slope = views[h][pl.ds(j + 1, SUB), :] - views[h][pl.ds(j - 1, SUB), :]
                surf_out[at, span] = here[h]
                x_out[at, span] = jnp.where(wet, flow_x[at, span] - 0.25 * slope, 0.0)
                y_out[at, span] = jnp.where(
                    wet, flow_y[at, span] - 0.25 * (nxt[h] - prv[h]), 0.0
                )
        return carry

    lax.fori_loop(0, CHUNKS, finish, 0)
    outward.wait()


def solve_pass(tracer, peak, depth, surf, flow_x, flow_y, force, west, east, south, north):
    rows, cols = depth.shape
    shape = (cols // LANES + 1, rows + 4 * SUB, LANES)
    ext = pltpu.VMEM(shape, F32)
    three = pltpu.VMEM((3, *shape), F32)
    plain = jax.ShapeDtypeStruct((rows, cols), F32)
    return pl.pallas_call(
        solve_kernel,
        in_specs=[IN_VMEM] * 11,
        out_specs=[IN_HBM] + [IN_VMEM] * 3,
        out_shape=[jax.ShapeDtypeStruct(tracer.shape, F32)] + [plain] * 3,
        scratch_shapes=[ext] * 8
        + [pltpu.VMEM((7, *shape), F32), three, three, ext, pltpu.SemaphoreType.DMA],
        compiler_params=pltpu.CompilerParams(vmem_limit_bytes=VMEM_LIMIT),
        cost_estimate=pl.CostEstimate(
            flops=200 * depth.size, bytes_accessed=32 * depth.size, transcendentals=0
        ),
        name="solve",
    )(tracer, peak, depth, surf, flow_x, flow_y, force, west, east, south, north)


def both_ways(axis, to_next, to_previous):
    size = lax.axis_size(axis)
    up = [(i, (i + 1) % size) for i in range(size)]
    down = [(j, i) for i, j in up]
    return lax.ppermute(to_next, axis, up), lax.ppermute(to_previous, axis, down)


def spread_rounds(axis):
    size = lax.axis_size(axis)
    reach = 1
    while reach < size:
        if size & (size - 1) == 0:
            yield axis, [(i, i ^ reach) for i in range(size)]
        else:
            yield axis, [(i, (i + reach) % size) for i in range(size)]
        reach *= 2


def local(
    tracer, zonal_flow, meridional_flow, surface_prev, transport_x, transport_y, land_mask, levels
):
    count = tracer.shape[1]
    (
        force, depth, to_south, to_north, to_previous, to_next,
        tracer, surface_prev, transport_x, transport_y,
    ) = column_pass(tracer, land_mask, levels, surface_prev, transport_x, transport_y)
    west, east = both_ways("gx", to_next, to_previous)
    to_south, to_north = pack_pass(to_south, to_north, west, east)
    south, north = both_ways("gy", to_north, to_south)
    halo = (west, east, south, north)
    peak = peak_pass(depth, *halo)
    state = ()
    rounds = [r for axis in ("gx", "gy") for r in spread_rounds(axis)]
    cuts = [count * i // PARTS for i in range(PARTS + 1)]
    first = len(rounds) - PARTS
    for turn, (axis, pairs) in enumerate(rounds):
        moved = lax.ppermute(peak, axis, pairs)
        if turn >= first:
            part = turn - first
            state = tracer_pass(
                cuts[part], cuts[part + 1], tracer, zonal_flow, meridional_flow, depth, *halo,
                before=state,
            )
        peak = jnp.maximum(peak, moved)
        if first <= turn < len(rounds) - 1:
            peak, state = lax.optimization_barrier((peak, state))
    return solve_pass(
        state[0], peak, depth, surface_prev, transport_x, transport_y, force, *halo
    )


def solution(mesh):
    cell = P("gx", "gy")
    level = P(None, "gx", "gy")
    stack = P(None, None, "gx", "gy")
    return jax.shard_map(
        local,
        mesh=mesh,
        in_specs=(stack, level, level, cell, cell, cell, cell, cell),
        out_specs=(stack, cell, cell, cell),
        check_vma=False,
    )
```

time: 57.9 us -> 44.5 us (0.77)
  local copies, waits for them, and re-layouts: 9.29 us -> 0.01 us
  Pallas kernels: 27.3 us -> 21.9 us
  waiting for transfers between devices: 6.73 us -> 8.21 us
    unnamed x24 -> x4, local copies, waits for them, and re-layouts: 9.29 us -> 0.01 us
    pallas_call x6, Pallas kernels: 26.7 us -> 21.3 us  [the longest x4 8.41 us: tracer_pass(): pl.pallas_call(functools.partial(tracer_kernel, start, stop), in_specs=[I...]
    ppermute x5, waiting for transfers between devices: 1.17 us -> 2.66 us  [local(): moved = lax.ppermute(peak, axis, pairs)]
  transfers between devices with their start and end apart: 9 -> 9, of which waited for: 4 -> 7; matrix products, arithmetic and copies ran while one was open for 0% -> 0% of each run, Pallas kernels for 27% -> 19%
where the time goes in v2:
time: 44.5 us; the launch traced here: 44.3 us
  Pallas kernels  21.9 us (49%)
  starting transfers between devices  13.4 us (30%)
  waiting for transfers between devices  8.21 us (18%)
  between operations  0.72 us (2%)
    pallas_call x4, Pallas kernels, tracer_pass(): pl.pallas_call(functools.partial(tracer_kernel, start, stop), in_specs=[I...  8.41 us
    pallas_call x1, Pallas kernels, solve_pass(): pl.pallas_call(solve_kernel, in_specs=[IN_VMEM] * 11, out_specs=[IN_HBM]...  6.81 us
    pallas_call x1, Pallas kernels, column_pass(): pl.pallas_call(column_kernel, in_specs=[IN_HBM] * 6, out_specs=[IN_VMEM]...  6.13 us
    ppermute x5, starting transfers between devices, local(): moved = lax.ppermute(peak, axis, pairs)  5.53 us
    ppermute x2, starting transfers between devices, both_ways(): lax.ppermute(to_previous, axis, down)  5.01 us
    ppermute x2, waiting for transfers between devices, both_ways(): lax.ppermute(to_next, axis, up)  4.87 us
    ppermute x2, starting transfers between devices, both_ways(): lax.ppermute(to_next, axis, up)  2.87 us
    ppermute x5, waiting for transfers between devices, local(): moved = lax.ppermute(peak, axis, pairs)  2.66 us
  transfers between devices with their start and end apart: 9, of which 7 were waited for; matrix products, arithmetic and copies ran while one was open for 0% of the time, Pallas kernels for 19%

profile of v2, /device:TPU:0, one launch (start us, length us, event | category | flops | bytes accessed | tf_op | source)
XLA Modules:
  0.0 44.3 jit_solution(11343088997103539197)
XLA Ops:
  0.6 0.0 copy-start.1
  0.6 0.0 copy-start
  0.7 6.1 %columns.1 = (f32[224,256]{1,0:T(8,128)S(1)}, f32[224,256]{1,0:T(8,128)S(1)}, f32[120,128]{1,0:T(8,128)S(1)}, f32[120,128]{1,0:T(8,128)S(1)}, f32[72,256]{1,0:T(...) custom-call(f32[2,16,224,256]{3,2,1,0:T(8,128)} %tracer_hbm.1, ...), custom_call_target="tpu_custom_call" | custom-call | flops 11010048 | bytes 7340032 | tf_op jit(solution)/shard_map/columns/pallas_call | solution.py:161
  6.8 0.5 %collective-permute-start = (f32[72,256]{1,0:T(8,128)S(1)}, f32[72,256]{1,0:T(8,128)S(1)}, u32[]{:S(2)}, u32[]{:S(2)}) collective-permute-start(f32[72,256]{1,0:T(8,128)S(1)} %get-tuple-element.40), channel_id=1, source_target_pairs={{0,4},{4,8},{8,12},{12,16},{16,20},{20,24},{24,28},{28,0},{1,5},{5... | collective-permute-start | bytes 221192 | tf_op jit(solution)/shard_map/ppermute | solution.py:699
  7.3 2.9 %collective-permute-start.1 = (f32[72,256]{1,0:T(8,128)S(1)}, f32[72,256]{1,0:T(8,128)S(1)}, u32[]{:S(2)}, u32[]{:S(2)}) collective-permute-start(f32[72,256]{1,0:T(8,128)S(1)} %get-tuple-element.41), channel_id=1, source_target_pairs={{4,0},{8,4},{12,8},{16,12},{20,16},{24,20},{28,24},{0,28},{5,1},{9... | collective-permute-start | bytes 221192 | tf_op jit(solution)/shard_map/ppermute | solution.py:699
  10.3 2.0 %collective-permute-done.west = f32[72,256]{1,0:T(8,128)S(1)} collective-permute-done((f32[72,256]{1,0:T(8,128)S(1)}, f32[72,256]{1,0:T(8,128)S(1)}, u32[]{:S(2)}, u32[]{:S(2)}) %collective-permute-start) | collective-permute-done | bytes 73760 | tf_op jit(solution)/shard_map/ppermute | solution.py:699
  12.2 0.0 collective-permute-done.1.east
  12.3 0.1 corners.1
  12.4 2.3 %collective-permute-start.2 = (f32[120,128]{1,0:T(8,128)S(1)}, f32[120,128]{1,0:T(8,128)S(1)}, u32[]{:S(2)}, u32[]{:S(2)}) collective-permute-start(f32[120,128]{1,0:T(8,128)S(1)} %get-tuple-element.44), channel_id=1, source_target_pairs={{0,1},{1,2},{2,3},{3,0},{4,5},{5,6},{6,7},{7,4},{8,9},{9,10},{10,1... | collective-permute-start | bytes 184328 | tf_op jit(solution)/shard_map/ppermute | solution.py:699
  14.7 2.1 %collective-permute-start.3 = (f32[120,128]{1,0:T(8,128)S(1)}, f32[120,128]{1,0:T(8,128)S(1)}, u32[]{:S(2)}, u32[]{:S(2)}) collective-permute-start(f32[120,128]{1,0:T(8,128)S(1)} %get-tuple-element.45), channel_id=1, source_target_pairs={{1,0},{2,1},{3,2},{0,3},{5,4},{6,5},{7,6},{4,7},{9,8},{10,9},{11,1... | collective-permute-start | bytes 184328 | tf_op jit(solution)/shard_map/ppermute | solution.py:699
  16.8 2.9 %collective-permute-done.2.south = f32[120,128]{1,0:T(8,128)S(1)} collective-permute-done((f32[120,128]{1,0:T(8,128)S(1)}, f32[120,128]{1,0:T(8,128)S(1)}, u32[]{:S(2)}, u32[]{:S(2)}) %collective-permute-start.2) | collective-permute-done | bytes 61472 | tf_op jit(solution)/shard_map/ppermute | solution.py:699
  19.7 0.7 %collective-permute-done.3.north = f32[120,128]{1,0:T(8,128)S(1)} collective-permute-done((f32[120,128]{1,0:T(8,128)S(1)}, f32[120,128]{1,0:T(8,128)S(1)}, u32[]{:S(2)}, u32[]{:S(2)}) %collective-permute-start.3) | collective-permute-done | bytes 61472 | tf_op jit(solution)/shard_map/ppermute | solution.py:699
  20.4 0.5 %peak.1 = f32[8,128]{1,0:T(8,128)S(1)} custom-call(f32[224,256]{1,0:T(8,128)S(1)} %get-tuple-element.39.depth, f32[72,256]{1,0:T(8,128)S(1)} %collective-permute-done.west, f32[72,256]{1,0:T(8,128)S(1)} %collective-permute-done.1.east, f32[120,128]{1,0:T(8,128)S(1)} %collective-permute-done.2.south, f32[120,128]{1,0:T(8,128)S(1)} %collective-permute-done.3.north), custom_call_target="tpu_custom_call" | custom-call | flops 1720320 | bytes 229376 | tf_op jit(solution)/shard_map/peak/pallas_call | solution.py:306
  20.8 0.0 collective-permute-start.4
  20.8 1.2 %collective-permute-done.4 = f32[8,128]{1,0:T(8,128)S(1)} collective-permute-done((f32[8,128]{1,0:T(8,128)S(1)}, f32[8,128]{1,0:T(8,128)S(1)}, u32[]{:S(2)}, u32[]{:S(2)}) %collective-permute-start.4) | collective-permute-done | bytes 4128 | tf_op jit(solution)/shard_map/ppermute | solution.py:731
  22.0 0.9 %collective-permute-start.5 = (f32[8,128]{1,0:T(8,128)S(1)}, f32[8,128]{1,0:T(8,128)S(1)}, u32[]{:S(2)}, u32[]{:S(2)}) collective-permute-start(f32[8,128]{1,0:T(8,128)S(1)} %max.15), channel_id=1, source_target_pairs={{0,8},{4,12},{8,0},{12,4},{16,24},{20,28},{24,16},{28,20},{1,9},{5... | collective-permute-start | bytes 12296 | tf_op jit(solution)/shard_map/ppermute | solution.py:731
  22.9 0.0 copy-done.1
  22.9 0.0 copy-done
  22.9 2.8 %tracers.4 = (f32[2,16,224,256]{3,2,1,0:T(8,128)S(1)}, f32[2,224,128]{2,1,0:T(8,128)S(1)}, bf16[4,2,224,128]{3,2,1,0:T(8,128)(2,1)S(1)}) custom-call(f32[2,16,224,256]{3,2,1,0:T(8,128)S(1)} %get-tuple-element.38.tracer, bf16[16,224,256]{2,1,0:T(8,128)(2,1)S(1)} %copy-done, bf16[16,224,256]{2,1,0:T(8,128)(2,1)S(1)} %copy-done.1, ...), custom_call_target="tpu_custom_call" | custom-call | flops 18350080 | bytes 4587520 | tf_op jit(solution)/shard_map/tracers/pallas_call | solution.py:433
  25.7 0.0 collective-permute-done.5
  25.7 1.6 %collective-permute-start.6 = (f32[8,128]{1,0:T(8,128)S(1)}, f32[8,128]{1,0:T(8,128)S(1)}, u32[]{:S(2)}, u32[]{:S(2)}) collective-permute-start(f32[8,128]{1,0:T(8,128)S(1)} %max.16), channel_id=1, source_target_pairs={{0,16},{4,20},{8,24},{12,28},{16,0},{20,4},{24,8},{28,12},{1,17},{... | collective-permute-start | bytes 12296 | tf_op jit(solution)/shard_map/ppermute | solution.py:731
  27.3 1.9 %tracers.5 = (f32[2,16,224,256]{3,2,1,0:T(8,128)S(1)}, f32[2,224,128]{2,1,0:T(8,128)S(1)}, bf16[4,2,224,128]{3,2,1,0:T(8,128)(2,1)S(1)}) custom-call(f32[2,16,224,256]{3,2,1,0:T(8,128)S(1)} %get-tuple-element.38.tracer, bf16[16,224,256]{2,1,0:T(8,128)(2,1)S(1)} %copy-done, ...), custom_call_target="tpu_custom_call", output_to_operand_aliasing={{0}: (8, {}), {1}: (9, {}), {2}: (10, {})} | custom-call | flops 18350080 | bytes 4587520 | tf_op jit(solution)/shard_map/tracers/pallas_call | solution.py:433
  29.2 0.2 collective-permute-done.6
  29.4 1.0 %collective-permute-start.7 = (f32[8,128]{1,0:T(8,128)S(1)}, f32[8,128]{1,0:T(8,128)S(1)}, u32[]{:S(2)}, u32[]{:S(2)}) collective-permute-start(f32[8,128]{1,0:T(8,128)S(1)} %max.17), channel_id=1, source_target_pairs={{0,1},{1,0},{2,3},{3,2},{4,5},{5,4},{6,7},{7,6},{8,9},{9,8},{10,11... | collective-permute-start | bytes 12296 | tf_op jit(solution)/shard_map/ppermute | solution.py:731
  30.3 1.9 %tracers.6 = (f32[2,16,224,256]{3,2,1,0:T(8,128)S(1)}, f32[2,224,128]{2,1,0:T(8,128)S(1)}, bf16[4,2,224,128]{3,2,1,0:T(8,128)(2,1)S(1)}) custom-call(f32[2,16,224,256]{3,2,1,0:T(8,128)S(1)} %get-tuple-element.38.tracer, bf16[16,224,256]{2,1,0:T(8,128)(2,1)S(1)} %copy-done, ...), custom_call_target="tpu_custom_call", output_to_operand_aliasing={{0}: (8, {}), {1}: (9, {}), {2}: (10, {})} | custom-call | flops 18350080 | bytes 4587520 | tf_op jit(solution)/shard_map/tracers/pallas_call | solution.py:433
  32.2 0.8 %collective-permute-done.7 = f32[8,128]{1,0:T(8,128)S(1)} collective-permute-done((f32[8,128]{1,0:T(8,128)S(1)}, f32[8,128]{1,0:T(8,128)S(1)}, u32[]{:S(2)}, u32[]{:S(2)}) %collective-permute-start.7) | collective-permute-done | bytes 4128 | tf_op jit(solution)/shard_map/ppermute | solution.py:731
  33.0 2.1 %collective-permute-start.8 = (f32[8,128]{1,0:T(8,128)S(1)}, f32[8,128]{1,0:T(8,128)S(1)}, u32[]{:S(2)}, u32[]{:S(2)}) collective-permute-start(f32[8,128]{1,0:T(8,128)S(1)} %max.18), channel_id=1, source_target_pairs={{0,2},{1,3},{2,0},{3,1},{4,6},{5,7},{6,4},{7,5},{8,10},{9,11},{10,... | collective-permute-start | bytes 12296 | tf_op jit(solution)/shard_map/ppermute | solution.py:731
  35.1 1.9 %tracers.7 = (f32[2,16,224,256]{3,2,1,0:T(8,128)S(1)}, f32[2,224,128]{2,1,0:T(8,128)S(1)}, bf16[4,2,224,128]{3,2,1,0:T(8,128)(2,1)S(1)}) custom-call(f32[2,16,224,256]{3,2,1,0:T(8,128)S(1)} %get-tuple-element.38.tracer, bf16[16,224,256]{2,1,0:T(8,128)(2,1)S(1)} %copy-done, ...), custom_call_target="tpu_custom_call", output_to_operand_aliasing={{0}: (8, {}), {1}: (9, {}), {2}: (10, {})} | custom-call | flops 18350080 | bytes 4587520 | tf_op jit(solution)/shard_map/tracers/pallas_call | solution.py:433
  37.0 0.5 %collective-permute-done.8 = f32[8,128]{1,0:T(8,128)S(1)} collective-permute-done((f32[8,128]{1,0:T(8,128)S(1)}, f32[8,128]{1,0:T(8,128)S(1)}, u32[]{:S(2)}, u32[]{:S(2)}) %collective-permute-start.8) | collective-permute-done | bytes 4128 | tf_op jit(solution)/shard_map/ppermute | solution.py:731
  37.5 6.8 %solve.1 = (f32[2,16,224,256]{3,2,1,0:T(8,128)}, f32[224,256]{1,0:T(8,128)}, f32[224,256]{1,0:T(8,128)}, f32[224,256]{1,0:T(8,128)}) custom-call(f32[2,16,224,256]{3,2,1,0:T(8,128)S(1)} %get-tuple-element.66.tracer_in, f32[8,128]{1,0:T(8,128)S(1)} %max.19.peak, f32[224,256]{1,0:T(8,128)S(1)} %get-tuple-element.39.depth, ...), custom_call_target="tpu_custom_call" | custom-call | flops 11468800 | bytes 1835008 | tf_op jit(solution)/shard_map/solve/pallas_call | solution.py:680
  (5 shorter events, 0.0 us)
Async XLA Ops:
  0.6 22.3 %copy-start.1 = (bf16[16,224,256]{2,1,0:T(8,128)(2,1)S(1)}, bf16[16,224,256]{2,1,0:T(8,128)(2,1)}, u32[]{:S(2)}) copy-start(bf16[16,224,256]{2,1,0:T(8,128)(2,1)} %merid.7) | copy-start | bytes 5505028
  0.6 22.3 %copy-start = (bf16[16,224,256]{2,1,0:T(8,128)(2,1)S(1)}, bf16[16,224,256]{2,1,0:T(8,128)(2,1)}, u32[]{:S(2)}) copy-start(bf16[16,224,256]{2,1,0:T(8,128)(2,1)} %zonal.7) | copy-start | bytes 5505028
  6.8 5.5 %collective-permute-start = (f32[72,256]{1,0:T(8,128)S(1)}, f32[72,256]{1,0:T(8,128)S(1)}, u32[]{:S(2)}, u32[]{:S(2)}) collective-permute-start(f32[72,256]{1,0:T(8,128)S(1)} %get-tuple-element.40), channel_id=1, source_target_pairs={{0,4},{4,8},{8,12},{12,16},{16,20},{20,24},{24,28},{28,0},{1,5},{5... | collective-permute-start | bytes 221192 | tf_op jit(solution)/shard_map/ppermute | solution.py:699
  7.3 4.9 %collective-permute-start.1 = (f32[72,256]{1,0:T(8,128)S(1)}, f32[72,256]{1,0:T(8,128)S(1)}, u32[]{:S(2)}, u32[]{:S(2)}) collective-permute-start(f32[72,256]{1,0:T(8,128)S(1)} %get-tuple-element.41), channel_id=1, source_target_pairs={{4,0},{8,4},{12,8},{16,12},{20,16},{24,20},{28,24},{0,28},{5,1},{9... | collective-permute-start | bytes 221192 | tf_op jit(solution)/shard_map/ppermute | solution.py:699
  12.4 7.3 %collective-permute-start.2 = (f32[120,128]{1,0:T(8,128)S(1)}, f32[120,128]{1,0:T(8,128)S(1)}, u32[]{:S(2)}, u32[]{:S(2)}) collective-permute-start(f32[120,128]{1,0:T(8,128)S(1)} %get-tuple-element.44), channel_id=1, source_target_pairs={{0,1},{1,2},{2,3},{3,0},{4,5},{5,6},{6,7},{7,4},{8,9},{9,10},{10,1... | collective-permute-start | bytes 184328 | tf_op jit(solution)/shard_map/ppermute | solution.py:699
  14.7 5.7 %collective-permute-start.3 = (f32[120,128]{1,0:T(8,128)S(1)}, f32[120,128]{1,0:T(8,128)S(1)}, u32[]{:S(2)}, u32[]{:S(2)}) collective-permute-start(f32[120,128]{1,0:T(8,128)S(1)} %get-tuple-element.45), channel_id=1, source_target_pairs={{1,0},{2,1},{3,2},{0,3},{5,4},{6,5},{7,6},{4,7},{9,8},{10,9},{11,1... | collective-permute-start | bytes 184328 | tf_op jit(solution)/shard_map/ppermute | solution.py:699
  20.8 1.2 %collective-permute-start.4 = (f32[8,128]{1,0:T(8,128)S(1)}, f32[8,128]{1,0:T(8,128)S(1)}, u32[]{:S(2)}, u32[]{:S(2)}) collective-permute-start(f32[8,128]{1,0:T(8,128)S(1)} %peak.1), channel_id=1, source_target_pairs={{0,4},{4,0},{8,12},{12,8},{16,20},{20,16},{24,28},{28,24},{1,5},{5... | collective-permute-start | bytes 12296 | tf_op jit(solution)/shard_map/ppermute | solution.py:731
  22.0 3.7 %collective-permute-start.5 = (f32[8,128]{1,0:T(8,128)S(1)}, f32[8,128]{1,0:T(8,128)S(1)}, u32[]{:S(2)}, u32[]{:S(2)}) collective-permute-start(f32[8,128]{1,0:T(8,128)S(1)} %max.15), channel_id=1, source_target_pairs={{0,8},{4,12},{8,0},{12,4},{16,24},{20,28},{24,16},{28,20},{1,9},{5... | collective-permute-start | bytes 12296 | tf_op jit(solution)/shard_map/ppermute | solution.py:731
  25.7 3.7 %collective-permute-start.6 = (f32[8,128]{1,0:T(8,128)S(1)}, f32[8,128]{1,0:T(8,128)S(1)}, u32[]{:S(2)}, u32[]{:S(2)}) collective-permute-start(f32[8,128]{1,0:T(8,128)S(1)} %max.16), channel_id=1, source_target_pairs={{0,16},{4,20},{8,24},{12,28},{16,0},{20,4},{24,8},{28,12},{1,17},{... | collective-permute-start | bytes 12296 | tf_op jit(solution)/shard_map/ppermute | solution.py:731
  29.4 3.6 %collective-permute-start.7 = (f32[8,128]{1,0:T(8,128)S(1)}, f32[8,128]{1,0:T(8,128)S(1)}, u32[]{:S(2)}, u32[]{:S(2)}) collective-permute-start(f32[8,128]{1,0:T(8,128)S(1)} %max.17), channel_id=1, source_target_pairs={{0,1},{1,0},{2,3},{3,2},{4,5},{5,4},{6,7},{7,6},{8,9},{9,8},{10,11... | collective-permute-start | bytes 12296 | tf_op jit(solution)/shard_map/ppermute | solution.py:731
  33.0 4.5 %collective-permute-start.8 = (f32[8,128]{1,0:T(8,128)S(1)}, f32[8,128]{1,0:T(8,128)S(1)}, u32[]{:S(2)}, u32[]{:S(2)}) collective-permute-start(f32[8,128]{1,0:T(8,128)S(1)} %max.18), channel_id=1, source_target_pairs={{0,2},{1,3},{2,0},{3,1},{4,6},{5,7},{6,4},{7,5},{8,10},{9,11},{10,... | collective-permute-start | bytes 12296 | tf_op jit(solution)/shard_map/ppermute | solution.py:731

commit v3 on v2

--- a/solution.py
+++ b/solution.py
@@ -43,7 +43,7 @@
 
 def column_kernel(
     tracer_hbm, land_hbm, levels_hbm, surf_hbm, flow_x_hbm, flow_y_hbm,
-    force, depth, to_south, to_north, to_previous, to_next, tracer, surf, flow_x, flow_y,
+    force, depth, to_south, to_north, to_twin, to_other, tracer, surf, flow_x, flow_y,
     land, levels, flat_sem, chunk_sem,
 ):
     count = tracer.shape[1]
@@ -135,7 +135,8 @@
         return carry
 
     lax.fori_loop(0, CHUNKS, chunk, 0)
-    for out, line, tile in ((to_previous, 0, 0), (to_next, rows - 1, rows - SUB)):
+
+    def edge_rows(out, line, tile):
         for h in range(sides):
             span = pl.ds(h * LANES, LANES)
             deep = depth[pl.ds(line, 1), span]
@@ -146,6 +147,22 @@
                     )
             for f, ref in enumerate((depth, surf, flow_x, flow_y, force)):
                 out[pl.ds(base + f * SUB, SUB), span] = ref[pl.ds(tile, SUB), span]
+
+    even = is_even("gx")
+
+    @pl.when(even)
+    def _():
+        edge_rows(to_twin, rows - 1, rows - SUB)
+        edge_rows(to_other, 0, 0)
+
+    @pl.when(jnp.logical_not(even))
+    def _():
+        edge_rows(to_twin, 0, 0)
+        edge_rows(to_other, rows - 1, rows - SUB)
+
+
+def is_even(axis):
+    return lax.rem(lax.axis_index(axis), 2) == 0
 
 
 IN_HBM = pl.BlockSpec(memory_space=pltpu.HBM)
@@ -182,10 +199,17 @@
     )
 
 
-def pack_kernel(south_in, north_in, west, east, south_out, north_out):
-    half = south_in.shape[0] - SUB
+def pack_kernel(to_south, to_north, from_twin, from_other, to_twin, to_other, west, east):
+    half = to_south.shape[0] - SUB
     sides = west.shape[1] // LANES
     lanes = lane_ids(SUB)
+    even_x, even_y = is_even("gx"), is_even("gy")
+    for r in range(0, west.shape[0], SUB):
+        for h in range(sides):
+            at = (pl.ds(r, SUB), pl.ds(h * LANES, LANES))
+            first, second = from_twin[at], from_other[at]
+            east[at] = jnp.where(even_x, first, second)
+            west[at] = jnp.where(even_x, second, first)
     strips = []
     for ref in (west, east):
         zero = jnp.zeros((SUB, LANES), F32)
@@ -194,24 +218,33 @@
             tuple(ref[pl.ds(BASE + f * SUB, SUB), span] for span in ends) for f in range(FIELDS)
         ]
         strips.append(strip_pair(zero, zero, lanes, values))
-    for index, (source, out) in enumerate(((south_in, south_out), (north_in, north_out))):
-        out[pl.ds(0, half), :] = source[pl.ds(0, half), :]
-        out[pl.ds(half, SUB), :] = jnp.where(
-            lanes < HALF, strips[0][index], pltpu.roll(strips[1][index], HALF, 1)
-        )
-
-
-def pack_pass(to_south, to_north, west, east):
-    shape = jax.ShapeDtypeStruct(to_south.shape, F32)
+    for r in range(0, half + SUB, SUB):
+        at = pl.ds(r, SUB)
+        if r < half:
+            low, high = to_south[at, :], to_north[at, :]
+        else:
+            low, high = (
+                jnp.where(lanes < HALF, before, pltpu.roll(after, HALF, 1))
+                for before, after in zip(*strips)
+            )
+        to_twin[at, :] = jnp.where(even_y, high, low)
+        to_other[at, :] = jnp.where(even_y, low, high)
+
+
+def pack_pass(to_south, to_north, from_twin, from_other):
+    strip = jax.ShapeDtypeStruct(to_south.shape, F32)
+    lines = jax.ShapeDtypeStruct(from_twin.shape, F32)
     return pl.pallas_call(
         pack_kernel,
-        out_shape=[shape, shape],
+        in_specs=[IN_VMEM] * 4,
+        out_specs=[IN_VMEM] * 4,
+        out_shape=[strip, strip, lines, lines],
         compiler_params=pltpu.CompilerParams(vmem_limit_bytes=VMEM_LIMIT),
         cost_estimate=pl.CostEstimate(
             flops=to_south.size, bytes_accessed=16 * to_south.size, transcendentals=0
         ),
         name="corners",
-    )(to_south, to_north, west, east)
+    )(to_south, to_north, from_twin, from_other)
 
 
 def message_rows(ref, rows, r):
@@ -273,12 +306,18 @@
     return [sides[h] + (nxt[h] + prv[h]) for h in range(ref.shape[0])]
 
 
-def peak_kernel(depth, west, east, south, north, peak, coded):
+def peak_kernel(depth, west, east, from_twin, from_other, peak, south, north, coded):
     rows, cols = depth.shape
     sides = cols // LANES
     lanes = lane_ids(SUB)
     open_south, open_north = latitude_ends()
     scale = 2.0 / (BASE // 2)
+    even = is_even("gy")
+    for r in range(0, south.shape[0], SUB):
+        at = pl.ds(r, SUB)
+        first, second = from_twin[at, :], from_other[at, :]
+        north[at, :] = jnp.where(even, first, second)
+        south[at, :] = jnp.where(even, second, first)
     extend(coded, BASE, 0, depth, west, east, south, north, open_south, open_north)
     for r in range(0, rows + 2 * SUB, SUB):
         for h in range(sides + 1):
@@ -300,55 +339,81 @@
     return wet, sums - CODE * wet
 
 
-def peak_pass(depth, west, east, south, north):
+def peak_pass(depth, west, east, from_twin, from_other):
     rows, cols = depth.shape
+    strip = jax.ShapeDtypeStruct(from_twin.shape, F32)
     ext = pltpu.VMEM((cols // LANES + 1, rows + 2 * SUB, LANES), F32)
     return pl.pallas_call(
         peak_kernel,
-        out_shape=jax.ShapeDtypeStruct((SUB, LANES), F32),
+        in_specs=[IN_VMEM] * 5,
+        out_specs=[IN_VMEM] * 3,
+        out_shape=[jax.ShapeDtypeStruct((SUB, LANES), F32), strip, strip],
         scratch_shapes=[ext],
         compiler_params=pltpu.CompilerParams(vmem_limit_bytes=VMEM_LIMIT),
         cost_estimate=pl.CostEstimate(
             flops=30 * depth.size, bytes_accessed=4 * depth.size, transcendentals=0
         ),
         name="peak",
+    )(depth, west, east, from_twin, from_other)
+
+
+def around_kernel(depth, west, east, south, north, edge_y, around, masked):
+    rows, cols = depth.shape
+    sides = cols // LANES
+    lanes = lane_ids(SUB)
+    spans = [pl.ds(h * LANES, LANES) for h in range(sides)]
+    open_south, open_north = latitude_ends()
+    for h in range(sides):
+        masked[h, pl.ds(0, SUB), :] = west[pl.ds(BASE, SUB), spans[h]]
+        masked[h, pl.ds(SUB, rows), :] = depth[:, spans[h]]
+        masked[h, pl.ds(SUB + rows, SUB), :] = east[pl.ds(BASE, SUB), spans[h]]
+    for big in range(0, rows, 2 * SUB):
+        shifted = []
+        for r in (big, big + SUB):
+            low, high = message_rows(south, rows, r), message_rows(north, rows, r)
+            edge_y[0, pl.ds(r, SUB), :] = jnp.where(open_south, low, 0.0)
+            edge_y[1, pl.ds(r, SUB), :] = jnp.where(
+                open_north, pltpu.roll(high, LANES - 2, 1), 0.0
+            )
+            tiles = [depth[pl.ds(r, SUB), span] for span in spans]
+            tiles.append(outer_tile(south, north, rows, r, 0, open_south, open_north, lanes))
+            shifted.append(ring_shift(tiles, lanes))
+        at = pl.ds(big, 2 * SUB)
+        for h in range(sides):
+            around[0, h, at, :] = masked[h, pl.ds(SUB + big + 1, 2 * SUB), :].astype(BF16)
+            around[1, h, at, :] = masked[h, pl.ds(SUB + big - 1, 2 * SUB), :].astype(BF16)
+            for n in range(2):
+                pair = jnp.concatenate([shifted[0][n][h], shifted[1][n][h]], 0)
+                around[2 + n, h, at, :] = pair.astype(BF16)
+
+
+def around_pass(depth, west, east, south, north):
+    rows, cols = depth.shape
+    sides = cols // LANES
+    return pl.pallas_call(
+        around_kernel,
+        in_specs=[IN_VMEM] * 5,
+        out_specs=[IN_VMEM] * 2,
+        out_shape=[
+            jax.ShapeDtypeStruct((2, rows, LANES), F32),
+            jax.ShapeDtypeStruct((4, sides, rows, LANES), BF16),
+        ],
+        scratch_shapes=[pltpu.VMEM((sides, rows + 2 * SUB, LANES), F32)],
+        compiler_params=pltpu.CompilerParams(vmem_limit_bytes=VMEM_LIMIT),
+        cost_estimate=pl.CostEstimate(
+            flops=30 * depth.size, bytes_accessed=16 * depth.size, transcendentals=0
+        ),
+        name="around",
     )(depth, west, east, south, north)
 
 
-def tracer_kernel(start, stop, tracer, zonal, merid, depth, west, east, south, north, *rest):
-    out, edge_y, around, masked = rest[-4:]
+def tracer_kernel(start, stop, tracer, zonal, merid, depth, west, east, edge_y, around, *rest):
+    out, masked = rest[-2:]
     rows, cols = depth.shape
     sides = cols // LANES
     count = BASE // 2
     lanes = lane_ids(SUB)
     spans = [pl.ds(h * LANES, LANES) for h in range(sides)]
-
-    if start == 0:
-        open_south, open_north = latitude_ends()
-        for h in range(sides):
-            masked[0, h, pl.ds(0, SUB), :] = west[pl.ds(BASE, SUB), spans[h]]
-            masked[0, h, pl.ds(SUB, rows), :] = depth[:, spans[h]]
-            masked[0, h, pl.ds(SUB + rows, SUB), :] = east[pl.ds(BASE, SUB), spans[h]]
-        for big in range(0, rows, 2 * SUB):
-            shifted = []
-            for r in (big, big + SUB):
-                low, high = message_rows(south, rows, r), message_rows(north, rows, r)
-                edge_y[0, pl.ds(r, SUB), :] = jnp.where(open_south, low, 0.0)
-                edge_y[1, pl.ds(r, SUB), :] = jnp.where(
-                    open_north, pltpu.roll(high, LANES - 2, 1), 0.0
-                )
-                tiles = [depth[pl.ds(r, SUB), span] for span in spans]
-                tiles.append(
-                    outer_tile(south, north, rows, r, 0, open_south, open_north, lanes)
-                )
-                shifted.append(ring_shift(tiles, lanes))
-            at = pl.ds(big, 2 * SUB)
-            for h in range(sides):
-                around[0, h, at, :] = masked[0, h, pl.ds(SUB + big + 1, 2 * SUB), :].astype(BF16)
-                around[1, h, at, :] = masked[0, h, pl.ds(SUB + big - 1, 2 * SUB), :].astype(BF16)
-                for n in range(2):
-                    pair = jnp.concatenate([shifted[0][n][h], shifted[1][n][h]], 0)
-                    around[2 + n, h, at, :] = pair.astype(BF16)
 
     def one_level(level, carry):
         mark = lax.convert_element_type(level, F32)
@@ -419,24 +484,18 @@
     lax.fori_loop(start, stop, one_level, 0)
 
 
-def tracer_pass(start, stop, tracer, zonal, merid, depth, west, east, south, north, before=()):
+def tracer_pass(start, stop, tracer, zonal, merid, depth, west, east, edge_y, around, before=()):
     two, count, rows, cols = tracer.shape
     sides = cols // LANES
-    operands = [tracer, zonal, merid, depth, west, east, south, north, *before]
-    first = len(operands) - len(before)
-    shapes = [
-        jax.ShapeDtypeStruct(tracer.shape, F32),
-        jax.ShapeDtypeStruct((2, rows, LANES), F32),
-        jax.ShapeDtypeStruct((4, sides, rows, LANES), BF16),
-    ]
+    operands = [tracer, zonal, merid, depth, west, east, edge_y, around, *before]
     part = stop - start
     return pl.pallas_call(
         functools.partial(tracer_kernel, start, stop),
         in_specs=[IN_VMEM] * len(operands),
-        out_specs=[IN_VMEM] * 3,
-        out_shape=shapes,
+        out_specs=IN_VMEM,
+        out_shape=jax.ShapeDtypeStruct(tracer.shape, F32),
         scratch_shapes=[pltpu.VMEM((2, sides, rows + 2 * SUB, LANES), F32)],
-        input_output_aliases={first + i: i for i in range(len(before))},
+        input_output_aliases={len(operands) - 1: 0} if before else {},
         compiler_params=pltpu.CompilerParams(vmem_limit_bytes=VMEM_LIMIT),
         cost_estimate=pl.CostEstimate(
             flops=40 * tracer.size * part // count,
@@ -448,13 +507,13 @@
 
 
 def group_of(tiles):
-    return max(n for n in range(1, 8) if tiles % n == 0)
+    return max(n for n in range(1, 17) if tiles % n == 0)
 
 
 def solve_kernel(
     tracer_in, peak, depth, surf, flow_x, flow_y, force, west, east, south, north,
-    tracer_hbm, surf_out, x_out, y_out,
-    old, deep, deep_n, deep_s, coded, flux, part, ease, pairs, now, then, total, sem,
+    tracer_hbm, surf_hbm, x_hbm, y_hbm,
+    surf_out, x_out, y_out, old, deep, deep_n, deep_s, coded, flux, part, ease, pairs, now, then, total, sem, out_sem,
 ):
     rows, cols = depth.shape
     sides = cols // LANES
@@ -463,8 +522,12 @@
     scale = 2.0 / BASE
     open_south, open_north = latitude_ends()
     beyond = ((lanes < WIDTH) & open_north) | ((lanes >= LANES - WIDTH) & open_south)
-    outward = pltpu.make_async_copy(tracer_in, tracer_hbm, sem)
-    outward.start()
+    outward = [
+        pltpu.make_async_copy(tracer_in.at[:, k], tracer_hbm.at[:, k], sem.at[k])
+        for k in range(BASE // 2)
+    ]
+    for copy in outward:
+        copy.start()
 
     lowest = 0.5 / peak[...]
     shrink = (1.0 - lowest) * (1.0 - lowest)
@@ -647,6 +710,17 @@
         over_tiles(apply)
         source, target = target, source
 
+    def results(i):
+        part_of = pl.ds(pl.multiple_of(i * size, SUB), size)
+        return [
+            pltpu.make_async_copy(
+                value.at[part_of, :], place.at[part_of, :], out_sem.at[n * CHUNKS + i]
+            )
+            for n, (value, place) in enumerate(
+                ((surf_out, surf_hbm), (x_out, x_hbm), (y_out, y_hbm))
+            )
+        ]
+
     def finish(i, carry):
         window = pl.ds(pl.multiple_of(i * size + SUB, SUB), size + 2 * SUB)
         for r in range(0, size, SUB):
@@ -665,10 +739,16 @@
                 y_out[at, span] = jnp.where(
                     wet, flow_y[at, span] - 0.25 * (nxt[h] - prv[h]), 0.0
                 )
+        for copy in results(i):
+            copy.start()
         return carry
 
     lax.fori_loop(0, CHUNKS, finish, 0)
-    outward.wait()
+    for i in range(CHUNKS):
+        for copy in results(i):
+            copy.wait()
+    for copy in outward:
+        copy.wait()
 
 
 def solve_pass(tracer, peak, depth, surf, flow_x, flow_y, force, west, east, south, north):
@@ -680,10 +760,12 @@
     return pl.pallas_call(
         solve_kernel,
         in_specs=[IN_VMEM] * 11,
-        out_specs=[IN_HBM] + [IN_VMEM] * 3,
+        out_specs=[IN_HBM] * 4,
         out_shape=[jax.ShapeDtypeStruct(tracer.shape, F32)] + [plain] * 3,
-        scratch_shapes=[ext] * 8
-        + [pltpu.VMEM((7, *shape), F32), three, three, ext, pltpu.SemaphoreType.DMA],
+        scratch_shapes=[pltpu.VMEM((rows, cols), F32)] * 3
+        + [ext] * 8
+        + [pltpu.VMEM((7, *shape), F32), three, three, ext]
+        + [pltpu.SemaphoreType.DMA((BASE // 2,)), pltpu.SemaphoreType.DMA((3 * CHUNKS,))],
         compiler_params=pltpu.CompilerParams(vmem_limit_bytes=VMEM_LIMIT),
         cost_estimate=pl.CostEstimate(
             flops=200 * depth.size, bytes_accessed=32 * depth.size, transcendentals=0
@@ -692,11 +774,26 @@
     )(tracer, peak, depth, surf, flow_x, flow_y, force, west, east, south, north)
 
 
-def both_ways(axis, to_next, to_previous):
-    size = lax.axis_size(axis)
-    up = [(i, (i + 1) % size) for i in range(size)]
-    down = [(j, i) for i, j in up]
-    return lax.ppermute(to_next, axis, up), lax.ppermute(to_previous, axis, down)
+def twin_pairs(axis):
+    return [(i, i ^ 1) for i in range(lax.axis_size(axis))]
+
+
+def other_x_pairs():
+    size = lax.axis_size("gx")
+    return [(i, (i + 1 if i % 2 else i - 1) % size) for i in range(size)]
+
+
+def other_y_pairs():
+    size_x, size_y = lax.axis_size("gx"), lax.axis_size("gy")
+    pairs = []
+    for i in range(size_x):
+        for j in range(size_y):
+            if j in (0, size_y - 1):
+                target = (i ^ 1, j)
+            else:
+                target = (i, j + 1 if j % 2 else j - 1)
+            pairs.append((i * size_y + j, target[0] * size_y + target[1]))
+    return pairs
 
 
 def spread_rounds(axis):
@@ -715,31 +812,39 @@
 ):
     count = tracer.shape[1]
     (
-        force, depth, to_south, to_north, to_previous, to_next,
+        force, depth, to_south, to_north, to_twin, to_other,
         tracer, surface_prev, transport_x, transport_y,
     ) = column_pass(tracer, land_mask, levels, surface_prev, transport_x, transport_y)
-    west, east = both_ways("gx", to_next, to_previous)
-    to_south, to_north = pack_pass(to_south, to_north, west, east)
-    south, north = both_ways("gy", to_north, to_south)
+    to_twin, to_other, zonal_flow, meridional_flow = lax.optimization_barrier(
+        (to_twin, to_other, zonal_flow, meridional_flow)
+    )
+    from_other = lax.ppermute(to_other, "gx", other_x_pairs())
+    from_twin = lax.ppermute(to_twin, "gx", twin_pairs("gx"))
+    to_twin, to_other, west, east = pack_pass(to_south, to_north, from_twin, from_other)
+    from_twin = lax.ppermute(to_twin, "gy", twin_pairs("gy"))
+    from_other = lax.ppermute(to_other, ("gx", "gy"), other_y_pairs())
+    peak, south, north = peak_pass(depth, west, east, from_twin, from_other)
     halo = (west, east, south, north)
-    peak = peak_pass(depth, *halo)
-    state = ()
     rounds = [r for axis in ("gx", "gy") for r in spread_rounds(axis)]
     cuts = [count * i // PARTS for i in range(PARTS + 1)]
     first = len(rounds) - PARTS
+    known, tracer_next = (), ()
     for turn, (axis, pairs) in enumerate(rounds):
         moved = lax.ppermute(peak, axis, pairs)
+        if turn == 0:
+            known = around_pass(depth, *halo)
+            moved, known = lax.optimization_barrier((moved, known))
         if turn >= first:
             part = turn - first
-            state = tracer_pass(
-                cuts[part], cuts[part + 1], tracer, zonal_flow, meridional_flow, depth, *halo,
-                before=state,
+            tracer_next = tracer_pass(
+                cuts[part], cuts[part + 1], tracer, zonal_flow, meridional_flow, depth,
+                west, east, *known, before=(tracer_next,) if part else (),
             )
         peak = jnp.maximum(peak, moved)
         if first <= turn < len(rounds) - 1:
-            peak, state = lax.optimization_barrier((peak, state))
+            peak, tracer_next = lax.optimization_barrier((peak, tracer_next))
     return solve_pass(
-        state[0], peak, depth, surface_prev, transport_x, transport_y, force, *halo
+        tracer_next, peak, depth, surface_prev, transport_x, transport_y, force, *halo
     )
 
 

time: 44.5 us -> 42.7 us (0.960)
  waiting for transfers between devices: 8.21 us -> 5.34 us
  starting transfers between devices: 13.4 us -> 15 us
    ppermute x5, starting transfers between devices: 5.53 us -> 8.98 us  [local(): moved = lax.ppermute(peak, axis, pairs)]
    ppermute x4, starting transfers between devices: 7.88 us -> 5.97 us  [the longest x1 3.55 us: local(): from_other = lax.ppermute(to_other, 'gx', other_x_pairs())]
    ppermute x5, waiting for transfers between devices: 2.66 us -> 0.94 us  [local(): moved = lax.ppermute(peak, axis, pairs)]
    ppermute x4, waiting for transfers between devices: 5.56 us -> 4.4 us  [the longest x1 2.36 us: local(): from_twin = lax.ppermute(to_twin, 'gy', twin_pairs('gy'))]
    pallas_call x2 -> x3, Pallas kernels: 0.59 us -> 1.47 us  [the longest x1 0.86 us: around_pass(): pl.pallas_call(around_kernel, in_specs=[IN_VMEM] * 5, out_specs=[IN_VMEM]...]
    pallas_call x1, Pallas kernels: 6.81 us -> 6.1 us  [solve_pass(): pl.pallas_call(solve_kernel, in_specs=[IN_VMEM] * 11, out_specs=[IN_HBM]...]
    pallas_call x4, Pallas kernels: 8.41 us -> 7.82 us  [tracer_pass(): pl.pallas_call(functools.partial(tracer_kernel, start, stop), in_specs=[I...]
  transfers between devices with their start and end apart: 9 -> 9, of which waited for: 7 -> 4; matrix products, arithmetic and copies ran while one was open for 0% -> 0% of each run, Pallas kernels for 19% -> 20%
where the time goes in v3:
time: 42.7 us; the launch traced here: 42.6 us
  Pallas kernels  21.5 us (50%)
  starting transfers between devices  15 us (35%)
  waiting for transfers between devices  5.34 us (13%)
  between operations  0.75 us (2%)
    ppermute x5, starting transfers between devices, local(): moved = lax.ppermute(peak, axis, pairs)  8.98 us
    pallas_call x4, Pallas kernels, tracer_pass(): pl.pallas_call(functools.partial(tracer_kernel, start, stop), in_specs=[I...  7.82 us
    pallas_call x1, Pallas kernels, column_pass(): pl.pallas_call(column_kernel, in_specs=[IN_HBM] * 6, out_specs=[IN_VMEM]...  6.13 us
    pallas_call x1, Pallas kernels, solve_pass(): pl.pallas_call(solve_kernel, in_specs=[IN_VMEM] * 11, out_specs=[IN_HBM]...  6.1 us
    ppermute x1, starting transfers between devices, local(): from_other = lax.ppermute(to_other, 'gx', other_x_pairs())  3.55 us
    ppermute x1, waiting for transfers between devices, local(): from_twin = lax.ppermute(to_twin, 'gy', twin_pairs('gy'))  2.36 us
    ppermute x1, waiting for transfers between devices, local(): from_other = lax.ppermute(to_other, 'gx', other_x_pairs())  2.03 us
    ppermute x1, starting transfers between devices, local(): from_twin = lax.ppermute(to_twin, 'gy', twin_pairs('gy'))  1.86 us
  transfers between devices with their start and end apart: 9, of which 4 were waited for; matrix products, arithmetic and copies ran while one was open for 0% of the time, Pallas kernels for 20%

profile of v3, /device:TPU:0, one launch (start us, length us, event | category | flops | bytes accessed | tf_op | source)
XLA Modules:
  0.0 42.6 jit_solution(4685230306393165992)
XLA Ops:
  0.6 0.0 copy-start.1
  0.6 0.0 copy-start
  0.7 6.1 %columns.1 = (f32[224,256]{1,0:T(8,128)S(1)}, f32[224,256]{1,0:T(8,128)S(1)}, f32[120,128]{1,0:T(8,128)S(1)}, f32[120,128]{1,0:T(8,128)S(1)}, f32[72,256]{1,0:T(...) custom-call(f32[2,16,224,256]{3,2,1,0:T(8,128)} %tracer_hbm.1, ...), custom_call_target="tpu_custom_call" | custom-call | flops 11010048 | bytes 7340032 | tf_op jit(solution)/shard_map/columns/pallas_call | solution.py:178
  6.8 0.6 %collective-permute-start = (f32[72,256]{1,0:T(8,128)S(1)}, f32[72,256]{1,0:T(8,128)S(1)}, u32[]{:S(2)}, u32[]{:S(2)}) collective-permute-start(f32[72,256]{1,0:T(8,128)S(1)} %get-tuple-element.44), channel_id=1, source_target_pairs={{0,4},{4,0},{8,12},{12,8},{16,20},{20,16},{24,28},{28,24},{1,5},{5... | collective-permute-start | bytes 221192 | tf_op jit(solution)/shard_map/ppermute | solution.py:822
  7.4 3.5 %collective-permute-start.1 = (f32[72,256]{1,0:T(8,128)S(1)}, f32[72,256]{1,0:T(8,128)S(1)}, u32[]{:S(2)}, u32[]{:S(2)}) collective-permute-start(f32[72,256]{1,0:T(8,128)S(1)} %get-tuple-element.45), channel_id=1, source_target_pairs={{0,28},{4,8},{8,4},{12,16},{16,12},{20,24},{24,20},{28,0},{1,29},{... | collective-permute-start | bytes 221192 | tf_op jit(solution)/shard_map/ppermute | solution.py:821
  10.9 0.0 collective-permute-done.from_twin
  10.9 2.0 %collective-permute-done.1.from_other = f32[72,256]{1,0:T(8,128)S(1)} collective-permute-done((f32[72,256]{1,0:T(8,128)S(1)}, f32[72,256]{1,0:T(8,128)S(1)}, u32[]{:S(2)}, u32[]{:S(2)}) %collective-permute-start.1) | collective-permute-done | bytes 73760 | tf_op jit(solution)/shard_map/ppermute | solution.py:821
  12.9 0.2 corners.1
  13.1 1.9 %collective-permute-start.2 = (f32[120,128]{1,0:T(8,128)S(1)}, f32[120,128]{1,0:T(8,128)S(1)}, u32[]{:S(2)}, u32[]{:S(2)}) collective-permute-start(f32[120,128]{1,0:T(8,128)S(1)} %get-tuple-element.48), channel_id=1, source_target_pairs={{0,1},{1,0},{2,3},{3,2},{4,5},{5,4},{6,7},{7,6},{8,9},{9,8},{10,11... | collective-permute-start | bytes 184328 | tf_op jit(solution)/shard_map/ppermute | solution.py:824
  15.0 0.0 collective-permute-start.3
  15.0 2.4 %collective-permute-done.2.from_twin = f32[120,128]{1,0:T(8,128)S(1)} collective-permute-done((f32[120,128]{1,0:T(8,128)S(1)}, f32[120,128]{1,0:T(8,128)S(1)}, u32[]{:S(2)}, u32[]{:S(2)}) %collective-permute-start.2) | collective-permute-done | bytes 61472 | tf_op jit(solution)/shard_map/ppermute | solution.py:824
  17.3 0.0 collective-permute-done.3.from_other
  17.3 0.5 %peak.1 = (f32[8,128]{1,0:T(8,128)S(1)}, f32[120,128]{1,0:T(8,128)S(1)}, f32[120,128]{1,0:T(8,128)S(1)}) custom-call(f32[224,256]{1,0:T(8,128)S(1)} %get-tuple-element.41.depth, f32[72,256]{1,0:T(8,128)S(1)} %get-tuple-element.46.west, f32[72,256]{1,0:T(8,128)S(1)} %get-tuple-element.47.east, f32[120,128]{1,0:T(8,128)S(1)} %collective-permute-done.2.from_twin, ...), custom_call_target="tpu_custom_call" | custom-call | flops 1720320 | bytes 229376 | tf_op jit(solution)/shard_map/peak/pallas_call | solution.py:346
  17.8 0.0 collective-permute-start.4
  17.8 0.9 %around.1 = (f32[2,224,128]{2,1,0:T(8,128)S(1)}, bf16[4,2,224,128]{3,2,1,0:T(8,128)(2,1)S(1)}) custom-call(f32[224,256]{1,0:T(8,128)S(1)} %get-tuple-element.41.depth, f32[72,256]{1,0:T(8,128)S(1)} %get-tuple-element.46.west, f32[72,256]{1,0:T(8,128)S(1)} %get-tuple-element.47.east, f32[120,128]{1,0:T(8,128)S(1)} %get-tuple-element.51.south, ...), custom_call_target="tpu_custom_call" | custom-call | flops 1720320 | bytes 917504 | tf_op jit(solution)/shard_map/around/pallas_call | solution.py:393
  18.6 0.3 collective-permute-done.4
  19.0 1.0 %collective-permute-start.5 = (f32[8,128]{1,0:T(8,128)S(1)}, f32[8,128]{1,0:T(8,128)S(1)}, u32[]{:S(2)}, u32[]{:S(2)}) collective-permute-start(f32[8,128]{1,0:T(8,128)S(1)} %max.15), channel_id=1, source_target_pairs={{0,8},{4,12},{8,0},{12,4},{16,24},{20,28},{24,16},{28,20},{1,9},{5... | collective-permute-start | bytes 12296 | tf_op jit(solution)/shard_map/ppermute | solution.py:833
  20.0 0.0 copy-done.1
  20.0 0.0 copy-done
  20.0 2.0 %tracers.4.rest_0_ = f32[2,16,224,256]{3,2,1,0:T(8,128)S(1)} custom-call(f32[2,16,224,256]{3,2,1,0:T(8,128)S(1)} %get-tuple-element.36.tracer, bf16[16,224,256]{2,1,0:T(8,128)(2,1)S(1)} %copy-done, bf16[16,224,256]{2,1,0:T(8,128)(2,1)S(1)} %copy-done.1, f32[224,256]{1,0:T(8,128)S(1)} %get-tuple-element.41.depth, f32[72,256]{1,0:T(8,128)S(1)} %get-tuple-element.46.west, ...), custom_call_target="tpu_custom_call" | custom-call | flops 18350080 | bytes 4587520 | tf_op jit(solution)/shard_map/tracers/pallas_call | solution.py:492
  21.9 0.6 %collective-permute-done.5 = f32[8,128]{1,0:T(8,128)S(1)} collective-permute-done((f32[8,128]{1,0:T(8,128)S(1)}, f32[8,128]{1,0:T(8,128)S(1)}, u32[]{:S(2)}, u32[]{:S(2)}) %collective-permute-start.5) | collective-permute-done | bytes 4128 | tf_op jit(solution)/shard_map/ppermute | solution.py:833
  22.6 1.7 %collective-permute-start.6 = (f32[8,128]{1,0:T(8,128)S(1)}, f32[8,128]{1,0:T(8,128)S(1)}, u32[]{:S(2)}, u32[]{:S(2)}) collective-permute-start(f32[8,128]{1,0:T(8,128)S(1)} %max.16), channel_id=1, source_target_pairs={{0,16},{4,20},{8,24},{12,28},{16,0},{20,4},{24,8},{28,12},{1,17},{... | collective-permute-start | bytes 12296 | tf_op jit(solution)/shard_map/ppermute | solution.py:833
  24.2 2.0 %tracers.5.rest_0_ = f32[2,16,224,256]{3,2,1,0:T(8,128)S(1)} custom-call(f32[2,16,224,256]{3,2,1,0:T(8,128)S(1)} %get-tuple-element.36.tracer, bf16[16,224,256]{2,1,0:T(8,128)(2,1)S(1)} %copy-done, bf16[16,224,256]{2,1,0:T(8,128)(2,1)S(1)} %copy-done.1, f32[224,256]{1,0:T(8,128)S(1)} %get-tuple-element.41.depth, ...), custom_call_target="tpu_custom_call", output_to_operand_aliasing={{}: (8, {})} | custom-call | flops 18350080 | bytes 4587520 | tf_op jit(solution)/shard_map/tracers/pallas_call | solution.py:492
  26.2 0.0 collective-permute-done.6
  26.2 3.2 %collective-permute-start.7 = (f32[8,128]{1,0:T(8,128)S(1)}, f32[8,128]{1,0:T(8,128)S(1)}, u32[]{:S(2)}, u32[]{:S(2)}) collective-permute-start(f32[8,128]{1,0:T(8,128)S(1)} %max.17), channel_id=1, source_target_pairs={{0,1},{1,0},{2,3},{3,2},{4,5},{5,4},{6,7},{7,6},{8,9},{9,8},{10,11... | collective-permute-start | bytes 12296 | tf_op jit(solution)/shard_map/ppermute | solution.py:833
  29.4 2.0 %tracers.6.rest_0_ = f32[2,16,224,256]{3,2,1,0:T(8,128)S(1)} custom-call(f32[2,16,224,256]{3,2,1,0:T(8,128)S(1)} %get-tuple-element.36.tracer, bf16[16,224,256]{2,1,0:T(8,128)(2,1)S(1)} %copy-done, bf16[16,224,256]{2,1,0:T(8,128)(2,1)S(1)} %copy-done.1, f32[224,256]{1,0:T(8,128)S(1)} %get-tuple-element.41.depth, ...), custom_call_target="tpu_custom_call", output_to_operand_aliasing={{}: (8, {})} | custom-call | flops 18350080 | bytes 4587520 | tf_op jit(solution)/shard_map/tracers/pallas_call | solution.py:492
  31.4 0.0 collective-permute-done.7
  31.4 3.1 %collective-permute-start.8 = (f32[8,128]{1,0:T(8,128)S(1)}, f32[8,128]{1,0:T(8,128)S(1)}, u32[]{:S(2)}, u32[]{:S(2)}) collective-permute-start(f32[8,128]{1,0:T(8,128)S(1)} %max.18), channel_id=1, source_target_pairs={{0,2},{1,3},{2,0},{3,1},{4,6},{5,7},{6,4},{7,5},{8,10},{9,11},{10,... | collective-permute-start | bytes 12296 | tf_op jit(solution)/shard_map/ppermute | solution.py:833
  34.5 2.0 %tracers.7.tracer_in = f32[2,16,224,256]{3,2,1,0:T(8,128)S(1)} custom-call(f32[2,16,224,256]{3,2,1,0:T(8,128)S(1)} %get-tuple-element.36.tracer, bf16[16,224,256]{2,1,0:T(8,128)(2,1)S(1)} %copy-done, bf16[16,224,256]{2,1,0:T(8,128)(2,1)S(1)} %copy-done.1, f32[224,256]{1,0:T(8,128)S(1)} %get-tuple-element.41.depth, ...), custom_call_target="tpu_custom_call", output_to_operand_aliasing={{}: (8, {})} | custom-call | flops 18350080 | bytes 4587520 | tf_op jit(solution)/shard_map/tracers/pallas_call | solution.py:492
  36.5 0.0 collective-permute-done.8
  36.5 6.1 %solve.1 = (f32[2,16,224,256]{3,2,1,0:T(8,128)}, f32[224,256]{1,0:T(8,128)}, f32[224,256]{1,0:T(8,128)}, f32[224,256]{1,0:T(8,128)}) custom-call(f32[2,16,224,256]{3,2,1,0:T(8,128)S(1)} %tracers.7.tracer_in, f32[8,128]{1,0:T(8,128)S(1)} %max.19.peak, f32[224,256]{1,0:T(8,128)S(1)} %get-tuple-element.41.depth, f32[224,256]{1,0:T(8,128)S(1)} %get-tuple-element.64.surf, ...), custom_call_target="tpu_custom_call" | custom-call | flops 11468800 | bytes 1835008 | tf_op jit(solution)/shard_map/solve/pallas_call | solution.py:760
  (5 shorter events, 0.0 us)
Async XLA Ops:
  0.6 19.3 %copy-start.1 = (bf16[16,224,256]{2,1,0:T(8,128)(2,1)S(1)}, bf16[16,224,256]{2,1,0:T(8,128)(2,1)}, u32[]{:S(2)}) copy-start(bf16[16,224,256]{2,1,0:T(8,128)(2,1)} %merid.3) | copy-start | bytes 5505028
  0.6 19.3 %copy-start = (bf16[16,224,256]{2,1,0:T(8,128)(2,1)S(1)}, bf16[16,224,256]{2,1,0:T(8,128)(2,1)}, u32[]{:S(2)}) copy-start(bf16[16,224,256]{2,1,0:T(8,128)(2,1)} %zonal.3) | copy-start | bytes 5505028
  6.8 4.1 %collective-permute-start = (f32[72,256]{1,0:T(8,128)S(1)}, f32[72,256]{1,0:T(8,128)S(1)}, u32[]{:S(2)}, u32[]{:S(2)}) collective-permute-start(f32[72,256]{1,0:T(8,128)S(1)} %get-tuple-element.44), channel_id=1, source_target_pairs={{0,4},{4,0},{8,12},{12,8},{16,20},{20,16},{24,28},{28,24},{1,5},{5... | collective-permute-start | bytes 221192 | tf_op jit(solution)/shard_map/ppermute | solution.py:822
  7.4 5.6 %collective-permute-start.1 = (f32[72,256]{1,0:T(8,128)S(1)}, f32[72,256]{1,0:T(8,128)S(1)}, u32[]{:S(2)}, u32[]{:S(2)}) collective-permute-start(f32[72,256]{1,0:T(8,128)S(1)} %get-tuple-element.45), channel_id=1, source_target_pairs={{0,28},{4,8},{8,4},{12,16},{16,12},{20,24},{24,20},{28,0},{1,29},{... | collective-permute-start | bytes 221192 | tf_op jit(solution)/shard_map/ppermute | solution.py:821
  13.1 4.2 %collective-permute-start.2 = (f32[120,128]{1,0:T(8,128)S(1)}, f32[120,128]{1,0:T(8,128)S(1)}, u32[]{:S(2)}, u32[]{:S(2)}) collective-permute-start(f32[120,128]{1,0:T(8,128)S(1)} %get-tuple-element.48), channel_id=1, source_target_pairs={{0,1},{1,0},{2,3},{3,2},{4,5},{5,4},{6,7},{7,6},{8,9},{9,8},{10,11... | collective-permute-start | bytes 184328 | tf_op jit(solution)/shard_map/ppermute | solution.py:824
  15.0 2.4 %collective-permute-start.3 = (f32[120,128]{1,0:T(8,128)S(1)}, f32[120,128]{1,0:T(8,128)S(1)}, u32[]{:S(2)}, u32[]{:S(2)}) collective-permute-start(f32[120,128]{1,0:T(8,128)S(1)} %get-tuple-element.49), channel_id=1, source_target_pairs={{0,4},{1,2},{2,1},{3,7},{4,0},{5,6},{6,5},{7,3},{8,12},{9,10},{10,... | collective-permute-start | bytes 184328 | tf_op jit(solution)/shard_map/ppermute | solution.py:825
  17.8 1.2 %collective-permute-start.4 = (f32[8,128]{1,0:T(8,128)S(1)}, f32[8,128]{1,0:T(8,128)S(1)}, u32[]{:S(2)}, u32[]{:S(2)}) collective-permute-start(f32[8,128]{1,0:T(8,128)S(1)} %get-tuple-element.50), channel_id=1, source_target_pairs={{0,4},{4,0},{8,12},{12,8},{16,20},{20,16},{24,28},{28,24},{1,5},{5... | collective-permute-start | bytes 12296 | tf_op jit(solution)/shard_map/ppermute | solution.py:833
  19.0 3.6 %collective-permute-start.5 = (f32[8,128]{1,0:T(8,128)S(1)}, f32[8,128]{1,0:T(8,128)S(1)}, u32[]{:S(2)}, u32[]{:S(2)}) collective-permute-start(f32[8,128]{1,0:T(8,128)S(1)} %max.15), channel_id=1, source_target_pairs={{0,8},{4,12},{8,0},{12,4},{16,24},{20,28},{24,16},{28,20},{1,9},{5... | collective-permute-start | bytes 12296 | tf_op jit(solution)/shard_map/ppermute | solution.py:833
  22.6 3.6 %collective-permute-start.6 = (f32[8,128]{1,0:T(8,128)S(1)}, f32[8,128]{1,0:T(8,128)S(1)}, u32[]{:S(2)}, u32[]{:S(2)}) collective-permute-start(f32[8,128]{1,0:T(8,128)S(1)} %max.16), channel_id=1, source_target_pairs={{0,16},{4,20},{8,24},{12,28},{16,0},{20,4},{24,8},{28,12},{1,17},{... | collective-permute-start | bytes 12296 | tf_op jit(solution)/shard_map/ppermute | solution.py:833
  26.2 5.2 %collective-permute-start.7 = (f32[8,128]{1,0:T(8,128)S(1)}, f32[8,128]{1,0:T(8,128)S(1)}, u32[]{:S(2)}, u32[]{:S(2)}) collective-permute-start(f32[8,128]{1,0:T(8,128)S(1)} %max.17), channel_id=1, source_target_pairs={{0,1},{1,0},{2,3},{3,2},{4,5},{5,4},{6,7},{7,6},{8,9},{9,8},{10,11... | collective-permute-start | bytes 12296 | tf_op jit(solution)/shard_map/ppermute | solution.py:833
  31.4 5.1 %collective-permute-start.8 = (f32[8,128]{1,0:T(8,128)S(1)}, f32[8,128]{1,0:T(8,128)S(1)}, u32[]{:S(2)}, u32[]{:S(2)}) collective-permute-start(f32[8,128]{1,0:T(8,128)S(1)} %max.18), channel_id=1, source_target_pairs={{0,2},{1,3},{2,0},{3,1},{4,6},{5,7},{6,4},{7,5},{8,10},{9,11},{10,... | collective-permute-start | bytes 12296 | tf_op jit(solution)/shard_map/ppermute | solution.py:833

commit v4 on v3

--- a/solution.py
+++ b/solution.py
@@ -357,11 +357,17 @@
     )(depth, west, east, from_twin, from_other)
 
 
-def around_kernel(depth, west, east, south, north, edge_y, around, masked):
+def around_kernel(
+    part, depth, west, east, south, north, zonal_hbm, merid_hbm,
+    edge_y, around, zonal, merid, masked, sem,
+):
     rows, cols = depth.shape
     sides = cols // LANES
     lanes = lane_ids(SUB)
     spans = [pl.ds(h * LANES, LANES) for h in range(sides)]
+    flows = flow_copies(part, zonal_hbm, merid_hbm, zonal, merid, sem)
+    for copy in flows:
+        copy.start()
     open_south, open_north = latitude_ends()
     for h in range(sides):
         masked[h, pl.ds(0, SUB), :] = west[pl.ds(BASE, SUB), spans[h]]
@@ -385,30 +391,68 @@
             for n in range(2):
                 pair = jnp.concatenate([shifted[0][n][h], shifted[1][n][h]], 0)
                 around[2 + n, h, at, :] = pair.astype(BF16)
-
-
-def around_pass(depth, west, east, south, north):
+    for copy in flows:
+        copy.wait()
+
+
+def flow_copies(part, zonal_hbm, merid_hbm, zonal, merid, sem):
+    levels = pl.ds(part[0], part[1] - part[0])
+    return [
+        pltpu.make_async_copy(source.at[levels], target, sem.at[i])
+        for i, (source, target) in enumerate(((zonal_hbm, zonal), (merid_hbm, merid)))
+    ]
+
+
+def in_hbm(*values):
+    return [pltpu.with_memory_space_constraint(value, pltpu.HBM) for value in values]
+
+
+def around_pass(part, depth, west, east, south, north, zonal, merid):
     rows, cols = depth.shape
     sides = cols // LANES
     return pl.pallas_call(
-        around_kernel,
-        in_specs=[IN_VMEM] * 5,
-        out_specs=[IN_VMEM] * 2,
+        functools.partial(around_kernel, part),
+        in_specs=[IN_VMEM] * 5 + [IN_HBM] * 2,
+        out_specs=[IN_VMEM] * 4,
         out_shape=[
             jax.ShapeDtypeStruct((2, rows, LANES), F32),
             jax.ShapeDtypeStruct((4, sides, rows, LANES), BF16),
+        ]
+        + [jax.ShapeDtypeStruct((part[1] - part[0], rows, cols), BF16)] * 2,
+        scratch_shapes=[
+            pltpu.VMEM((sides, rows + 2 * SUB, LANES), F32),
+            pltpu.SemaphoreType.DMA((2,)),
         ],
-        scratch_shapes=[pltpu.VMEM((sides, rows + 2 * SUB, LANES), F32)],
         compiler_params=pltpu.CompilerParams(vmem_limit_bytes=VMEM_LIMIT),
         cost_estimate=pl.CostEstimate(
             flops=30 * depth.size, bytes_accessed=16 * depth.size, transcendentals=0
         ),
         name="around",
-    )(depth, west, east, south, north)
-
-
-def tracer_kernel(start, stop, tracer, zonal, merid, depth, west, east, edge_y, around, *rest):
-    out, masked = rest[-2:]
+    )(depth, west, east, south, north, *in_hbm(zonal, merid))
+
+
+def tracer_kernel(parts, index, tracer, zonal, merid, depth, west, east, edge_y, around, *rest):
+    start, stop = parts[index]
+    rest = list(rest)
+    later = index + 1 < len(parts)
+    flows_hbm = [rest.pop(0), rest.pop(0)] if later else []
+    earlier = rest.pop(0) if index else None
+    if index > 1:
+        rest.pop(0)
+    out = rest.pop(0)
+    flows = [rest.pop(0), rest.pop(0)] if later else []
+    placed = rest.pop(0) if index else None
+    masked, sem = rest
+    copies = []
+    if later:
+        copies += flow_copies(parts[index + 1], *flows_hbm, *flows, sem)
+    if index:
+        first, last = parts[index - 1]
+        for c in range(2):
+            target = placed.at[c, pl.ds(first, last - first)]
+            copies.append(pltpu.make_async_copy(earlier.at[c], target, sem.at[2 + c]))
+    for copy in copies:
+        copy.start()
     rows, cols = depth.shape
     sides = cols // LANES
     count = BASE // 2
@@ -450,8 +494,8 @@
                 pairs.append(
                     (
                         1.0 - 0.2 * near.astype(F32),
-                        (zonal[level, wide, spans[h]] * quarter).astype(F32),
-                        (merid[level, wide, spans[h]] * quarter).astype(F32),
+                        (zonal[level - start, wide, spans[h]] * quarter).astype(F32),
+                        (merid[level - start, wide, spans[h]] * quarter).astype(F32),
                     )
                 )
             for sub in range(2):
@@ -476,26 +520,51 @@
                         value = own * tiles[h] + to_n * nxt + to_s * prv
                         value = value + to_e * masked[c, h, pl.ds(SUB + r + 1, SUB), :]
                         value = value + to_w * masked[c, h, pl.ds(SUB + r - 1, SUB), :]
-                        out[c, level, at, spans[h]] = jnp.where(
+                        out[c, level - start, at, spans[h]] = jnp.where(
                             here, value, tracer[c, level, at, spans[h]]
                         )
         return carry
 
     lax.fori_loop(start, stop, one_level, 0)
-
-
-def tracer_pass(start, stop, tracer, zonal, merid, depth, west, east, edge_y, around, before=()):
+    for copy in copies:
+        copy.wait()
+
+
+def tracer_pass(parts, index, tracer, flows, depth, west, east, known, flows_hbm, earlier, placed):
     two, count, rows, cols = tracer.shape
     sides = cols // LANES
-    operands = [tracer, zonal, merid, depth, west, east, edge_y, around, *before]
-    part = stop - start
-    return pl.pallas_call(
-        functools.partial(tracer_kernel, start, stop),
-        in_specs=[IN_VMEM] * len(operands),
-        out_specs=IN_VMEM,
-        out_shape=jax.ShapeDtypeStruct(tracer.shape, F32),
-        scratch_shapes=[pltpu.VMEM((2, sides, rows + 2 * SUB, LANES), F32)],
-        input_output_aliases={len(operands) - 1: 0} if before else {},
+    part = parts[index][1] - parts[index][0]
+    later = index + 1 < len(parts)
+    operands = [tracer, *flows, depth, west, east, *known]
+    specs = [IN_VMEM] * len(operands)
+    shapes = [jax.ShapeDtypeStruct((two, part, rows, cols), F32)]
+    outs = [IN_VMEM]
+    aliases = {}
+    if later:
+        after = parts[index + 1][1] - parts[index + 1][0]
+        operands += in_hbm(*flows_hbm)
+        specs += [IN_HBM] * 2
+        shapes += [jax.ShapeDtypeStruct((after, rows, cols), BF16)] * 2
+        outs += [IN_VMEM] * 2
+    if index:
+        operands.append(earlier)
+        specs.append(IN_VMEM)
+        if index > 1:
+            aliases = {len(operands): len(shapes)}
+            operands.append(placed)
+            specs.append(IN_HBM)
+        shapes.append(jax.ShapeDtypeStruct(tracer.shape, F32))
+        outs.append(IN_HBM)
+    results = pl.pallas_call(
+        functools.partial(tracer_kernel, parts, index),
+        in_specs=specs,
+        out_specs=outs,
+        out_shape=shapes,
+        scratch_shapes=[
+            pltpu.VMEM((2, sides, rows + 2 * SUB, LANES), F32),
+            pltpu.SemaphoreType.DMA((4,)),
+        ],
+        input_output_aliases=aliases,
         compiler_params=pltpu.CompilerParams(vmem_limit_bytes=VMEM_LIMIT),
         cost_estimate=pl.CostEstimate(
             flops=40 * tracer.size * part // count,
@@ -504,6 +573,10 @@
         ),
         name="tracers",
     )(*operands)
+    results = list(results)
+    made = results.pop(0)
+    flows = (results.pop(0), results.pop(0)) if later else ()
+    return made, flows, results.pop(0) if index else None
 
 
 def group_of(tiles):
@@ -511,7 +584,7 @@
 
 
 def solve_kernel(
-    tracer_in, peak, depth, surf, flow_x, flow_y, force, west, east, south, north,
+    last_part, tracer_in, _, peak, depth, surf, flow_x, flow_y, force, west, east, south, north,
     tracer_hbm, surf_hbm, x_hbm, y_hbm,
     surf_out, x_out, y_out, old, deep, deep_n, deep_s, coded, flux, part, ease, pairs, now, then, total, sem, out_sem,
 ):
@@ -522,9 +595,10 @@
     scale = 2.0 / BASE
     open_south, open_north = latitude_ends()
     beyond = ((lanes < WIDTH) & open_north) | ((lanes >= LANES - WIDTH) & open_south)
+    part_at = pl.ds(last_part[0], last_part[1] - last_part[0])
     outward = [
-        pltpu.make_async_copy(tracer_in.at[:, k], tracer_hbm.at[:, k], sem.at[k])
-        for k in range(BASE // 2)
+        pltpu.make_async_copy(tracer_in.at[c], tracer_hbm.at[c, part_at], sem.at[c])
+        for c in range(2)
     ]
     for copy in outward:
         copy.start()
@@ -751,27 +825,28 @@
         copy.wait()
 
 
-def solve_pass(tracer, peak, depth, surf, flow_x, flow_y, force, west, east, south, north):
+def solve_pass(last_part, made, placed, peak, depth, surf, flow_x, flow_y, force, west, east, south, north):
     rows, cols = depth.shape
     shape = (cols // LANES + 1, rows + 4 * SUB, LANES)
     ext = pltpu.VMEM(shape, F32)
     three = pltpu.VMEM((3, *shape), F32)
     plain = jax.ShapeDtypeStruct((rows, cols), F32)
     return pl.pallas_call(
-        solve_kernel,
-        in_specs=[IN_VMEM] * 11,
+        functools.partial(solve_kernel, last_part),
+        in_specs=[IN_VMEM, IN_HBM] + [IN_VMEM] * 10,
         out_specs=[IN_HBM] * 4,
-        out_shape=[jax.ShapeDtypeStruct(tracer.shape, F32)] + [plain] * 3,
+        out_shape=[jax.ShapeDtypeStruct(placed.shape, F32)] + [plain] * 3,
+        input_output_aliases={1: 0},
         scratch_shapes=[pltpu.VMEM((rows, cols), F32)] * 3
         + [ext] * 8
         + [pltpu.VMEM((7, *shape), F32), three, three, ext]
-        + [pltpu.SemaphoreType.DMA((BASE // 2,)), pltpu.SemaphoreType.DMA((3 * CHUNKS,))],
+        + [pltpu.SemaphoreType.DMA((2,)), pltpu.SemaphoreType.DMA((3 * CHUNKS,))],
         compiler_params=pltpu.CompilerParams(vmem_limit_bytes=VMEM_LIMIT),
         cost_estimate=pl.CostEstimate(
             flops=200 * depth.size, bytes_accessed=32 * depth.size, transcendentals=0
         ),
         name="solve",
-    )(tracer, peak, depth, surf, flow_x, flow_y, force, west, east, south, north)
+    )(made, placed, peak, depth, surf, flow_x, flow_y, force, west, east, south, north)
 
 
 def twin_pairs(axis):
@@ -815,9 +890,6 @@
         force, depth, to_south, to_north, to_twin, to_other,
         tracer, surface_prev, transport_x, transport_y,
     ) = column_pass(tracer, land_mask, levels, surface_prev, transport_x, transport_y)
-    to_twin, to_other, zonal_flow, meridional_flow = lax.optimization_barrier(
-        (to_twin, to_other, zonal_flow, meridional_flow)
-    )
     from_other = lax.ppermute(to_other, "gx", other_x_pairs())
     from_twin = lax.ppermute(to_twin, "gx", twin_pairs("gx"))
     to_twin, to_other, west, east = pack_pass(to_south, to_north, from_twin, from_other)
@@ -827,24 +899,24 @@
     halo = (west, east, south, north)
     rounds = [r for axis in ("gx", "gy") for r in spread_rounds(axis)]
     cuts = [count * i // PARTS for i in range(PARTS + 1)]
+    parts = tuple(zip(cuts, cuts[1:]))
+    flows_hbm = (zonal_flow, meridional_flow)
     first = len(rounds) - PARTS
-    known, tracer_next = (), ()
+    known, flows, made, placed = (), (), None, None
     for turn, (axis, pairs) in enumerate(rounds):
         moved = lax.ppermute(peak, axis, pairs)
         if turn == 0:
-            known = around_pass(depth, *halo)
-            moved, known = lax.optimization_barrier((moved, known))
+            *known, zonal, merid = around_pass(parts[0], depth, *halo, *flows_hbm)
+            moved, known, flows = lax.optimization_barrier((moved, known, (zonal, merid)))
         if turn >= first:
-            part = turn - first
-            tracer_next = tracer_pass(
-                cuts[part], cuts[part + 1], tracer, zonal_flow, meridional_flow, depth,
-                west, east, *known, before=(tracer_next,) if part else (),
+            made, flows, placed = tracer_pass(
+                parts, turn - first, tracer, flows, depth, west, east, known, flows_hbm, made, placed
             )
         peak = jnp.maximum(peak, moved)
         if first <= turn < len(rounds) - 1:
-            peak, tracer_next = lax.optimization_barrier((peak, tracer_next))
+            peak, made, flows = lax.optimization_barrier((peak, made, flows))
     return solve_pass(
-        tracer_next, peak, depth, surface_prev, transport_x, transport_y, force, *halo
+        parts[-1], made, placed, peak, depth, surface_prev, transport_x, transport_y, force, *halo
     )
 
 

time: 42.7 us -> 43.3 us (1.014)
  Pallas kernels: 21.5 us -> 22.2 us
  waiting for transfers between devices: 5.34 us -> 4.83 us
    pallas_call x6, Pallas kernels: 14.8 us -> 15.6 us  [the longest x4 7.72 us: tracer_pass(): pl.pallas_call(functools.partial(tracer_kernel, parts, index), in_specs=s...]
    ppermute x5, waiting for transfers between devices: 0.94 us -> 0.43 us  [local(): moved = lax.ppermute(peak, axis, pairs)]
  transfers between devices with their start and end apart: 9 -> 9, of which waited for: 4 -> 3; matrix products, arithmetic and copies ran while one was open for 0% -> 0% of each run, Pallas kernels for 20% -> 22%
where the time goes in v4:
time: 43.3 us; the launch traced here: 43.1 us
  Pallas kernels  22.2 us (51%)
  starting transfers between devices  15.3 us (35%)
  waiting for transfers between devices  4.83 us (11%)
  between operations  0.75 us (2%)
    ppermute x5, starting transfers between devices, local(): moved = lax.ppermute(peak, axis, pairs)  9.3 us
    pallas_call x4, Pallas kernels, tracer_pass(): pl.pallas_call(functools.partial(tracer_kernel, parts, index), in_specs=s...  7.72 us
    pallas_call x1, Pallas kernels, column_pass(): pl.pallas_call(column_kernel, in_specs=[IN_HBM] * 6, out_specs=[IN_VMEM]...  6 us
    pallas_call x1, Pallas kernels, solve_pass(): pl.pallas_call(functools.partial(solve_kernel, last_part), in_specs=[IN_V...  5.95 us
    ppermute x1, starting transfers between devices, local(): from_other = lax.ppermute(to_other, 'gx', other_x_pairs())  3.55 us
    ppermute x1, waiting for transfers between devices, local(): from_twin = lax.ppermute(to_twin, 'gy', twin_pairs('gy'))  2.36 us
    ppermute x1, waiting for transfers between devices, local(): from_other = lax.ppermute(to_other, 'gx', other_x_pairs())  2.03 us
    pallas_call x1, Pallas kernels, around_pass(): pl.pallas_call(functools.partial(around_kernel, part), in_specs=[IN_VMEM]...  1.95 us
  transfers between devices with their start and end apart: 9, of which 3 were waited for; matrix products, arithmetic and copies ran while one was open for 0% of the time, Pallas kernels for 22%

profile of v4, /device:TPU:0, one launch (start us, length us, event | category | flops | bytes accessed | tf_op | source)
XLA Modules:
  0.0 43.1 jit_solution(17993498506512454653)
XLA Ops:
  0.6 6.0 %columns.1 = (f32[224,256]{1,0:T(8,128)S(1)}, f32[224,256]{1,0:T(8,128)S(1)}, f32[120,128]{1,0:T(8,128)S(1)}, f32[120,128]{1,0:T(8,128)S(1)}, f32[72,256]{1,0:T(...) custom-call(f32[2,16,224,256]{3,2,1,0:T(8,128)} %tracer_hbm.1, ...), custom_call_target="tpu_custom_call" | custom-call | flops 11010048 | bytes 7340032 | tf_op jit(solution)/shard_map/columns/pallas_call | solution.py:178
  6.6 0.6 %collective-permute-start = (f32[72,256]{1,0:T(8,128)S(1)}, f32[72,256]{1,0:T(8,128)S(1)}, u32[]{:S(2)}, u32[]{:S(2)}) collective-permute-start(f32[72,256]{1,0:T(8,128)S(1)} %get-tuple-element.59), channel_id=1, source_target_pairs={{0,4},{4,0},{8,12},{12,8},{16,20},{20,16},{24,28},{28,24},{1,5},{5... | collective-permute-start | bytes 221192 | tf_op jit(solution)/shard_map/ppermute | solution.py:894
  7.2 3.5 %collective-permute-start.1 = (f32[72,256]{1,0:T(8,128)S(1)}, f32[72,256]{1,0:T(8,128)S(1)}, u32[]{:S(2)}, u32[]{:S(2)}) collective-permute-start(f32[72,256]{1,0:T(8,128)S(1)} %get-tuple-element.60), channel_id=1, source_target_pairs={{0,28},{4,8},{8,4},{12,16},{16,12},{20,24},{24,20},{28,0},{1,29},{... | collective-permute-start | bytes 221192 | tf_op jit(solution)/shard_map/ppermute | solution.py:893
  10.7 0.0 collective-permute-done.from_twin
  10.7 2.0 %collective-permute-done.1.from_other = f32[72,256]{1,0:T(8,128)S(1)} collective-permute-done((f32[72,256]{1,0:T(8,128)S(1)}, f32[72,256]{1,0:T(8,128)S(1)}, u32[]{:S(2)}, u32[]{:S(2)}) %collective-permute-start.1) | collective-permute-done | bytes 73760 | tf_op jit(solution)/shard_map/ppermute | solution.py:893
  12.8 0.2 corners.1
  12.9 1.9 %collective-permute-start.2 = (f32[120,128]{1,0:T(8,128)S(1)}, f32[120,128]{1,0:T(8,128)S(1)}, u32[]{:S(2)}, u32[]{:S(2)}) collective-permute-start(f32[120,128]{1,0:T(8,128)S(1)} %get-tuple-element.63), channel_id=1, source_target_pairs={{0,1},{1,0},{2,3},{3,2},{4,5},{5,4},{6,7},{7,6},{8,9},{9,8},{10,11... | collective-permute-start | bytes 184328 | tf_op jit(solution)/shard_map/ppermute | solution.py:896
  14.8 0.0 collective-permute-start.3
  14.8 2.4 %collective-permute-done.2.from_twin = f32[120,128]{1,0:T(8,128)S(1)} collective-permute-done((f32[120,128]{1,0:T(8,128)S(1)}, f32[120,128]{1,0:T(8,128)S(1)}, u32[]{:S(2)}, u32[]{:S(2)}) %collective-permute-start.2) | collective-permute-done | bytes 61472 | tf_op jit(solution)/shard_map/ppermute | solution.py:896
  17.2 0.0 collective-permute-done.3.from_other
  17.2 0.4 %peak.1 = (f32[8,128]{1,0:T(8,128)S(1)}, f32[120,128]{1,0:T(8,128)S(1)}, f32[120,128]{1,0:T(8,128)S(1)}) custom-call(f32[224,256]{1,0:T(8,128)S(1)} %get-tuple-element.56.depth, f32[72,256]{1,0:T(8,128)S(1)} %get-tuple-element.61.west, f32[72,256]{1,0:T(8,128)S(1)} %get-tuple-element.62.east, f32[120,128]{1,0:T(8,128)S(1)} %collective-permute-done.2.from_twin, ...), custom_call_target="tpu_custom_call" | custom-call | flops 1720320 | bytes 229376 | tf_op jit(solution)/shard_map/peak/pallas_call | solution.py:346
  17.6 0.0 collective-permute-start.4
  17.6 2.0 %around.1 = (f32[2,224,128]{2,1,0:T(8,128)S(1)}, bf16[4,2,224,128]{3,2,1,0:T(8,128)(2,1)S(1)}, bf16[4,224,256]{2,1,0:T(8,128)(2,1)S(1)}, bf16[4,224,256]{2,1,0:T(8,128)(2,1)S(1)}) custom-call(f32[224,256]{1,0:T(8,128)S(1)} %get-tuple-element.56.depth, f32[72,256]{1,0:T(8,128)S(1)} %get-tuple-element.61.west, f32[72,256]{1,0:T(8,128)S(1)} %get-tuple-element.62.east, ...), custom_call_target="tpu_custom_call" | custom-call | flops 1720320 | bytes 917504 | tf_op jit(solution)/shard_map/around/pallas_call | solution.py:413
  19.6 0.0 collective-permute-done.4
  19.6 1.3 %collective-permute-start.5 = (f32[8,128]{1,0:T(8,128)S(1)}, f32[8,128]{1,0:T(8,128)S(1)}, u32[]{:S(2)}, u32[]{:S(2)}) collective-permute-start(f32[8,128]{1,0:T(8,128)S(1)} %max.15), channel_id=1, source_target_pairs={{0,8},{4,12},{8,0},{12,4},{16,24},{20,28},{24,16},{28,20},{1,9},{5... | collective-permute-start | bytes 12296 | tf_op jit(solution)/shard_map/ppermute | solution.py:907
  20.9 2.0 %tracers.4 = (f32[2,4,224,256]{3,2,1,0:T(8,128)S(1)}, bf16[4,224,256]{2,1,0:T(8,128)(2,1)S(1)}, bf16[4,224,256]{2,1,0:T(8,128)(2,1)S(1)}) custom-call(f32[2,16,224,256]{3,2,1,0:T(8,128)S(1)} %get-tuple-element.55.tracer, bf16[4,224,256]{2,1,0:T(8,128)(2,1)S(1)} %get-tuple-element.73.zonal, bf16[4,224,256]{2,1,0:T(8,128)(2,1)S(1)} %get-tuple-element.74.merid, ...), custom_call_target="tpu_custom_call" | custom-call | flops 18350080 | bytes 4587520 | tf_op jit(solution)/shard_map/tracers/pallas_call | solution.py:558
  22.9 0.4 collective-permute-done.5
  23.3 1.7 %collective-permute-start.6 = (f32[8,128]{1,0:T(8,128)S(1)}, f32[8,128]{1,0:T(8,128)S(1)}, u32[]{:S(2)}, u32[]{:S(2)}) collective-permute-start(f32[8,128]{1,0:T(8,128)S(1)} %max.16), channel_id=1, source_target_pairs={{0,16},{4,20},{8,24},{12,28},{16,0},{20,4},{24,8},{28,12},{1,17},{... | collective-permute-start | bytes 12296 | tf_op jit(solution)/shard_map/ppermute | solution.py:907
  25.0 1.9 %tracers.5 = (f32[2,4,224,256]{3,2,1,0:T(8,128)S(1)}, bf16[4,224,256]{2,1,0:T(8,128)(2,1)S(1)}, bf16[4,224,256]{2,1,0:T(8,128)(2,1)S(1)}, f32[2,16,224,256]{3,2,1,0:T(8,128)}) custom-call(f32[2,16,224,256]{3,2,1,0:T(8,128)S(1)} %get-tuple-element.55.tracer, bf16[4,224,256]{2,1,0:T(8,128)(2,1)S(1)} %get-tuple-element.81.zonal, ...), custom_call_target="tpu_custom_call" | custom-call | flops 18350080 | bytes 4587520 | tf_op jit(solution)/shard_map/tracers/pallas_call | solution.py:558
  26.9 0.0 collective-permute-done.6
  26.9 3.2 %collective-permute-start.7 = (f32[8,128]{1,0:T(8,128)S(1)}, f32[8,128]{1,0:T(8,128)S(1)}, u32[]{:S(2)}, u32[]{:S(2)}) collective-permute-start(f32[8,128]{1,0:T(8,128)S(1)} %max.17), channel_id=1, source_target_pairs={{0,1},{1,0},{2,3},{3,2},{4,5},{5,4},{6,7},{7,6},{8,9},{9,8},{10,11... | collective-permute-start | bytes 12296 | tf_op jit(solution)/shard_map/ppermute | solution.py:907
  30.1 1.9 %tracers.6 = (f32[2,4,224,256]{3,2,1,0:T(8,128)S(1)}, bf16[4,224,256]{2,1,0:T(8,128)(2,1)S(1)}, bf16[4,224,256]{2,1,0:T(8,128)(2,1)S(1)}, f32[2,16,224,256]{3,2,1,0:T(8,128)}) custom-call(f32[2,16,224,256]{3,2,1,0:T(8,128)S(1)} %get-tuple-element.55.tracer, bf16[4,224,256]{2,1,0:T(8,128)(2,1)S(1)} %get-tuple-element.88.zonal, ...), custom_call_target="tpu_custom_call", output_to_operand_aliasing={{3}: (11, {})} | custom-call | flops 18350080 | bytes 4587520 | tf_op jit(solution)/shard_map/tracers/pallas_call | solution.py:558
  32.1 0.0 collective-permute-done.7
  32.1 3.1 %collective-permute-start.8 = (f32[8,128]{1,0:T(8,128)S(1)}, f32[8,128]{1,0:T(8,128)S(1)}, u32[]{:S(2)}, u32[]{:S(2)}) collective-permute-start(f32[8,128]{1,0:T(8,128)S(1)} %max.18), channel_id=1, source_target_pairs={{0,2},{1,3},{2,0},{3,1},{4,6},{5,7},{6,4},{7,5},{8,10},{9,11},{10,... | collective-permute-start | bytes 12296 | tf_op jit(solution)/shard_map/ppermute | solution.py:907
  35.2 1.9 %tracers.7 = (f32[2,4,224,256]{3,2,1,0:T(8,128)S(1)}, f32[2,16,224,256]{3,2,1,0:T(8,128)}) custom-call(f32[2,16,224,256]{3,2,1,0:T(8,128)S(1)} %get-tuple-element.55.tracer, bf16[4,224,256]{2,1,0:T(8,128)(2,1)S(1)} %get-tuple-element.95.zonal, bf16[4,224,256]{2,1,0:T(8,128)(2,1)S(1)} %get-tuple-element.96.merid, ...), custom_call_target="tpu_custom_call", output_to_operand_aliasing={{1}: (9, {})} | custom-call | flops 18350080 | bytes 4587520 | tf_op jit(solution)/shard_map/tracers/pallas_call | solution.py:558
  37.1 0.0 collective-permute-done.8
  37.1 6.0 %solve.1 = (f32[2,16,224,256]{3,2,1,0:T(8,128)}, f32[224,256]{1,0:T(8,128)}, f32[224,256]{1,0:T(8,128)}, f32[224,256]{1,0:T(8,128)}) custom-call(f32[2,4,224,256]{3,2,1,0:T(8,128)S(1)} %get-tuple-element.99.tracer_in, f32[2,16,224,256]{3,2,1,0:T(8,128)} %get-tuple-element.100._, f32[8,128]{1,0:T(8,128)S(1)} %max.19.peak, ...), custom_call_target="tpu_custom_call", output_to_operand_aliasing={{0}: (1, {})} | custom-call | flops 11468800 | bytes 1835008 | tf_op jit(solution)/shard_map/solve/pallas_call | solution.py:834
  (5 shorter events, 0.0 us)
Async XLA Ops:
  6.6 4.1 %collective-permute-start = (f32[72,256]{1,0:T(8,128)S(1)}, f32[72,256]{1,0:T(8,128)S(1)}, u32[]{:S(2)}, u32[]{:S(2)}) collective-permute-start(f32[72,256]{1,0:T(8,128)S(1)} %get-tuple-element.59), channel_id=1, source_target_pairs={{0,4},{4,0},{8,12},{12,8},{16,20},{20,16},{24,28},{28,24},{1,5},{5... | collective-permute-start | bytes 221192 | tf_op jit(solution)/shard_map/ppermute | solution.py:894
  7.2 5.6 %collective-permute-start.1 = (f32[72,256]{1,0:T(8,128)S(1)}, f32[72,256]{1,0:T(8,128)S(1)}, u32[]{:S(2)}, u32[]{:S(2)}) collective-permute-start(f32[72,256]{1,0:T(8,128)S(1)} %get-tuple-element.60), channel_id=1, source_target_pairs={{0,28},{4,8},{8,4},{12,16},{16,12},{20,24},{24,20},{28,0},{1,29},{... | collective-permute-start | bytes 221192 | tf_op jit(solution)/shard_map/ppermute | solution.py:893
  12.9 4.2 %collective-permute-start.2 = (f32[120,128]{1,0:T(8,128)S(1)}, f32[120,128]{1,0:T(8,128)S(1)}, u32[]{:S(2)}, u32[]{:S(2)}) collective-permute-start(f32[120,128]{1,0:T(8,128)S(1)} %get-tuple-element.63), channel_id=1, source_target_pairs={{0,1},{1,0},{2,3},{3,2},{4,5},{5,4},{6,7},{7,6},{8,9},{9,8},{10,11... | collective-permute-start | bytes 184328 | tf_op jit(solution)/shard_map/ppermute | solution.py:896
  14.8 2.4 %collective-permute-start.3 = (f32[120,128]{1,0:T(8,128)S(1)}, f32[120,128]{1,0:T(8,128)S(1)}, u32[]{:S(2)}, u32[]{:S(2)}) collective-permute-start(f32[120,128]{1,0:T(8,128)S(1)} %get-tuple-element.64), channel_id=1, source_target_pairs={{0,4},{1,2},{2,1},{3,7},{4,0},{5,6},{6,5},{7,3},{8,12},{9,10},{10,... | collective-permute-start | bytes 184328 | tf_op jit(solution)/shard_map/ppermute | solution.py:897
  17.6 2.0 %collective-permute-start.4 = (f32[8,128]{1,0:T(8,128)S(1)}, f32[8,128]{1,0:T(8,128)S(1)}, u32[]{:S(2)}, u32[]{:S(2)}) collective-permute-start(f32[8,128]{1,0:T(8,128)S(1)} %get-tuple-element.65), channel_id=1, source_target_pairs={{0,4},{4,0},{8,12},{12,8},{16,20},{20,16},{24,28},{28,24},{1,5},{5... | collective-permute-start | bytes 12296 | tf_op jit(solution)/shard_map/ppermute | solution.py:907
  19.6 3.7 %collective-permute-start.5 = (f32[8,128]{1,0:T(8,128)S(1)}, f32[8,128]{1,0:T(8,128)S(1)}, u32[]{:S(2)}, u32[]{:S(2)}) collective-permute-start(f32[8,128]{1,0:T(8,128)S(1)} %max.15), channel_id=1, source_target_pairs={{0,8},{4,12},{8,0},{12,4},{16,24},{20,28},{24,16},{28,20},{1,9},{5... | collective-permute-start | bytes 12296 | tf_op jit(solution)/shard_map/ppermute | solution.py:907
  23.3 3.6 %collective-permute-start.6 = (f32[8,128]{1,0:T(8,128)S(1)}, f32[8,128]{1,0:T(8,128)S(1)}, u32[]{:S(2)}, u32[]{:S(2)}) collective-permute-start(f32[8,128]{1,0:T(8,128)S(1)} %max.16), channel_id=1, source_target_pairs={{0,16},{4,20},{8,24},{12,28},{16,0},{20,4},{24,8},{28,12},{1,17},{... | collective-permute-start | bytes 12296 | tf_op jit(solution)/shard_map/ppermute | solution.py:907
  26.9 5.1 %collective-permute-start.7 = (f32[8,128]{1,0:T(8,128)S(1)}, f32[8,128]{1,0:T(8,128)S(1)}, u32[]{:S(2)}, u32[]{:S(2)}) collective-permute-start(f32[8,128]{1,0:T(8,128)S(1)} %max.17), channel_id=1, source_target_pairs={{0,1},{1,0},{2,3},{3,2},{4,5},{5,4},{6,7},{7,6},{8,9},{9,8},{10,11... | collective-permute-start | bytes 12296 | tf_op jit(solution)/shard_map/ppermute | solution.py:907
  32.1 5.0 %collective-permute-start.8 = (f32[8,128]{1,0:T(8,128)S(1)}, f32[8,128]{1,0:T(8,128)S(1)}, u32[]{:S(2)}, u32[]{:S(2)}) collective-permute-start(f32[8,128]{1,0:T(8,128)S(1)} %max.18), channel_id=1, source_target_pairs={{0,2},{1,3},{2,0},{3,1},{4,6},{5,7},{6,4},{7,5},{8,10},{9,11},{10,... | collective-permute-start | bytes 12296 | tf_op jit(solution)/shard_map/ppermute | solution.py:907

commit v5 on v4

--- a/solution.py
+++ b/solution.py
@@ -43,14 +43,13 @@
 
 def column_kernel(
     tracer_hbm, land_hbm, levels_hbm, surf_hbm, flow_x_hbm, flow_y_hbm,
-    force, depth, to_south, to_north, to_twin, to_other, tracer, surf, flow_x, flow_y,
+    force, depth, to_twin, to_other, tracer, surf, flow_x, flow_y,
     land, levels, flat_sem, chunk_sem,
 ):
     count = tracer.shape[1]
     rows, cols = land.shape
     sides = cols // LANES
     base = 2 * count
-    lanes = lane_ids(SUB)
     size = rows // CHUNKS
 
     def copy_in(i):
@@ -75,63 +74,24 @@
         copy.start()
     for i in range(CHUNKS):
         copy_in(i).start()
-    low_kind = jnp.where((lanes >= 1) & (lanes <= base), lax.rem(lanes - 1 + count, count), -1)
-    low_kind = low_kind.astype(F32)
-    high_kind = jnp.where(lanes < base, lax.rem(lanes, count), -1).astype(F32)
-    odd = (lanes & 1) == 1
-    ends = [pl.ds(0, LANES), pl.ds((sides - 1) * LANES, LANES)]
     for copy in flats:
         copy.wait()
 
     def chunk(i, carry):
         copy_in(i).wait()
-        upper = i >= CHUNKS // 2
-        turn = jnp.where(upper, HALF, 0)
-        keep = (lanes < HALF) & upper
-        first_row = jnp.where(upper, i - CHUNKS // 2, i) * size
         for r in range(0, size, SUB):
             at = pl.ds(pl.multiple_of(i * size + r, SUB), SUB)
-            packed = [jnp.zeros((SUB, LANES), F32)] * 2
-            totals = [jnp.zeros((SUB, LANES), F32)] * sides
-            deeps = []
             for h in range(sides):
                 span = pl.ds(h * LANES, LANES)
-                deeps.append((land[at, span] * levels[at, span]).astype(F32))
-            for k in range(count):
-                values = [
-                    [tracer[c, k, at, pl.ds(h * LANES, LANES)] for h in range(sides)]
-                    for c in range(2)
-                ]
-                for h in range(sides):
-                    gain = jnp.maximum(deeps[h] - k, 0.0)
-                    totals[h] = totals[h] + gain * (values[0][h] - 0.75 * values[1][h])
-                for c in range(2):
-                    line = c * count + k
-                    both = jnp.where(lanes < HALF, values[c][0], values[c][-1])
-                    both = put_lane(both, 0, line + 1)
-                    packed[line % 2] = jnp.where(
-                        (lanes == line) | (lanes == line + 1), both, packed[line % 2]
+                deep = (land[at, span] * levels[at, span]).astype(F32)
+                total = jnp.zeros((SUB, LANES), F32)
+                for k in range(count):
+                    gain = jnp.maximum(deep - k, 0.0)
+                    total = total + gain * (
+                        tracer[0, k, at, span] - 0.75 * tracer[1, k, at, span]
                     )
-            totals = [t * (0.8 / count) for t in totals]
-            for h in range(sides):
-                span = pl.ds(h * LANES, LANES)
-                force[at, span] = totals[h]
-                depth[at, span] = deeps[h]
-            low = jnp.where(odd, packed[0], packed[1])
-            high = jnp.where(odd, packed[1], packed[0])
-            low = jnp.where(deeps[0][:, 0:1] > low_kind, low, 0.0)
-            high = jnp.where(deeps[-1][:, LANES - 1 : LANES] > high_kind, high, 0.0)
-            low, high = strip_pair(
-                low,
-                high,
-                lanes,
-                [(deeps[0], deeps[-1])]
-                + [tuple(ref[at, span] for span in ends) for ref in (surf, flow_x, flow_y)]
-                + [(totals[0], totals[-1])],
-            )
-            to = pl.ds(pl.multiple_of(first_row + r, SUB), SUB)
-            for out, value in ((to_south, low), (to_north, high)):
-                out[to, :] = jnp.where(keep, out[to, :], pltpu.roll(value, turn, 1))
+                force[at, span] = total * (0.8 / count)
+                depth[at, span] = deep
         return carry
 
     lax.fori_loop(0, CHUNKS, chunk, 0)
@@ -172,9 +132,8 @@
 def column_pass(tracer, land, levels, surf, flow_x, flow_y):
     two, count, rows, cols = tracer.shape
     lines = (two * count + FIELDS * SUB, cols)
-    strip = (rows // 2 + SUB, LANES)
     plain = (rows, cols)
-    shapes = [plain, plain, strip, strip, lines, lines, tracer.shape, plain, plain, plain]
+    shapes = [plain, plain, lines, lines, tracer.shape, plain, plain, plain]
     return pl.pallas_call(
         column_kernel,
         in_specs=[IN_HBM] * 6,
@@ -196,6 +155,83 @@
             pltpu.with_memory_space_constraint(value, pltpu.HBM)
             for value in (tracer, land, levels, surf, flow_x, flow_y)
         )
+    )
+
+
+def strip_kernel(
+    tracer, depth, surf, flow_x, flow_y, force, zonal_hbm, merid_hbm,
+    to_south, to_north, zonal, merid, sem,
+):
+    flows = [
+        pltpu.make_async_copy(source, target, sem.at[i])
+        for i, (source, target) in enumerate(((zonal_hbm, zonal), (merid_hbm, merid)))
+    ]
+    for copy in flows:
+        copy.start()
+    count = tracer.shape[1]
+    rows, cols = depth.shape
+    base = 2 * count
+    lanes = lane_ids(SUB)
+    size = rows // CHUNKS
+    low_kind = jnp.where((lanes >= 1) & (lanes <= base), lax.rem(lanes - 1 + count, count), -1)
+    low_kind = low_kind.astype(F32)
+    high_kind = jnp.where(lanes < base, lax.rem(lanes, count), -1).astype(F32)
+    odd = (lanes & 1) == 1
+    ends = [pl.ds(0, LANES), pl.ds(cols - LANES, LANES)]
+
+    def chunk(i, carry):
+        upper = i >= CHUNKS // 2
+        turn = jnp.where(upper, HALF, 0)
+        keep = (lanes < HALF) & upper
+        first_row = jnp.where(upper, i - CHUNKS // 2, i) * size
+        for r in range(0, size, SUB):
+            at = pl.ds(pl.multiple_of(i * size + r, SUB), SUB)
+            packed = [jnp.zeros((SUB, LANES), F32)] * 2
+            for line in range(base):
+                c, k = divmod(line, count)
+                both = jnp.where(lanes < HALF, tracer[c, k, at, ends[0]], tracer[c, k, at, ends[1]])
+                both = put_lane(both, 0, line + 1)
+                packed[line % 2] = jnp.where(
+                    (lanes == line) | (lanes == line + 1), both, packed[line % 2]
+                )
+            pairs = [
+                tuple(ref[at, span] for span in ends)
+                for ref in (depth, surf, flow_x, flow_y, force)
+            ]
+            low = jnp.where(odd, packed[0], packed[1])
+            high = jnp.where(odd, packed[1], packed[0])
+            low = jnp.where(pairs[0][0][:, 0:1] > low_kind, low, 0.0)
+            high = jnp.where(pairs[0][1][:, LANES - 1 : LANES] > high_kind, high, 0.0)
+            low, high = strip_pair(low, high, lanes, pairs)
+            to = pl.ds(pl.multiple_of(first_row + r, SUB), SUB)
+            for out, value in ((to_south, low), (to_north, high)):
+                out[to, :] = jnp.where(keep, out[to, :], pltpu.roll(value, turn, 1))
+        return carry
+
+    lax.fori_loop(0, CHUNKS, chunk, 0)
+    for out in (to_south, to_north):
+        out[pl.ds(rows // 2, SUB), :] = jnp.zeros((SUB, LANES), F32)
+    for copy in flows:
+        copy.wait()
+
+
+def strip_pass(zonal, merid, tracer, depth, surf, flow_x, flow_y, force):
+    shape = jax.ShapeDtypeStruct((depth.shape[0] // 2 + SUB, LANES), F32)
+    return pl.pallas_call(
+        strip_kernel,
+        in_specs=[IN_VMEM] * 6 + [IN_HBM] * 2,
+        out_specs=[IN_VMEM] * 4,
+        out_shape=[shape, shape]
+        + [jax.ShapeDtypeStruct(value.shape, BF16) for value in (zonal, merid)],
+        scratch_shapes=[pltpu.SemaphoreType.DMA((2,))],
+        compiler_params=pltpu.CompilerParams(vmem_limit_bytes=VMEM_LIMIT),
+        cost_estimate=pl.CostEstimate(
+            flops=6 * tracer.size, bytes_accessed=4 * tracer.size, transcendentals=0
+        ),
+        name="strips",
+    )(
+        tracer, depth, surf, flow_x, flow_y, force,
+        *(pltpu.with_memory_space_constraint(value, pltpu.HBM) for value in (zonal, merid)),
     )
 
 
@@ -357,17 +393,11 @@
     )(depth, west, east, from_twin, from_other)
 
 
-def around_kernel(
-    part, depth, west, east, south, north, zonal_hbm, merid_hbm,
-    edge_y, around, zonal, merid, masked, sem,
-):
+def around_kernel(depth, west, east, south, north, edge_y, around, masked):
     rows, cols = depth.shape
     sides = cols // LANES
     lanes = lane_ids(SUB)
     spans = [pl.ds(h * LANES, LANES) for h in range(sides)]
-    flows = flow_copies(part, zonal_hbm, merid_hbm, zonal, merid, sem)
-    for copy in flows:
-        copy.start()
     open_south, open_north = latitude_ends()
     for h in range(sides):
         masked[h, pl.ds(0, SUB), :] = west[pl.ds(BASE, SUB), spans[h]]
@@ -391,66 +421,38 @@
             for n in range(2):
                 pair = jnp.concatenate([shifted[0][n][h], shifted[1][n][h]], 0)
                 around[2 + n, h, at, :] = pair.astype(BF16)
-    for copy in flows:
-        copy.wait()
-
-
-def flow_copies(part, zonal_hbm, merid_hbm, zonal, merid, sem):
-    levels = pl.ds(part[0], part[1] - part[0])
-    return [
-        pltpu.make_async_copy(source.at[levels], target, sem.at[i])
-        for i, (source, target) in enumerate(((zonal_hbm, zonal), (merid_hbm, merid)))
-    ]
-
-
-def in_hbm(*values):
-    return [pltpu.with_memory_space_constraint(value, pltpu.HBM) for value in values]
-
-
-def around_pass(part, depth, west, east, south, north, zonal, merid):
+
+
+def around_pass(depth, west, east, south, north):
     rows, cols = depth.shape
     sides = cols // LANES
     return pl.pallas_call(
-        functools.partial(around_kernel, part),
-        in_specs=[IN_VMEM] * 5 + [IN_HBM] * 2,
-        out_specs=[IN_VMEM] * 4,
+        around_kernel,
+        in_specs=[IN_VMEM] * 5,
+        out_specs=[IN_VMEM] * 2,
         out_shape=[
             jax.ShapeDtypeStruct((2, rows, LANES), F32),
             jax.ShapeDtypeStruct((4, sides, rows, LANES), BF16),
-        ]
-        + [jax.ShapeDtypeStruct((part[1] - part[0], rows, cols), BF16)] * 2,
-        scratch_shapes=[
-            pltpu.VMEM((sides, rows + 2 * SUB, LANES), F32),
-            pltpu.SemaphoreType.DMA((2,)),
         ],
+        scratch_shapes=[pltpu.VMEM((sides, rows + 2 * SUB, LANES), F32)],
         compiler_params=pltpu.CompilerParams(vmem_limit_bytes=VMEM_LIMIT),
         cost_estimate=pl.CostEstimate(
             flops=30 * depth.size, bytes_accessed=16 * depth.size, transcendentals=0
         ),
         name="around",
-    )(depth, west, east, south, north, *in_hbm(zonal, merid))
+    )(depth, west, east, south, north)
 
 
 def tracer_kernel(parts, index, tracer, zonal, merid, depth, west, east, edge_y, around, *rest):
     start, stop = parts[index]
-    rest = list(rest)
-    later = index + 1 < len(parts)
-    flows_hbm = [rest.pop(0), rest.pop(0)] if later else []
-    earlier = rest.pop(0) if index else None
-    if index > 1:
-        rest.pop(0)
-    out = rest.pop(0)
-    flows = [rest.pop(0), rest.pop(0)] if later else []
-    placed = rest.pop(0) if index else None
-    masked, sem = rest
     copies = []
-    if later:
-        copies += flow_copies(parts[index + 1], *flows_hbm, *flows, sem)
     if index:
+        earlier, placed = rest[0], rest[-3]
         first, last = parts[index - 1]
         for c in range(2):
             target = placed.at[c, pl.ds(first, last - first)]
-            copies.append(pltpu.make_async_copy(earlier.at[c], target, sem.at[2 + c]))
+            copies.append(pltpu.make_async_copy(earlier.at[c], target, rest[-1].at[c]))
+    out, masked = rest[-4 if index else -3], rest[-2]
     for copy in copies:
         copy.start()
     rows, cols = depth.shape
@@ -494,8 +496,8 @@
                 pairs.append(
                     (
                         1.0 - 0.2 * near.astype(F32),
-                        (zonal[level - start, wide, spans[h]] * quarter).astype(F32),
-                        (merid[level - start, wide, spans[h]] * quarter).astype(F32),
+                        (zonal[level, wide, spans[h]] * quarter).astype(F32),
+                        (merid[level, wide, spans[h]] * quarter).astype(F32),
                     )
                 )
             for sub in range(2):
@@ -530,22 +532,15 @@
         copy.wait()
 
 
-def tracer_pass(parts, index, tracer, flows, depth, west, east, known, flows_hbm, earlier, placed):
+def tracer_pass(parts, index, tracer, zonal, merid, depth, west, east, known, earlier, placed):
     two, count, rows, cols = tracer.shape
     sides = cols // LANES
     part = parts[index][1] - parts[index][0]
-    later = index + 1 < len(parts)
-    operands = [tracer, *flows, depth, west, east, *known]
+    operands = [tracer, zonal, merid, depth, west, east, *known]
     specs = [IN_VMEM] * len(operands)
     shapes = [jax.ShapeDtypeStruct((two, part, rows, cols), F32)]
     outs = [IN_VMEM]
     aliases = {}
-    if later:
-        after = parts[index + 1][1] - parts[index + 1][0]
-        operands += in_hbm(*flows_hbm)
-        specs += [IN_HBM] * 2
-        shapes += [jax.ShapeDtypeStruct((after, rows, cols), BF16)] * 2
-        outs += [IN_VMEM] * 2
     if index:
         operands.append(earlier)
         specs.append(IN_VMEM)
@@ -562,7 +557,7 @@
         out_shape=shapes,
         scratch_shapes=[
             pltpu.VMEM((2, sides, rows + 2 * SUB, LANES), F32),
-            pltpu.SemaphoreType.DMA((4,)),
+            pltpu.SemaphoreType.DMA((2,)),
         ],
         input_output_aliases=aliases,
         compiler_params=pltpu.CompilerParams(vmem_limit_bytes=VMEM_LIMIT),
@@ -573,10 +568,7 @@
         ),
         name="tracers",
     )(*operands)
-    results = list(results)
-    made = results.pop(0)
-    flows = (results.pop(0), results.pop(0)) if later else ()
-    return made, flows, results.pop(0) if index else None
+    return results if index else (results[0], None)
 
 
 def group_of(tiles):
@@ -887,11 +879,14 @@
 ):
     count = tracer.shape[1]
     (
-        force, depth, to_south, to_north, to_twin, to_other,
-        tracer, surface_prev, transport_x, transport_y,
+        force, depth, to_twin, to_other, tracer, surface_prev, transport_x, transport_y,
     ) = column_pass(tracer, land_mask, levels, surface_prev, transport_x, transport_y)
+    fields = (depth, surface_prev, transport_x, transport_y, force)
     from_other = lax.ppermute(to_other, "gx", other_x_pairs())
     from_twin = lax.ppermute(to_twin, "gx", twin_pairs("gx"))
+    to_south, to_north, zonal_flow, meridional_flow = strip_pass(
+        zonal_flow, meridional_flow, tracer, *fields
+    )
     to_twin, to_other, west, east = pack_pass(to_south, to_north, from_twin, from_other)
     from_twin = lax.ppermute(to_twin, "gy", twin_pairs("gy"))
     from_other = lax.ppermute(to_other, ("gx", "gy"), other_y_pairs())
@@ -900,24 +895,22 @@
     rounds = [r for axis in ("gx", "gy") for r in spread_rounds(axis)]
     cuts = [count * i // PARTS for i in range(PARTS + 1)]
     parts = tuple(zip(cuts, cuts[1:]))
-    flows_hbm = (zonal_flow, meridional_flow)
     first = len(rounds) - PARTS
-    known, flows, made, placed = (), (), None, None
+    known, made, placed = (), None, None
     for turn, (axis, pairs) in enumerate(rounds):
         moved = lax.ppermute(peak, axis, pairs)
         if turn == 0:
-            *known, zonal, merid = around_pass(parts[0], depth, *halo, *flows_hbm)
-            moved, known, flows = lax.optimization_barrier((moved, known, (zonal, merid)))
+            known = around_pass(depth, *halo)
+            moved, known = lax.optimization_barrier((moved, known))
         if turn >= first:
-            made, flows, placed = tracer_pass(
-                parts, turn - first, tracer, flows, depth, west, east, known, flows_hbm, made, placed
+            made, placed = tracer_pass(
+                parts, turn - first, tracer, zonal_flow, meridional_flow, depth,
+                west, east, known, made, placed,
             )
         peak = jnp.maximum(peak, moved)
         if first <= turn < len(rounds) - 1:
-            peak, made, flows = lax.optimization_barrier((peak, made, flows))
-    return solve_pass(
-        parts[-1], made, placed, peak, depth, surface_prev, transport_x, transport_y, force, *halo
-    )
+            peak, made = lax.optimization_barrier((peak, made))
+    return solve_pass(parts[-1], made, placed, peak, *fields, *halo)
 
 
 def solution(mesh):

time: 43.3 us -> 40.6 us (0.938)
  starting transfers between devices: 15.3 us -> 12.5 us
  waiting for transfers between devices: 4.83 us -> 5.38 us
    ppermute x5, starting transfers between devices: 9.3 us -> 6.78 us  [local(): moved = lax.ppermute(peak, axis, pairs)]
    ppermute x5, waiting for transfers between devices: 0.43 us -> 2.73 us  [local(): moved = lax.ppermute(peak, axis, pairs)]
    pallas_call x1, Pallas kernels: 6 us -> 3.94 us  [column_pass(): pl.pallas_call(column_kernel, in_specs=[IN_HBM] * 6, out_specs=[IN_VMEM]...]
    ppermute x1, waiting for transfers between devices: 2.03 us -> 0.01 us  [local(): from_other = lax.ppermute(to_other, 'gx', other_x_pairs())]
    pallas_call x1 -> x2, Pallas kernels: 1.95 us -> 3.72 us  [the longest x1 2.87 us: strip_pass(): pl.pallas_call(strip_kernel, in_specs=[IN_VMEM] * 6 + [IN_HBM] * 2, out_s...]
  transfers between devices with their start and end apart: 9 -> 9, of which waited for: 3 -> 4; matrix products, arithmetic and copies ran while one was open for 0% -> 0% of each run, Pallas kernels for 22% -> 28%
where the time goes in v5:
time: 40.6 us; the launch traced here: 40.5 us
  Pallas kernels  21.9 us (54%)
  starting transfers between devices  12.5 us (31%)
  waiting for transfers between devices  5.38 us (13%)
  between operations  0.75 us (2%)
    pallas_call x4, Pallas kernels, tracer_pass(): pl.pallas_call(functools.partial(tracer_kernel, parts, index), in_specs=s...  7.66 us
    ppermute x5, starting transfers between devices, local(): moved = lax.ppermute(peak, axis, pairs)  6.78 us
    pallas_call x1, Pallas kernels, solve_pass(): pl.pallas_call(functools.partial(solve_kernel, last_part), in_specs=[IN_V...  5.95 us
    pallas_call x1, Pallas kernels, column_pass(): pl.pallas_call(column_kernel, in_specs=[IN_HBM] * 6, out_specs=[IN_VMEM]...  3.94 us
    ppermute x1, starting transfers between devices, local(): from_other = lax.ppermute(to_other, 'gx', other_x_pairs())  3.54 us
    pallas_call x1, Pallas kernels, strip_pass(): pl.pallas_call(strip_kernel, in_specs=[IN_VMEM] * 6 + [IN_HBM] * 2, out_s...  2.87 us
    ppermute x5, waiting for transfers between devices, local(): moved = lax.ppermute(peak, axis, pairs)  2.73 us
    ppermute x1, waiting for transfers between devices, local(): from_twin = lax.ppermute(to_twin, 'gy', twin_pairs('gy'))  2.64 us
  transfers between devices with their start and end apart: 9, of which 4 were waited for; matrix products, arithmetic and copies ran while one was open for 0% of the time, Pallas kernels for 28%

profile of v5, /device:TPU:0, one launch (start us, length us, event | category | flops | bytes accessed | tf_op | source)
XLA Modules:
  0.0 40.5 jit_solution(14695563136593808908)
XLA Ops:
  0.6 3.9 %columns.1 = (f32[224,256]{1,0:T(8,128)S(1)}, f32[224,256]{1,0:T(8,128)S(1)}, f32[72,256]{1,0:T(8,128)S(1)}, f32[72,256]{1,0:T(8,128)S(1)}, f32[2,16,224,256]{3,...) custom-call(f32[2,16,224,256]{3,2,1,0:T(8,128)} %tracer_hbm.1, ...), custom_call_target="tpu_custom_call" | custom-call | flops 11010048 | bytes 7340032 | tf_op jit(solution)/shard_map/columns/pallas_call | solution.py:137
  4.6 0.6 %collective-permute-start = (f32[72,256]{1,0:T(8,128)S(1)}, f32[72,256]{1,0:T(8,128)S(1)}, u32[]{:S(2)}, u32[]{:S(2)}) collective-permute-start(f32[72,256]{1,0:T(8,128)S(1)} %get-tuple-element.50), channel_id=1, source_target_pairs={{0,4},{4,0},{8,12},{12,8},{16,20},{20,16},{24,28},{28,24},{1,5},{5... | collective-permute-start | bytes 221192 | tf_op jit(solution)/shard_map/ppermute | solution.py:886
  5.1 3.5 %collective-permute-start.1 = (f32[72,256]{1,0:T(8,128)S(1)}, f32[72,256]{1,0:T(8,128)S(1)}, u32[]{:S(2)}, u32[]{:S(2)}) collective-permute-start(f32[72,256]{1,0:T(8,128)S(1)} %get-tuple-element.51), channel_id=1, source_target_pairs={{0,28},{4,8},{8,4},{12,16},{16,12},{20,24},{24,20},{28,0},{1,29},{... | collective-permute-start | bytes 221192 | tf_op jit(solution)/shard_map/ppermute | solution.py:885
  8.7 2.9 %strips.1 = (f32[120,128]{1,0:T(8,128)S(1)}, f32[120,128]{1,0:T(8,128)S(1)}, bf16[16,224,256]{2,1,0:T(8,128)(2,1)S(1)}, bf16[16,224,256]{2,1,0:T(8,128)(2,1)S(1)}) custom-call(f32[2,16,224,256]{3,2,1,0:T(8,128)S(1)} %get-tuple-element.40.tracer, f32[224,256]{1,0:T(8,128)S(1)} %get-tuple-element.41.depth, f32[224,256]{1,0:T(8,128)S(1)} %get-tuple-element.42.surf, ...), custom_call_target="tpu_custom_call" | custom-call | flops 11010048 | bytes 7340032 | tf_op jit(solution)/shard_map/strips/pallas_call | solution.py:220
  11.6 0.0 collective-permute-done.from_twin
  11.6 0.0 collective-permute-done.1.from_other
  11.6 0.2 corners.1
  11.7 1.6 %collective-permute-start.2 = (f32[120,128]{1,0:T(8,128)S(1)}, f32[120,128]{1,0:T(8,128)S(1)}, u32[]{:S(2)}, u32[]{:S(2)}) collective-permute-start(f32[120,128]{1,0:T(8,128)S(1)} %get-tuple-element.54), channel_id=1, source_target_pairs={{0,1},{1,0},{2,3},{3,2},{4,5},{5,4},{6,7},{7,6},{8,9},{9,8},{10,11... | collective-permute-start | bytes 184328 | tf_op jit(solution)/shard_map/ppermute | solution.py:891
  13.3 0.0 collective-permute-start.3
  13.3 2.6 %collective-permute-done.2.from_twin = f32[120,128]{1,0:T(8,128)S(1)} collective-permute-done((f32[120,128]{1,0:T(8,128)S(1)}, f32[120,128]{1,0:T(8,128)S(1)}, u32[]{:S(2)}, u32[]{:S(2)}) %collective-permute-start.2) | collective-permute-done | bytes 61472 | tf_op jit(solution)/shard_map/ppermute | solution.py:891
  16.0 0.0 collective-permute-done.3.from_other
  16.0 0.4 %peak.1 = (f32[8,128]{1,0:T(8,128)S(1)}, f32[120,128]{1,0:T(8,128)S(1)}, f32[120,128]{1,0:T(8,128)S(1)}) custom-call(f32[224,256]{1,0:T(8,128)S(1)} %get-tuple-element.41.depth, f32[72,256]{1,0:T(8,128)S(1)} %get-tuple-element.52.west, f32[72,256]{1,0:T(8,128)S(1)} %get-tuple-element.53.east, f32[120,128]{1,0:T(8,128)S(1)} %collective-permute-done.2.from_twin, ...), custom_call_target="tpu_custom_call" | custom-call | flops 1720320 | bytes 229376 | tf_op jit(solution)/shard_map/peak/pallas_call | solution.py:382
  16.4 0.0 collective-permute-start.4
  16.4 0.9 %around.1 = (f32[2,224,128]{2,1,0:T(8,128)S(1)}, bf16[4,2,224,128]{3,2,1,0:T(8,128)(2,1)S(1)}) custom-call(f32[224,256]{1,0:T(8,128)S(1)} %get-tuple-element.41.depth, f32[72,256]{1,0:T(8,128)S(1)} %get-tuple-element.52.west, f32[72,256]{1,0:T(8,128)S(1)} %get-tuple-element.53.east, f32[120,128]{1,0:T(8,128)S(1)} %get-tuple-element.57.south, ...), custom_call_target="tpu_custom_call" | custom-call | flops 1720320 | bytes 917504 | tf_op jit(solution)/shard_map/around/pallas_call | solution.py:429
  17.3 0.3 collective-permute-done.4
  17.6 0.1 collective-permute-start.5
  17.7 1.9 %tracers.4.rest_0_ = f32[2,4,224,256]{3,2,1,0:T(8,128)S(1)} custom-call(f32[2,16,224,256]{3,2,1,0:T(8,128)S(1)} %get-tuple-element.40.tracer, bf16[16,224,256]{2,1,0:T(8,128)(2,1)S(1)} %get-tuple-element.46.zonal, bf16[16,224,256]{2,1,0:T(8,128)(2,1)S(1)} %get-tuple-element.47.merid, f32[224,256]{1,0:T(8,128)S(1)} %get-tuple-element.41.depth, ...), custom_call_target="tpu_custom_call" | custom-call | flops 18350080 | bytes 4587520 | tf_op jit(solution)/shard_map/tracers/pallas_call | solution.py:553
  19.7 1.5 %collective-permute-done.5 = f32[8,128]{1,0:T(8,128)S(1)} collective-permute-done((f32[8,128]{1,0:T(8,128)S(1)}, f32[8,128]{1,0:T(8,128)S(1)}, u32[]{:S(2)}, u32[]{:S(2)}) %collective-permute-start.5) | collective-permute-done | bytes 4128 | tf_op jit(solution)/shard_map/ppermute | solution.py:901
  21.2 0.8 %collective-permute-start.6 = (f32[8,128]{1,0:T(8,128)S(1)}, f32[8,128]{1,0:T(8,128)S(1)}, u32[]{:S(2)}, u32[]{:S(2)}) collective-permute-start(f32[8,128]{1,0:T(8,128)S(1)} %max.16), channel_id=1, source_target_pairs={{0,16},{4,20},{8,24},{12,28},{16,0},{20,4},{24,8},{28,12},{1,17},{... | collective-permute-start | bytes 12296 | tf_op jit(solution)/shard_map/ppermute | solution.py:901
  22.0 1.9 %tracers.5 = (f32[2,4,224,256]{3,2,1,0:T(8,128)S(1)}, f32[2,16,224,256]{3,2,1,0:T(8,128)}) custom-call(f32[2,16,224,256]{3,2,1,0:T(8,128)S(1)} %get-tuple-element.40.tracer, bf16[16,224,256]{2,1,0:T(8,128)(2,1)S(1)} %get-tuple-element.46.zonal, bf16[16,224,256]{2,1,0:T(8,128)(2,1)S(1)} %get-tuple-element.47.merid, f32[224,256]{1,0:T(8,128)S(1)} %get-tuple-element.41.depth, ...), custom_call_target="tpu_custom_call" | custom-call | flops 18350080 | bytes 4587520 | tf_op jit(solution)/shard_map/tracers/pallas_call | solution.py:553
  23.9 0.9 %collective-permute-done.6 = f32[8,128]{1,0:T(8,128)S(1)} collective-permute-done((f32[8,128]{1,0:T(8,128)S(1)}, f32[8,128]{1,0:T(8,128)S(1)}, u32[]{:S(2)}, u32[]{:S(2)}) %collective-permute-start.6) | collective-permute-done | bytes 4128 | tf_op jit(solution)/shard_map/ppermute | solution.py:901
  24.8 2.7 %collective-permute-start.7 = (f32[8,128]{1,0:T(8,128)S(1)}, f32[8,128]{1,0:T(8,128)S(1)}, u32[]{:S(2)}, u32[]{:S(2)}) collective-permute-start(f32[8,128]{1,0:T(8,128)S(1)} %max.17), channel_id=1, source_target_pairs={{0,1},{1,0},{2,3},{3,2},{4,5},{5,4},{6,7},{7,6},{8,9},{9,8},{10,11... | collective-permute-start | bytes 12296 | tf_op jit(solution)/shard_map/ppermute | solution.py:901
  27.5 1.9 %tracers.6 = (f32[2,4,224,256]{3,2,1,0:T(8,128)S(1)}, f32[2,16,224,256]{3,2,1,0:T(8,128)}) custom-call(f32[2,16,224,256]{3,2,1,0:T(8,128)S(1)} %get-tuple-element.40.tracer, bf16[16,224,256]{2,1,0:T(8,128)(2,1)S(1)} %get-tuple-element.46.zonal, bf16[16,224,256]{2,1,0:T(8,128)(2,1)S(1)} %get-tuple-element.47.merid, ...), custom_call_target="tpu_custom_call", output_to_operand_aliasing={{1}: (9, {})} | custom-call | flops 18350080 | bytes 4587520 | tf_op jit(solution)/shard_map/tracers/pallas_call | solution.py:553
  29.4 0.0 collective-permute-done.7
  29.5 3.1 %collective-permute-start.8 = (f32[8,128]{1,0:T(8,128)S(1)}, f32[8,128]{1,0:T(8,128)S(1)}, u32[]{:S(2)}, u32[]{:S(2)}) collective-permute-start(f32[8,128]{1,0:T(8,128)S(1)} %max.18), channel_id=1, source_target_pairs={{0,2},{1,3},{2,0},{3,1},{4,6},{5,7},{6,4},{7,5},{8,10},{9,11},{10,... | collective-permute-start | bytes 12296 | tf_op jit(solution)/shard_map/ppermute | solution.py:901
  32.6 1.9 %tracers.7 = (f32[2,4,224,256]{3,2,1,0:T(8,128)S(1)}, f32[2,16,224,256]{3,2,1,0:T(8,128)}) custom-call(f32[2,16,224,256]{3,2,1,0:T(8,128)S(1)} %get-tuple-element.40.tracer, bf16[16,224,256]{2,1,0:T(8,128)(2,1)S(1)} %get-tuple-element.46.zonal, bf16[16,224,256]{2,1,0:T(8,128)(2,1)S(1)} %get-tuple-element.47.merid, ...), custom_call_target="tpu_custom_call", output_to_operand_aliasing={{1}: (9, {})} | custom-call | flops 18350080 | bytes 4587520 | tf_op jit(solution)/shard_map/tracers/pallas_call | solution.py:553
  34.5 0.0 collective-permute-done.8
  34.5 6.0 %solve.1 = (f32[2,16,224,256]{3,2,1,0:T(8,128)}, f32[224,256]{1,0:T(8,128)}, f32[224,256]{1,0:T(8,128)}, f32[224,256]{1,0:T(8,128)}) custom-call(f32[2,4,224,256]{3,2,1,0:T(8,128)S(1)} %get-tuple-element.73.tracer_in, f32[2,16,224,256]{3,2,1,0:T(8,128)} %get-tuple-element.74._, f32[8,128]{1,0:T(8,128)S(1)} %max.19.peak, ...), custom_call_target="tpu_custom_call", output_to_operand_aliasing={{0}: (1, {})} | custom-call | flops 11468800 | bytes 1835008 | tf_op jit(solution)/shard_map/solve/pallas_call | solution.py:826
  (5 shorter events, 0.0 us)
Async XLA Ops:
  4.6 7.0 %collective-permute-start = (f32[72,256]{1,0:T(8,128)S(1)}, f32[72,256]{1,0:T(8,128)S(1)}, u32[]{:S(2)}, u32[]{:S(2)}) collective-permute-start(f32[72,256]{1,0:T(8,128)S(1)} %get-tuple-element.50), channel_id=1, source_target_pairs={{0,4},{4,0},{8,12},{12,8},{16,20},{20,16},{24,28},{28,24},{1,5},{5... | collective-permute-start | bytes 221192 | tf_op jit(solution)/shard_map/ppermute | solution.py:886
  5.1 6.4 %collective-permute-start.1 = (f32[72,256]{1,0:T(8,128)S(1)}, f32[72,256]{1,0:T(8,128)S(1)}, u32[]{:S(2)}, u32[]{:S(2)}) collective-permute-start(f32[72,256]{1,0:T(8,128)S(1)} %get-tuple-element.51), channel_id=1, source_target_pairs={{0,28},{4,8},{8,4},{12,16},{16,12},{20,24},{24,20},{28,0},{1,29},{... | collective-permute-start | bytes 221192 | tf_op jit(solution)/shard_map/ppermute | solution.py:885
  11.7 4.2 %collective-permute-start.2 = (f32[120,128]{1,0:T(8,128)S(1)}, f32[120,128]{1,0:T(8,128)S(1)}, u32[]{:S(2)}, u32[]{:S(2)}) collective-permute-start(f32[120,128]{1,0:T(8,128)S(1)} %get-tuple-element.54), channel_id=1, source_target_pairs={{0,1},{1,0},{2,3},{3,2},{4,5},{5,4},{6,7},{7,6},{8,9},{9,8},{10,11... | collective-permute-start | bytes 184328 | tf_op jit(solution)/shard_map/ppermute | solution.py:891
  13.3 2.6 %collective-permute-start.3 = (f32[120,128]{1,0:T(8,128)S(1)}, f32[120,128]{1,0:T(8,128)S(1)}, u32[]{:S(2)}, u32[]{:S(2)}) collective-permute-start(f32[120,128]{1,0:T(8,128)S(1)} %get-tuple-element.55), channel_id=1, source_target_pairs={{0,4},{1,2},{2,1},{3,7},{4,0},{5,6},{6,5},{7,3},{8,12},{9,10},{10,... | collective-permute-start | bytes 184328 | tf_op jit(solution)/shard_map/ppermute | solution.py:892
  16.4 1.2 %collective-permute-start.4 = (f32[8,128]{1,0:T(8,128)S(1)}, f32[8,128]{1,0:T(8,128)S(1)}, u32[]{:S(2)}, u32[]{:S(2)}) collective-permute-start(f32[8,128]{1,0:T(8,128)S(1)} %get-tuple-element.56), channel_id=1, source_target_pairs={{0,4},{4,0},{8,12},{12,8},{16,20},{20,16},{24,28},{28,24},{1,5},{5... | collective-permute-start | bytes 12296 | tf_op jit(solution)/shard_map/ppermute | solution.py:901
  17.6 3.6 %collective-permute-start.5 = (f32[8,128]{1,0:T(8,128)S(1)}, f32[8,128]{1,0:T(8,128)S(1)}, u32[]{:S(2)}, u32[]{:S(2)}) collective-permute-start(f32[8,128]{1,0:T(8,128)S(1)} %max.15), channel_id=1, source_target_pairs={{0,8},{4,12},{8,0},{12,4},{16,24},{20,28},{24,16},{28,20},{1,9},{5... | collective-permute-start | bytes 12296 | tf_op jit(solution)/shard_map/ppermute | solution.py:901
  21.2 3.6 %collective-permute-start.6 = (f32[8,128]{1,0:T(8,128)S(1)}, f32[8,128]{1,0:T(8,128)S(1)}, u32[]{:S(2)}, u32[]{:S(2)}) collective-permute-start(f32[8,128]{1,0:T(8,128)S(1)} %max.16), channel_id=1, source_target_pairs={{0,16},{4,20},{8,24},{12,28},{16,0},{20,4},{24,8},{28,12},{1,17},{... | collective-permute-start | bytes 12296 | tf_op jit(solution)/shard_map/ppermute | solution.py:901
  24.8 4.6 %collective-permute-start.7 = (f32[8,128]{1,0:T(8,128)S(1)}, f32[8,128]{1,0:T(8,128)S(1)}, u32[]{:S(2)}, u32[]{:S(2)}) collective-permute-start(f32[8,128]{1,0:T(8,128)S(1)} %max.17), channel_id=1, source_target_pairs={{0,1},{1,0},{2,3},{3,2},{4,5},{5,4},{6,7},{7,6},{8,9},{9,8},{10,11... | collective-permute-start | bytes 12296 | tf_op jit(solution)/shard_map/ppermute | solution.py:901
  29.5 5.1 %collective-permute-start.8 = (f32[8,128]{1,0:T(8,128)S(1)}, f32[8,128]{1,0:T(8,128)S(1)}, u32[]{:S(2)}, u32[]{:S(2)}) collective-permute-start(f32[8,128]{1,0:T(8,128)S(1)} %max.18), channel_id=1, source_target_pairs={{0,2},{1,3},{2,0},{3,1},{4,6},{5,7},{6,4},{7,5},{8,10},{9,11},{10,... | collective-permute-start | bytes 12296 | tf_op jit(solution)/shard_map/ppermute | solution.py:901

commit v6 on v5

--- a/solution.py
+++ b/solution.py
@@ -41,6 +41,11 @@
     return low, high
 
 
+def slices_of(rows):
+    tiles = rows // SUB
+    return tiles // max(n for n in range(1, 5) if tiles % n == 0)
+
+
 def column_kernel(
     tracer_hbm, land_hbm, levels_hbm, surf_hbm, flow_x_hbm, flow_y_hbm,
     force, depth, to_twin, to_other, tracer, surf, flow_x, flow_y,
@@ -50,7 +55,8 @@
     rows, cols = land.shape
     sides = cols // LANES
     base = 2 * count
-    size = rows // CHUNKS
+    slices = slices_of(rows)
+    size = rows // slices
 
     def copy_in(i):
         part = pl.ds(pl.multiple_of(i * size, SUB), size)
@@ -70,11 +76,13 @@
             )
         )
     ]
-    for copy in flats:
+    for copy in flats[:2]:
         copy.start()
-    for i in range(CHUNKS):
+    for i in range(slices):
         copy_in(i).start()
-    for copy in flats:
+    for copy in flats[2:]:
+        copy.start()
+    for copy in flats[:2]:
         copy.wait()
 
     def chunk(i, carry):
@@ -94,7 +102,9 @@
                 depth[at, span] = deep
         return carry
 
-    lax.fori_loop(0, CHUNKS, chunk, 0)
+    lax.fori_loop(0, slices, chunk, 0)
+    for copy in flats[2:]:
+        copy.wait()
 
     def edge_rows(out, line, tile):
         for h in range(sides):
@@ -143,7 +153,7 @@
             pltpu.VMEM(plain, jnp.int32),
             pltpu.VMEM(plain, jnp.int32),
             pltpu.SemaphoreType.DMA((5,)),
-            pltpu.SemaphoreType.DMA((CHUNKS,)),
+            pltpu.SemaphoreType.DMA((slices_of(rows),)),
         ],
         compiler_params=pltpu.CompilerParams(vmem_limit_bytes=VMEM_LIMIT),
         cost_estimate=pl.CostEstimate(

time: 40.6 us -> 40.4 us (level)
  no operation moved by 1% of the time
where the time goes in v6:
time: 40.4 us; the launch traced here: 40.2 us
  Pallas kernels  21.6 us (53%)
  starting transfers between devices  12.5 us (31%)
  waiting for transfers between devices  5.38 us (13%)
  between operations  0.75 us (2%)
    pallas_call x4, Pallas kernels, tracer_pass(): pl.pallas_call(functools.partial(tracer_kernel, parts, index), in_specs=s...  7.66 us
    ppermute x5, starting transfers between devices, local(): moved = lax.ppermute(peak, axis, pairs)  6.78 us
    pallas_call x1, Pallas kernels, solve_pass(): pl.pallas_call(functools.partial(solve_kernel, last_part), in_specs=[IN_V...  5.95 us
    pallas_call x1, Pallas kernels, column_pass(): pl.pallas_call(column_kernel, in_specs=[IN_HBM] * 6, out_specs=[IN_VMEM]...  3.69 us
    ppermute x1, starting transfers between devices, local(): from_other = lax.ppermute(to_other, 'gx', other_x_pairs())  3.54 us
    pallas_call x1, Pallas kernels, strip_pass(): pl.pallas_call(strip_kernel, in_specs=[IN_VMEM] * 6 + [IN_HBM] * 2, out_s...  2.87 us
    ppermute x5, waiting for transfers between devices, local(): moved = lax.ppermute(peak, axis, pairs)  2.73 us
    ppermute x1, waiting for transfers between devices, local(): from_twin = lax.ppermute(to_twin, 'gy', twin_pairs('gy'))  2.64 us
  transfers between devices with their start and end apart: 9, of which 4 were waited for; matrix products, arithmetic and copies ran while one was open for 0% of the time, Pallas kernels for 28%

profile of v6, /device:TPU:0, one launch (start us, length us, event | category | flops | bytes accessed | tf_op | source)
XLA Modules:
  0.0 40.2 jit_solution(13394352242944338132)
XLA Ops:
  0.6 3.7 %columns.1 = (f32[224,256]{1,0:T(8,128)S(1)}, f32[224,256]{1,0:T(8,128)S(1)}, f32[72,256]{1,0:T(8,128)S(1)}, f32[72,256]{1,0:T(8,128)S(1)}, f32[2,16,224,256]{3,...) custom-call(f32[2,16,224,256]{3,2,1,0:T(8,128)} %tracer_hbm.1, ...), custom_call_target="tpu_custom_call" | custom-call | flops 11010048 | bytes 7340032 | tf_op jit(solution)/shard_map/columns/pallas_call | solution.py:147
  4.3 0.6 %collective-permute-start = (f32[72,256]{1,0:T(8,128)S(1)}, f32[72,256]{1,0:T(8,128)S(1)}, u32[]{:S(2)}, u32[]{:S(2)}) collective-permute-start(f32[72,256]{1,0:T(8,128)S(1)} %get-tuple-element.50), channel_id=1, source_target_pairs={{0,4},{4,0},{8,12},{12,8},{16,20},{20,16},{24,28},{28,24},{1,5},{5... | collective-permute-start | bytes 221192 | tf_op jit(solution)/shard_map/ppermute | solution.py:896
  4.9 3.5 %collective-permute-start.1 = (f32[72,256]{1,0:T(8,128)S(1)}, f32[72,256]{1,0:T(8,128)S(1)}, u32[]{:S(2)}, u32[]{:S(2)}) collective-permute-start(f32[72,256]{1,0:T(8,128)S(1)} %get-tuple-element.51), channel_id=1, source_target_pairs={{0,28},{4,8},{8,4},{12,16},{16,12},{20,24},{24,20},{28,0},{1,29},{... | collective-permute-start | bytes 221192 | tf_op jit(solution)/shard_map/ppermute | solution.py:895
  8.4 2.9 %strips.1 = (f32[120,128]{1,0:T(8,128)S(1)}, f32[120,128]{1,0:T(8,128)S(1)}, bf16[16,224,256]{2,1,0:T(8,128)(2,1)S(1)}, bf16[16,224,256]{2,1,0:T(8,128)(2,1)S(1)}) custom-call(f32[2,16,224,256]{3,2,1,0:T(8,128)S(1)} %get-tuple-element.40.tracer, f32[224,256]{1,0:T(8,128)S(1)} %get-tuple-element.41.depth, f32[224,256]{1,0:T(8,128)S(1)} %get-tuple-element.42.surf, ...), custom_call_target="tpu_custom_call" | custom-call | flops 11010048 | bytes 7340032 | tf_op jit(solution)/shard_map/strips/pallas_call | solution.py:230
  11.3 0.0 collective-permute-done.from_twin
  11.3 0.0 collective-permute-done.1.from_other
  11.3 0.2 corners.1
  11.5 1.6 %collective-permute-start.2 = (f32[120,128]{1,0:T(8,128)S(1)}, f32[120,128]{1,0:T(8,128)S(1)}, u32[]{:S(2)}, u32[]{:S(2)}) collective-permute-start(f32[120,128]{1,0:T(8,128)S(1)} %get-tuple-element.54), channel_id=1, source_target_pairs={{0,1},{1,0},{2,3},{3,2},{4,5},{5,4},{6,7},{7,6},{8,9},{9,8},{10,11... | collective-permute-start | bytes 184328 | tf_op jit(solution)/shard_map/ppermute | solution.py:901
  13.1 0.0 collective-permute-start.3
  13.1 2.6 %collective-permute-done.2.from_twin = f32[120,128]{1,0:T(8,128)S(1)} collective-permute-done((f32[120,128]{1,0:T(8,128)S(1)}, f32[120,128]{1,0:T(8,128)S(1)}, u32[]{:S(2)}, u32[]{:S(2)}) %collective-permute-start.2) | collective-permute-done | bytes 61472 | tf_op jit(solution)/shard_map/ppermute | solution.py:901
  15.7 0.0 collective-permute-done.3.from_other
  15.7 0.4 %peak.1 = (f32[8,128]{1,0:T(8,128)S(1)}, f32[120,128]{1,0:T(8,128)S(1)}, f32[120,128]{1,0:T(8,128)S(1)}) custom-call(f32[224,256]{1,0:T(8,128)S(1)} %get-tuple-element.41.depth, f32[72,256]{1,0:T(8,128)S(1)} %get-tuple-element.52.west, f32[72,256]{1,0:T(8,128)S(1)} %get-tuple-element.53.east, f32[120,128]{1,0:T(8,128)S(1)} %collective-permute-done.2.from_twin, ...), custom_call_target="tpu_custom_call" | custom-call | flops 1720320 | bytes 229376 | tf_op jit(solution)/shard_map/peak/pallas_call | solution.py:392
  16.2 0.0 collective-permute-start.4
  16.2 0.9 %around.1 = (f32[2,224,128]{2,1,0:T(8,128)S(1)}, bf16[4,2,224,128]{3,2,1,0:T(8,128)(2,1)S(1)}) custom-call(f32[224,256]{1,0:T(8,128)S(1)} %get-tuple-element.41.depth, f32[72,256]{1,0:T(8,128)S(1)} %get-tuple-element.52.west, f32[72,256]{1,0:T(8,128)S(1)} %get-tuple-element.53.east, f32[120,128]{1,0:T(8,128)S(1)} %get-tuple-element.57.south, ...), custom_call_target="tpu_custom_call" | custom-call | flops 1720320 | bytes 917504 | tf_op jit(solution)/shard_map/around/pallas_call | solution.py:439
  17.0 0.3 collective-permute-done.4
  17.3 0.1 collective-permute-start.5
  17.5 1.9 %tracers.4.rest_0_ = f32[2,4,224,256]{3,2,1,0:T(8,128)S(1)} custom-call(f32[2,16,224,256]{3,2,1,0:T(8,128)S(1)} %get-tuple-element.40.tracer, bf16[16,224,256]{2,1,0:T(8,128)(2,1)S(1)} %get-tuple-element.46.zonal, bf16[16,224,256]{2,1,0:T(8,128)(2,1)S(1)} %get-tuple-element.47.merid, f32[224,256]{1,0:T(8,128)S(1)} %get-tuple-element.41.depth, ...), custom_call_target="tpu_custom_call" | custom-call | flops 18350080 | bytes 4587520 | tf_op jit(solution)/shard_map/tracers/pallas_call | solution.py:563
  19.4 1.5 %collective-permute-done.5 = f32[8,128]{1,0:T(8,128)S(1)} collective-permute-done((f32[8,128]{1,0:T(8,128)S(1)}, f32[8,128]{1,0:T(8,128)S(1)}, u32[]{:S(2)}, u32[]{:S(2)}) %collective-permute-start.5) | collective-permute-done | bytes 4128 | tf_op jit(solution)/shard_map/ppermute | solution.py:911
  21.0 0.8 %collective-permute-start.6 = (f32[8,128]{1,0:T(8,128)S(1)}, f32[8,128]{1,0:T(8,128)S(1)}, u32[]{:S(2)}, u32[]{:S(2)}) collective-permute-start(f32[8,128]{1,0:T(8,128)S(1)} %max.16), channel_id=1, source_target_pairs={{0,16},{4,20},{8,24},{12,28},{16,0},{20,4},{24,8},{28,12},{1,17},{... | collective-permute-start | bytes 12296 | tf_op jit(solution)/shard_map/ppermute | solution.py:911
  21.8 1.9 %tracers.5 = (f32[2,4,224,256]{3,2,1,0:T(8,128)S(1)}, f32[2,16,224,256]{3,2,1,0:T(8,128)}) custom-call(f32[2,16,224,256]{3,2,1,0:T(8,128)S(1)} %get-tuple-element.40.tracer, bf16[16,224,256]{2,1,0:T(8,128)(2,1)S(1)} %get-tuple-element.46.zonal, bf16[16,224,256]{2,1,0:T(8,128)(2,1)S(1)} %get-tuple-element.47.merid, f32[224,256]{1,0:T(8,128)S(1)} %get-tuple-element.41.depth, ...), custom_call_target="tpu_custom_call" | custom-call | flops 18350080 | bytes 4587520 | tf_op jit(solution)/shard_map/tracers/pallas_call | solution.py:563
  23.7 0.9 %collective-permute-done.6 = f32[8,128]{1,0:T(8,128)S(1)} collective-permute-done((f32[8,128]{1,0:T(8,128)S(1)}, f32[8,128]{1,0:T(8,128)S(1)}, u32[]{:S(2)}, u32[]{:S(2)}) %collective-permute-start.6) | collective-permute-done | bytes 4128 | tf_op jit(solution)/shard_map/ppermute | solution.py:911
  24.6 2.7 %collective-permute-start.7 = (f32[8,128]{1,0:T(8,128)S(1)}, f32[8,128]{1,0:T(8,128)S(1)}, u32[]{:S(2)}, u32[]{:S(2)}) collective-permute-start(f32[8,128]{1,0:T(8,128)S(1)} %max.17), channel_id=1, source_target_pairs={{0,1},{1,0},{2,3},{3,2},{4,5},{5,4},{6,7},{7,6},{8,9},{9,8},{10,11... | collective-permute-start | bytes 12296 | tf_op jit(solution)/shard_map/ppermute | solution.py:911
  27.3 1.9 %tracers.6 = (f32[2,4,224,256]{3,2,1,0:T(8,128)S(1)}, f32[2,16,224,256]{3,2,1,0:T(8,128)}) custom-call(f32[2,16,224,256]{3,2,1,0:T(8,128)S(1)} %get-tuple-element.40.tracer, bf16[16,224,256]{2,1,0:T(8,128)(2,1)S(1)} %get-tuple-element.46.zonal, bf16[16,224,256]{2,1,0:T(8,128)(2,1)S(1)} %get-tuple-element.47.merid, ...), custom_call_target="tpu_custom_call", output_to_operand_aliasing={{1}: (9, {})} | custom-call | flops 18350080 | bytes 4587520 | tf_op jit(solution)/shard_map/tracers/pallas_call | solution.py:563
  29.2 0.0 collective-permute-done.7
  29.2 3.1 %collective-permute-start.8 = (f32[8,128]{1,0:T(8,128)S(1)}, f32[8,128]{1,0:T(8,128)S(1)}, u32[]{:S(2)}, u32[]{:S(2)}) collective-permute-start(f32[8,128]{1,0:T(8,128)S(1)} %max.18), channel_id=1, source_target_pairs={{0,2},{1,3},{2,0},{3,1},{4,6},{5,7},{6,4},{7,5},{8,10},{9,11},{10,... | collective-permute-start | bytes 12296 | tf_op jit(solution)/shard_map/ppermute | solution.py:911
  32.3 1.9 %tracers.7 = (f32[2,4,224,256]{3,2,1,0:T(8,128)S(1)}, f32[2,16,224,256]{3,2,1,0:T(8,128)}) custom-call(f32[2,16,224,256]{3,2,1,0:T(8,128)S(1)} %get-tuple-element.40.tracer, bf16[16,224,256]{2,1,0:T(8,128)(2,1)S(1)} %get-tuple-element.46.zonal, bf16[16,224,256]{2,1,0:T(8,128)(2,1)S(1)} %get-tuple-element.47.merid, ...), custom_call_target="tpu_custom_call", output_to_operand_aliasing={{1}: (9, {})} | custom-call | flops 18350080 | bytes 4587520 | tf_op jit(solution)/shard_map/tracers/pallas_call | solution.py:563
  34.3 0.0 collective-permute-done.8
  34.3 6.0 %solve.1 = (f32[2,16,224,256]{3,2,1,0:T(8,128)}, f32[224,256]{1,0:T(8,128)}, f32[224,256]{1,0:T(8,128)}, f32[224,256]{1,0:T(8,128)}) custom-call(f32[2,4,224,256]{3,2,1,0:T(8,128)S(1)} %get-tuple-element.73.tracer_in, f32[2,16,224,256]{3,2,1,0:T(8,128)} %get-tuple-element.74._, f32[8,128]{1,0:T(8,128)S(1)} %max.19.peak, ...), custom_call_target="tpu_custom_call", output_to_operand_aliasing={{0}: (1, {})} | custom-call | flops 11468800 | bytes 1835008 | tf_op jit(solution)/shard_map/solve/pallas_call | solution.py:836
  (5 shorter events, 0.0 us)
Async XLA Ops:
  4.3 7.0 %collective-permute-start = (f32[72,256]{1,0:T(8,128)S(1)}, f32[72,256]{1,0:T(8,128)S(1)}, u32[]{:S(2)}, u32[]{:S(2)}) collective-permute-start(f32[72,256]{1,0:T(8,128)S(1)} %get-tuple-element.50), channel_id=1, source_target_pairs={{0,4},{4,0},{8,12},{12,8},{16,20},{20,16},{24,28},{28,24},{1,5},{5... | collective-permute-start | bytes 221192 | tf_op jit(solution)/shard_map/ppermute | solution.py:896
  4.9 6.4 %collective-permute-start.1 = (f32[72,256]{1,0:T(8,128)S(1)}, f32[72,256]{1,0:T(8,128)S(1)}, u32[]{:S(2)}, u32[]{:S(2)}) collective-permute-start(f32[72,256]{1,0:T(8,128)S(1)} %get-tuple-element.51), channel_id=1, source_target_pairs={{0,28},{4,8},{8,4},{12,16},{16,12},{20,24},{24,20},{28,0},{1,29},{... | collective-permute-start | bytes 221192 | tf_op jit(solution)/shard_map/ppermute | solution.py:895
  11.5 4.2 %collective-permute-start.2 = (f32[120,128]{1,0:T(8,128)S(1)}, f32[120,128]{1,0:T(8,128)S(1)}, u32[]{:S(2)}, u32[]{:S(2)}) collective-permute-start(f32[120,128]{1,0:T(8,128)S(1)} %get-tuple-element.54), channel_id=1, source_target_pairs={{0,1},{1,0},{2,3},{3,2},{4,5},{5,4},{6,7},{7,6},{8,9},{9,8},{10,11... | collective-permute-start | bytes 184328 | tf_op jit(solution)/shard_map/ppermute | solution.py:901
  13.1 2.6 %collective-permute-start.3 = (f32[120,128]{1,0:T(8,128)S(1)}, f32[120,128]{1,0:T(8,128)S(1)}, u32[]{:S(2)}, u32[]{:S(2)}) collective-permute-start(f32[120,128]{1,0:T(8,128)S(1)} %get-tuple-element.55), channel_id=1, source_target_pairs={{0,4},{1,2},{2,1},{3,7},{4,0},{5,6},{6,5},{7,3},{8,12},{9,10},{10,... | collective-permute-start | bytes 184328 | tf_op jit(solution)/shard_map/ppermute | solution.py:902
  16.2 1.2 %collective-permute-start.4 = (f32[8,128]{1,0:T(8,128)S(1)}, f32[8,128]{1,0:T(8,128)S(1)}, u32[]{:S(2)}, u32[]{:S(2)}) collective-permute-start(f32[8,128]{1,0:T(8,128)S(1)} %get-tuple-element.56), channel_id=1, source_target_pairs={{0,4},{4,0},{8,12},{12,8},{16,20},{20,16},{24,28},{28,24},{1,5},{5... | collective-permute-start | bytes 12296 | tf_op jit(solution)/shard_map/ppermute | solution.py:911
  17.3 3.6 %collective-permute-start.5 = (f32[8,128]{1,0:T(8,128)S(1)}, f32[8,128]{1,0:T(8,128)S(1)}, u32[]{:S(2)}, u32[]{:S(2)}) collective-permute-start(f32[8,128]{1,0:T(8,128)S(1)} %max.15), channel_id=1, source_target_pairs={{0,8},{4,12},{8,0},{12,4},{16,24},{20,28},{24,16},{28,20},{1,9},{5... | collective-permute-start | bytes 12296 | tf_op jit(solution)/shard_map/ppermute | solution.py:911
  21.0 3.6 %collective-permute-start.6 = (f32[8,128]{1,0:T(8,128)S(1)}, f32[8,128]{1,0:T(8,128)S(1)}, u32[]{:S(2)}, u32[]{:S(2)}) collective-permute-start(f32[8,128]{1,0:T(8,128)S(1)} %max.16), channel_id=1, source_target_pairs={{0,16},{4,20},{8,24},{12,28},{16,0},{20,4},{24,8},{28,12},{1,17},{... | collective-permute-start | bytes 12296 | tf_op jit(solution)/shard_map/ppermute | solution.py:911
  24.6 4.6 %collective-permute-start.7 = (f32[8,128]{1,0:T(8,128)S(1)}, f32[8,128]{1,0:T(8,128)S(1)}, u32[]{:S(2)}, u32[]{:S(2)}) collective-permute-start(f32[8,128]{1,0:T(8,128)S(1)} %max.17), channel_id=1, source_target_pairs={{0,1},{1,0},{2,3},{3,2},{4,5},{5,4},{6,7},{7,6},{8,9},{9,8},{10,11... | collective-permute-start | bytes 12296 | tf_op jit(solution)/shard_map/ppermute | solution.py:911
  29.2 5.1 %collective-permute-start.8 = (f32[8,128]{1,0:T(8,128)S(1)}, f32[8,128]{1,0:T(8,128)S(1)}, u32[]{:S(2)}, u32[]{:S(2)}) collective-permute-start(f32[8,128]{1,0:T(8,128)S(1)} %max.18), channel_id=1, source_target_pairs={{0,2},{1,3},{2,0},{3,1},{4,6},{5,7},{6,4},{7,5},{8,10},{9,11},{10,... | collective-permute-start | bytes 12296 | tf_op jit(solution)/shard_map/ppermute | solution.py:911
